TPU v7x, 256 devices: a whole 4x4x8 slice. The times are simulated.
256 devices in a mesh: dp: 32 (over z_lo, y, x), tensor: 8 (over z_hi, core).
Axes of the slice: x: 4, y: 4, z: 8 (z_hi: 4, z_lo: 2; z = z_hi * 2 + z_lo), core: 2. Of those that a mesh axis runs over, the one named last changes fastest.
Arguments:
- rollout_rows: bfloat16 [16384, 4608], P(('dp', 'tensor')), may hold values from -6 to 6
- pack_dest: int32 [16384], P(('dp', 'tensor')), may hold values from 0 to 16383, as said below
- lengths: int32 [17], replicated, may hold values from 128 to 1536, as said below
- pattern: int32 [128, 128], P('dp'), may hold values from 0 to 1, as said below
- norm_gain: float32 [4608], replicated, may hold values from 0.1 to 1.9
- w_query: bfloat16 [4608, 2048], P(None, 'tensor'), may hold values from -0.1875 to 0.1875
- w_key: bfloat16 [4608, 1024], P(None, 'tensor'), may hold values from -0.1875 to 0.1875
- w_value: bfloat16 [4608, 1024], P(None, 'tensor'), may hold values from -0.09375 to 0.09375
- w_out: bfloat16 [2048, 4608], P('tensor'), may hold values from -0.125 to 0.125
- post_gain: float32 [4608], replicated, may hold values from 0.1 to 1.9
Outputs:
- layer_out: bfloat16 [16384, 4608], P(('dp', 'tensor'))
Inputs may be any that keep to these rules, and one draw needn't show every extreme that they name: `pack_dest`: a permutation of the pack rows; a rollout row goes to a pack row of the same tensor index, and the 64 rollout rows of one device go to each dp index exactly 2 at a time. `lengths`: all multiples of 128, summing to 16384; the prompt is shorter than 512. pattern[q, q] = 1; pattern[q, k] = 1 only where k <= q and key block k lies in the first 512 pack rows or in a dp shard at most 3 before query block q's shard.
All inputs are finite; a program needn't handle non-finite values.
Results may differ from a plain program's by a relative error of at most 0.017.
Values may be sent and summed in bfloat16 or wider, within the bound.
No kernel may reach another device: no remote copies, remote signals or barrier semaphores. Data moves between devices by JAX's collectives and lax.ppermute only.
A program may use at most 128 MiB of HBM per device.

v0:
```python
import functools
import math

import jax
import jax.numpy as jnp
import numpy as np
from jax import lax
from jax.experimental import pallas as pl
from jax.experimental.pallas import tpu as pltpu
from jax.sharding import PartitionSpec as P

HD = 128
BLK = 128
D = 4608
SHARD = 512
SLOTS = 64
PLANES = 4

SOFT_CAP = 50.0
QUERY_SCALE = 1.0 / 12.0
ROPE_BASE = 10000.0
EPSILON = 1e-06

OUT = [(t, (t + (6 if t % 2 else 2)) % 8) for t in range(8)]
BACK = [(t, (t + (2 if t % 2 else 6)) % 8) for t in range(8)]
FAR = [(t, (t + 4) % 8) for t in range(8)]
SIB = [(t, t ^ 1) for t in range(8)]
VMEM_BYTES = 16 << 20
TILES = 6
OTHER = (0, 2, 1, 3)


SMEM = pl.BlockSpec(memory_space=pltpu.SMEM)
VMEM = pl.BlockSpec(memory_space=pltpu.VMEM)


def inverse_freq():
    half = HD // 2
    steps = np.arange(half, dtype=np.float32) * np.float32(2.0) / np.float32(HD)
    freq = np.power(np.float32(ROPE_BASE), -steps).astype(np.float32)
    return jnp.asarray(np.concatenate([freq, freq])[None, :])


def rope(row_ids, lengths, freq):
    bound = lengths[0]
    past = jnp.where(row_ids >= bound, lengths[0], 0)
    for i in range(1, lengths.shape[0]):
        bound = bound + lengths[i]
        past = past + jnp.where(row_ids >= bound, lengths[i], 0)
    place = jnp.where(row_ids < lengths[0], row_ids, lengths[0] + row_ids - past)
    angles = place.astype(jnp.float32) * freq
    lane = lax.broadcasted_iota(jnp.int32, row_ids.shape, 1)
    sine = jnp.sin(angles)
    return jnp.cos(angles), jnp.where(lane < HD // 2, -sine, sine)


def plane_order():
    t = lax.axis_index("tensor")
    plane = t // 2
    core = t % 2
    side = 1 - 2 * core
    return core, [plane] + [(plane + PLANES + k) % PLANES for k in (-side, side, 2)]


def tables_kernel(lengths, freq, cos_a, sin_a, cos_c, sin_c):
    core, order = plane_order()
    base = lax.axis_index("dp") * SHARD
    local = lax.broadcasted_iota(jnp.int32, (BLK, HD), 0) ^ (core * SLOTS)
    for i in range(PLANES):
        c, s = rope(base + order[i] * BLK + local, lengths, freq[...])
        if i < 3:
            cos_a[i * BLK : (i + 1) * BLK] = c
            sin_a[i * BLK : (i + 1) * BLK] = s
        else:
            cos_c[...] = c
            sin_c[...] = s


def tables(lengths):
    return pl.pallas_call(
        tables_kernel,
        in_specs=[SMEM, VMEM],
        out_specs=[VMEM] * 4,
        out_shape=[jax.ShapeDtypeStruct((n, HD), jnp.float32) for n in (384, 384, BLK, BLK)],
        compiler_params=pltpu.CompilerParams(vmem_limit_bytes=VMEM_BYTES),
        name="tables",
    )(lengths, inverse_freq())


def early_kernel(lengths, freq, own, sib, gain, wk, wv, out):
    core, order = plane_order()
    rows = jnp.concatenate([own[...], sib[...]], axis=0)
    x = rms_scale(rows[:, :D].astype(jnp.float32), gain[...]).astype(jnp.bfloat16)
    slot = rows[:, D:].astype(jnp.int32)
    index = lax.broadcasted_iota(jnp.int32, slot.shape, 0) // 2
    source = jnp.zeros_like(index)
    for i in range(2 * PLANES):
        source = jnp.where(index == i, early_source(i, core, order), source)
    c, s = rope(source * SLOTS + slot, lengths, freq[...])
    kv = jnp.dot(x, jnp.concatenate([wk[...], wv[...]], axis=1), preferred_element_type=jnp.float32)
    k = kv[:, :HD]
    k = k * c + pltpu.roll(k, HD // 2, 1) * s
    both = jnp.concatenate([k, kv[:, HD:]], axis=1).astype(jnp.bfloat16)
    out[...] = jnp.broadcast_to(both[None], out.shape)


def early_source(i, core, order):
    if i < PLANES:
        return 2 * order[i] + core
    return 2 * order[OTHER[i - PLANES]] + 1 - core


def early_keys(lengths, own, sib, gain, w_key, w_value, copies):
    return pl.pallas_call(
        early_kernel,
        in_specs=[SMEM] + [VMEM] * 6,
        out_specs=VMEM,
        out_shape=jax.ShapeDtypeStruct((copies, 2 * own.shape[0], 2 * HD), jnp.bfloat16),
        compiler_params=pltpu.CompilerParams(vmem_limit_bytes=VMEM_BYTES),
        name="early",
    )(lengths, inverse_freq(), own, sib, gain[None, :], w_key, w_value)


def rms_scale(values, gain):
    return values * lax.rsqrt(jnp.mean(values * values, axis=-1, keepdims=True) + EPSILON) * gain


def to(values, pairs):
    return lax.ppermute(values, "tensor", pairs)


def qkv(pieces, wq, wk, wv, cos, sin):
    x = jnp.concatenate([r[...] for r in pieces], axis=0)
    c = cos[...]
    s = sin[...]

    def turn(v):
        return (v * c + pltpu.roll(v, HD // 2, 1) * s).astype(jnp.bfloat16)

    q = jnp.dot(x, wq[...], preferred_element_type=jnp.float32)
    wkv = jnp.concatenate([wk[...], wv[...]], axis=1)
    kv = jnp.dot(x, wkv, preferred_element_type=jnp.float32)
    return turn(q[:, :HD]), turn(q[:, HD:]), turn(kv[:, :HD]), kv[:, HD:].astype(jnp.bfloat16)


def near_kernel(x0, x1, x2, x3, x4, x5, wq, wk, wv, cos, sin, q_out, kv_out):
    q0, q1, k, v = qkv((x0, x1, x2, x3, x4, x5), wq, wk, wv, cos, sin)
    q_out[0] = q0
    q_out[1] = q1
    kv_out[:, :HD] = k
    kv_out[:, HD:] = v


def far_kernel(x0, x1, wq, wk, wv, cos, sin, q_in, q_out, kv_out):
    q0, q1, k, v = qkv((x0, x1), wq, wk, wv, cos, sin)
    near = SHARD - BLK
    q_out[:near] = q_in[0]
    q_out[near:SHARD] = q0
    q_out[SHARD : SHARD + near] = q_in[1]
    q_out[SHARD + near :] = q1
    kv_out[:, :HD] = k
    kv_out[:, HD:] = v


def project_near(*args):
    rows = SHARD - BLK
    return pl.pallas_call(
        near_kernel,
        in_specs=[VMEM] * len(args),
        out_specs=[VMEM] * 2,
        out_shape=[
            jax.ShapeDtypeStruct((2, rows, HD), jnp.bfloat16),
            jax.ShapeDtypeStruct((rows, 2 * HD), jnp.bfloat16),
        ],
        compiler_params=pltpu.CompilerParams(vmem_limit_bytes=VMEM_BYTES),
        name="project_near",
    )(*args)


def project_far(*args):
    return pl.pallas_call(
        far_kernel,
        in_specs=[VMEM] * len(args),
        out_specs=[VMEM] * 2,
        out_shape=[
            jax.ShapeDtypeStruct((2 * SHARD, HD), jnp.bfloat16),
            jax.ShapeDtypeStruct((BLK, 2 * HD), jnp.bfloat16),
        ],
        compiler_params=pltpu.CompilerParams(vmem_limit_bytes=VMEM_BYTES),
        name="project_far",
    )(*args)


def attend_kernel(pattern, q2, *refs):
    kvs = refs[:8]
    prompt = refs[8]
    ours, theirs, acc, tot = refs[9:]
    acc[...] = jnp.zeros_like(acc)
    tot[...] = jnp.zeros_like(tot)
    core, order = plane_order()
    d = lax.axis_index("dp")
    lane = lax.broadcasted_iota(jnp.int32, (1, BLK), 1)

    def block(ref, row, some, masks):
        @pl.when(some)
        def _():
            k = ref[row : row + BLK, :HD]
            v = ref[row : row + BLK, HD:]
            scores = lax.dot_general(
                q2[...], k, (((1,), (1,)), ((), ())), preferred_element_type=jnp.float32
            )
            weights = jnp.exp2(jnp.tanh(scores * (QUERY_SCALE / SOFT_CAP)) * (SOFT_CAP * math.log2(math.e)))
            parts = []
            for i in range(2 * PLANES):
                parts.append(masks[i % PLANES](weights[i * BLK : (i + 1) * BLK]))
            weights = jnp.concatenate(parts, axis=0)
            tot[...] += weights
            acc[...] += jnp.dot(weights.astype(jnp.bfloat16), v, preferred_element_type=jnp.float32)

    def scaled(flag):
        return lambda part: part * flag.astype(jnp.float32)

    def causal(flag):
        def mask(part):
            flip = core * SLOTS
            rows_id = lax.broadcasted_iota(jnp.int32, (BLK, BLK), 0) ^ flip
            cols_id = lax.broadcasted_iota(jnp.int32, (BLK, BLK), 1) ^ flip
            return jnp.where(cols_id <= rows_id, part, 0.0) * flag.astype(jnp.float32)

        return mask

    def seen(i, shard, plane):
        return (pattern[order[i], shard * PLANES + plane] == 1).astype(jnp.int32)

    for source in range(4):
        shard = jnp.maximum(d - source, 0)
        for b in range(PLANES):
            flags = [seen(i, shard, order[b]) for i in range(PLANES)]
            some = flags[0] + flags[1] + flags[2] + flags[3] > 0
            if source:
                some = some & (d - source >= 1)
            masks = [causal(f) if source == 0 and i == b else scaled(f) for i, f in enumerate(flags)]
            ref, row = (kvs[2 * source], b * BLK) if b < 3 else (kvs[2 * source + 1], 0)
            block(ref, row, some, masks)

    masks = []
    some = 0
    for i in range(PLANES):
        flags = [seen(i, 0, order[b]) for b in range(PLANES)]
        some += flags[0] + flags[1] + flags[2] + flags[3]
        row = jnp.zeros((1, BLK), jnp.float32)
        for b in range(2 * PLANES):
            flag = flags[b if b < PLANES else OTHER[b - PLANES]]
            row = jnp.where(lane % 16 // 2 == b, flag.astype(jnp.float32), row)
        masks.append(lambda part, row=row: part * row)
    for b in range(PLANES):
        block(prompt, b * BLK, (some > 0) & (d >= 1), masks)
    for head in range(2):
        for i in range(PLANES):
            lo = head * SHARD + i * BLK
            total = jnp.sum(tot[lo : lo + BLK], axis=1, keepdims=True)
            part = (acc[lo : lo + BLK] / total).astype(jnp.bfloat16)
            lanes = slice(head * HD, (head + 1) * HD)
            ours[i * SLOTS : (i + 1) * SLOTS, lanes] = part[:SLOTS]
            j = OTHER[i]
            theirs[j * SLOTS : (j + 1) * SLOTS, lanes] = part[SLOTS:]


def attend(pattern, q2, kvs, prompt):
    return pl.pallas_call(
        attend_kernel,
        in_specs=[SMEM] + [VMEM] * 10,
        out_specs=[VMEM] * 2,
        out_shape=[jax.ShapeDtypeStruct((PLANES * SLOTS, 2 * HD), jnp.bfloat16)] * 2,
        scratch_shapes=[
            pltpu.VMEM((1024, HD), jnp.float32),
            pltpu.VMEM((1024, HD), jnp.float32),
        ],
        compiler_params=pltpu.CompilerParams(vmem_limit_bytes=VMEM_BYTES),
        name="attend",
    )(pattern, q2, *kvs, prompt)


def out_kernel(chunks, ours, theirs, w0, w1, first, second, buf, sems):
    tile = D // TILES

    def copies(n):
        cols = pl.ds(n * tile, tile)
        return [
            pltpu.make_async_copy(w.at[:, cols], buf.at[n, pl.ds(i * 2 * HD, 2 * HD)], sems.at[n, i])
            for i, w in enumerate((w0, w1))
        ]

    for n in range(TILES):
        for copy in copies(n):
            copy.start()
    rows = jnp.concatenate(
        [
            jnp.concatenate([r[c * SLOTS : (c + 1) * SLOTS] for r in (ours, theirs)], axis=1)
            for c in chunks
        ],
        axis=0,
    )
    for n in range(TILES):
        for copy in copies(n):
            copy.wait()
        total = jnp.dot(rows, buf[n], preferred_element_type=jnp.float32)
        cols = slice(n * tile, (n + 1) * tile)
        first[:, cols] = total[:SLOTS].astype(first.dtype)
        second[:, cols] = total[SLOTS:].astype(second.dtype)


def project_out(chunks, dtype, ours, theirs, w_own, w_sib):
    hbm = pl.BlockSpec(memory_space=pltpu.HBM)
    return pl.pallas_call(
        functools.partial(out_kernel, chunks),
        in_specs=[VMEM] * 2 + [hbm] * 2,
        out_specs=[VMEM] * 2,
        out_shape=[jax.ShapeDtypeStruct((SLOTS, D), dtype)] * 2,
        scratch_shapes=[
            pltpu.VMEM((TILES, 4 * HD, D // TILES), jnp.bfloat16),
            pltpu.SemaphoreType.DMA((TILES, 2)),
        ],
        compiler_params=pltpu.CompilerParams(vmem_limit_bytes=VMEM_BYTES),
        name="project_out",
    )(ours, theirs, *[pltpu.with_memory_space_constraint(w, pltpu.HBM) for w in (w_own, w_sib)])


def body(
    rollout_rows, pack_dest, lengths, pattern, norm_gain, w_query, w_key, w_value, w_out, post_gain
):
    bf16 = jnp.bfloat16
    n_dp = lax.axis_size("dp")
    d = lax.axis_index("dp")
    per_peer = SLOTS // n_dp
    order_ids = jnp.arange(SLOTS, dtype=jnp.int32)

    target_dev = pack_dest // SHARD
    target_slot = pack_dest % SLOTS
    before = (target_dev[:, None] == target_dev[None, :]) & (order_ids[None, :] < order_ids[:, None])
    send_pos = target_dev * per_peer + jnp.sum(before.astype(jnp.int32), axis=1)
    placer = order_ids[:, None] == send_pos[None, :]
    send_rows = jnp.dot(placer.astype(bf16), rollout_rows, preferred_element_type=jnp.float32).astype(bf16)
    send_slots = jnp.sum(jnp.where(placer, target_slot[None, :], 0), axis=1)
    send = jnp.concatenate(
        [send_rows, jnp.broadcast_to(send_slots.astype(bf16)[:, None], (SLOTS, HD))], axis=1
    )
    width = D + HD
    got = lax.all_to_all(send.reshape(n_dp, per_peer, width), "dp", 0, 0, tiled=True)

    core, order = plane_order()
    later, _ = lax.optimization_barrier((lengths, send))
    cos_a, sin_a, cos_c, sin_c = tables(later)

    first = send[:per_peer]
    piece = jnp.pad(first, ((0, 8 - per_peer), (0, 0)))
    column = [to(piece, OUT), to(piece, BACK), to(piece, FAR)]
    w_sib = to(w_out, SIB)

    got, w_sib, _ = lax.optimization_barrier((got, w_sib, cos_a))
    got = got.reshape(SLOTS, width)
    arrange = order_ids[:, None] == got[:, D].astype(jnp.int32)[None, :]
    packed = jnp.dot(arrange.astype(bf16), got[:, :D], preferred_element_type=jnp.float32).astype(bf16)
    normed = rms_scale(packed.astype(jnp.float32), norm_gain).astype(bf16)

    near_o = to(normed, OUT)
    near_b = to(normed, BACK)
    own_s = to(normed, SIB)

    column, _ = lax.optimization_barrier((column, normed))
    early = jnp.concatenate([first] + [c[:per_peer] for c in column], axis=0)
    early_kv = early_keys(lengths, early, to(early, SIB), norm_gain, w_key, w_value, n_dp)
    prompt = lax.all_to_all(early_kv, "dp", 0, 0, tiled=True)
    prompt = prompt.reshape(SHARD, 2 * HD)
    near_o, near_b, prompt = lax.optimization_barrier((near_o, near_b, prompt))
    far_own = to(near_o, OUT)
    near_os = to(near_b, SIB)
    near_bs = to(near_o, SIB)
    q_a, kv_a = project_near(
        normed, own_s, near_o, near_os, near_b, near_bs, w_query, w_key, w_value, cos_a, sin_a
    )
    shifts = [[(s, s + k) for s in range(n_dp - k)] for k in (1, 2, 3)]
    kvs_a = [kv_a] + [lax.ppermute(kv_a, "dp", shift) for shift in shifts]
    far_own, kvs_a = lax.optimization_barrier((far_own, kvs_a))
    far_s = to(far_own, SIB)
    q, kv_c = project_far(far_own, far_s, w_query, w_key, w_value, cos_c, sin_c, q_a)
    kvs_c = [kv_c] + [lax.ppermute(kv_c, "dp", shift) for shift in shifts]
    kvs = [x for pair in zip(kvs_a, kvs_c) for x in pair]
    ours, theirs = attend(pattern, q, kvs, prompt)

    theirs = to(theirs, SIB)
    sum_far, sum_o = project_out((3, 1), bf16, ours, theirs, w_out, w_sib)
    theirs, sum_far = lax.optimization_barrier((theirs, sum_far))
    own, sum_b = project_out((0, 2), jnp.float32, ours, theirs, w_out, w_sib)
    from_far = to(sum_far, OUT)
    from_b = to(sum_o, BACK)
    from_o = to((sum_b + from_far.astype(jnp.float32)).astype(bf16), OUT)
    summed = own + from_b.astype(jnp.float32) + from_o.astype(jnp.float32)
    result = packed.astype(jnp.float32) + rms_scale(summed, post_gain)
    return result.astype(bf16)


def solution(mesh):
    placed = (
        P(("dp", "tensor"), None),
        P(("dp", "tensor")),
        P(),
        P("dp", None),
        P(),
        P(None, "tensor"),
        P(None, "tensor"),
        P(None, "tensor"),
        P("tensor", None),
        P(),
    )
    return jax.shard_map(
        body, mesh=mesh, in_specs=placed, out_specs=P(("dp", "tensor"), None), check_vma=False
    )
```

profile of v0, /device:TPU:40, one launch (start us, length us, event | category | flops | bytes accessed | tf_op | source)
XLA Modules:
  0.0 175.8 jit_solution(7899475572373446126)
XLA Ops:
  0.0 0.7 and_select_fusion.1
  1.1 0.3 convolution_convert_fusion.1
  1.6 0.6 copy-done.20
  2.2 0.9 pad_maximum_fusion
  3.1 2.6 %reshape.41 = bf16[32,2,4736]{2,1,0:T(2,128)(2,1)} reshape(bf16[64,4736]{1,0:T(8,128)(2,1)} %pad_maximum_fusion) | data formatting | bytes 1212416 | tf_op jit(solution)/shard_map/reshape | solution.py:349
  5.7 8.6 %all-to-all-start = ((bf16[32,2,4736]{2,1,0:T(2,128)(2,1)}), bf16[32,2,4736]{2,1,0:T(2,128)(2,1)}, u32[]{:S(2)}, u32[]{:S(2)}) async-start(bf16[32,2,4736]{2,1,0:T(2,128)(2,1)} %reshape.41), calls=%async_computation | async-start | bytes 1212416 | tf_op jit(solution)/shard_map/all_to_all | solution.py:349
  14.3 1.4 fusion.3
  15.7 6.3 %collective-permute-start.5 = (bf16[8,4736]{1,0:T(8,128)(2,1)}, bf16[8,4736]{1,0:T(8,128)(2,1)}, u32[]{:S(2)}, u32[]{:S(2)}) collective-permute-start(bf16[8,4736]{1,0:T(8,128)(2,1)} %fusion.3), channel_id=1, source_target_pairs={{0,4},{1,5},{2,6},{3,7},{4,0},{5,1},{6,2},{7,3},{8,12},{9,13},{10,... | collective-permute-start | bytes 227336 | tf_op jit(solution)/shard_map/ppermute | solution.py:129
  22.0 0.5 collective-permute-start.4
  22.6 2.4 %collective-permute-start.3 = (bf16[8,4736]{1,0:T(8,128)(2,1)}, bf16[8,4736]{1,0:T(8,128)(2,1)}, u32[]{:S(2)}, u32[]{:S(2)}) collective-permute-start(bf16[8,4736]{1,0:T(8,128)(2,1)} %fusion.3), channel_id=1, source_target_pairs={{0,2},{1,7},{2,4},{3,1},{4,6},{5,3},{6,0},{7,5},{8,10},{9,15},{10,... | collective-permute-start | bytes 227336 | tf_op jit(solution)/shard_map/ppermute | solution.py:129
  24.9 2.0 %tables.1 = (f32[384,128]{1,0:T(8,128)S(1)}, f32[384,128]{1,0:T(8,128)S(1)}, f32[128,128]{1,0:T(8,128)S(1)}, f32[128,128]{1,0:T(8,128)S(1)}) custom-call(s32[17]{0:T(128)S(1)} %copy-done.15, f32[1,128]{1,0:T(1,128)S(1)} %copy-done.16), custom_call_target="tpu_custom_call" | custom-call | tf_op jit(solution)/shard_map/tables/pallas_call | solution.py:80
  27.0 0.7 copy-done.6
  27.6 0.7 copy-done.8
  28.3 0.6 copy-done.10
  28.9 0.6 copy-done.12
  29.6 1.3 fusion.5
  30.9 3.0 %reshape.42 = bf16[64,4736]{1,0:T(8,128)(2,1)} reshape(bf16[32,2,4736]{2,1,0:T(2,128)(2,1)} %all-to-all-done) | data formatting | bytes 1212416 | tf_op jit(solution)/shard_map/reshape | solution.py:361
  33.9 0.8 convert_reduce_fusion
  34.8 1.6 multiply_reduce_fusion.1
  36.6 1.8 %collective-permute-start.2 = (bf16[64,4608]{1,0:T(8,128)(2,1)S(1)}, bf16[64,4608]{1,0:T(8,128)(2,1)}, u32[]{:S(2)}, u32[]{:S(2)}) collective-permute-start(bf16[64,4608]{1,0:T(8,128)(2,1)S(1)} %multiply_convert_fusion.x0), channel_id=1, source_target_pairs={{0,6},{1,3},{2,0},{3,5},{4,2},{5,7},{6,4},{7,1},{8,14},{9,11},{10,... | collective-permute-start | bytes 1769480 | tf_op jit(solution)/shard_map/ppermute | solution.py:129
  38.4 1.2 collective-permute-start.1
  39.6 0.9 slice.25
  40.5 0.9 slice.26
  41.4 0.9 slice.27
  42.4 0.8 collective-permute-start.6
  43.3 0.9 collective-permute-done.6.sib
  44.2 1.1 early.1
  45.3 0.7 copy-done.5
  46.0 8.4 %all-to-all-start.1 = ((bf16[32,16,256]{2,1,0:T(8,128)(2,1)}), bf16[32,16,256]{2,1,0:T(8,128)(2,1)}, u32[]{:S(2)}, u32[]{:S(2)}) async-start(bf16[32,16,256]{2,1,0:T(8,128)(2,1)} %copy-done.5), calls=%async_computation.1 | async-start | bytes 524288 | tf_op jit(solution)/shard_map/all_to_all | solution.py:373
  54.5 16.9 %all-to-all-done.1 = bf16[32,16,256]{2,1,0:T(8,128)(2,1)} async-done(((bf16[32,16,256]{2,1,0:T(8,128)(2,1)}), bf16[32,16,256]{2,1,0:T(8,128)(2,1)}, u32[]{:S(2)}, u32[]{:S(2)}) %all-to-all-start.1) | async-done | bytes 262176 | tf_op jit(solution)/shard_map/all_to_all | solution.py:373
  71.4 0.5 collective-permute-start.10
  71.9 0.4 collective-permute-start.7
  72.3 1.3 collective-permute-done.9.x3
  73.6 0.8 collective-permute-done.10.x5
  74.5 1.7 copy-done.3
  76.2 0.9 copy-done.7
  77.1 0.9 copy-done.9
  78.0 3.7 %project_near.1 = (bf16[2,384,128]{2,1,0:T(8,128)(2,1)S(1)}, bf16[384,256]{1,0:T(8,128)(2,1)S(1)}) custom-call(bf16[64,4608]{1,0:T(8,128)(2,1)S(1)} %multiply_convert_fusion.x0, bf16[64,4608]{1,0:T(8,128)(2,1)} %collective-permute-done.8.x1, bf16[64,4608]{1,0:T(8,128)(2,1)} %collective-permute-done.1.x2, bf16[64,4608]{1,0:T(8,128)(2,1)S(1)} %collective-permute-done.9.x3, ...), custom_call_target="tpu_custom_call" | custom-call | tf_op jit(solution)/shard_map/project_near/pallas_call | solution.py:167
  81.7 3.0 %collective-permute-start.13 = (bf16[384,256]{1,0:T(8,128)(2,1)S(1)}, bf16[384,256]{1,0:T(8,128)(2,1)S(1)}, u32[]{:S(2)}, u32[]{:S(2)}) collective-permute-start(bf16[384,256]{1,0:T(8,128)(2,1)S(1)} %get-tuple-element.50.refs_0_), channel_id=1, source_target_pairs={{0,24},{8,32},{16,40},{24,48},{32,56},{40,64},{48,72},{56,80},{64,... | collective-permute-start | bytes 589832 | tf_op jit(solution)/shard_map/ppermute | solution.py:383
  84.7 3.5 %collective-permute-start.12 = (bf16[384,256]{1,0:T(8,128)(2,1)S(1)}, bf16[384,256]{1,0:T(8,128)(2,1)S(1)}, u32[]{:S(2)}, u32[]{:S(2)}) collective-permute-start(bf16[384,256]{1,0:T(8,128)(2,1)S(1)} %get-tuple-element.50.refs_0_), channel_id=1, source_target_pairs={{0,16},{8,24},{16,32},{24,40},{32,48},{40,56},{48,64},{56,72},{64,... | collective-permute-start | bytes 589832 | tf_op jit(solution)/shard_map/ppermute | solution.py:383
  88.2 1.9 %collective-permute-start.11 = (bf16[384,256]{1,0:T(8,128)(2,1)S(1)}, bf16[384,256]{1,0:T(8,128)(2,1)S(1)}, u32[]{:S(2)}, u32[]{:S(2)}) collective-permute-start(bf16[384,256]{1,0:T(8,128)(2,1)S(1)} %get-tuple-element.50.refs_0_), channel_id=1, source_target_pairs={{0,8},{8,16},{16,24},{24,32},{32,40},{40,48},{48,56},{56,64},{64,7... | collective-permute-start | bytes 589832 | tf_op jit(solution)/shard_map/ppermute | solution.py:383
  90.1 0.3 collective-permute-done.7.x0
  90.4 2.2 %collective-permute-done.13.refs_6_ = bf16[384,256]{1,0:T(8,128)(2,1)S(1)} collective-permute-done((bf16[384,256]{1,0:T(8,128)(2,1)S(1)}, bf16[384,256]{1,0:T(8,128)(2,1)S(1)}, u32[]{:S(2)}, u32[]{:S(2)}) %collective-permute-start.13) | collective-permute-done | bytes 196640 | tf_op jit(solution)/shard_map/ppermute | solution.py:383
  92.6 3.9 %collective-permute-done.12.refs_4_ = bf16[384,256]{1,0:T(8,128)(2,1)S(1)} collective-permute-done((bf16[384,256]{1,0:T(8,128)(2,1)S(1)}, bf16[384,256]{1,0:T(8,128)(2,1)S(1)}, u32[]{:S(2)}, u32[]{:S(2)}) %collective-permute-start.12) | collective-permute-done | bytes 196640 | tf_op jit(solution)/shard_map/ppermute | solution.py:383
  96.5 3.7 %collective-permute-done.11.refs_2_ = bf16[384,256]{1,0:T(8,128)(2,1)S(1)} collective-permute-done((bf16[384,256]{1,0:T(8,128)(2,1)S(1)}, bf16[384,256]{1,0:T(8,128)(2,1)S(1)}, u32[]{:S(2)}, u32[]{:S(2)}) %collective-permute-start.11) | collective-permute-done | bytes 196640 | tf_op jit(solution)/shard_map/ppermute | solution.py:383
  100.3 2.0 %collective-permute-done.14.x1 = bf16[64,4608]{1,0:T(8,128)(2,1)S(1)} collective-permute-done((bf16[64,4608]{1,0:T(8,128)(2,1)S(1)}, bf16[64,4608]{1,0:T(8,128)(2,1)S(1)}, u32[]{:S(2)}, u32[]{:S(2)}) %collective-permute-start.14) | collective-permute-done | bytes 589856 | tf_op jit(solution)/shard_map/ppermute | solution.py:129
  102.3 0.9 project_far.1
  103.2 1.9 %collective-permute-start.17 = (bf16[128,256]{1,0:T(8,128)(2,1)S(1)}, bf16[128,256]{1,0:T(8,128)(2,1)S(1)}, u32[]{:S(2)}, u32[]{:S(2)}) collective-permute-start(bf16[128,256]{1,0:T(8,128)(2,1)S(1)} %get-tuple-element.51.refs_1_), channel_id=1, source_target_pairs={{0,24},{8,32},{16,40},{24,48},{32,56},{40,64},{48,72},{56,80},{64,... | collective-permute-start | bytes 196616 | tf_op jit(solution)/shard_map/ppermute | solution.py:387
  105.1 3.4 %collective-permute-start.16 = (bf16[128,256]{1,0:T(8,128)(2,1)S(1)}, bf16[128,256]{1,0:T(8,128)(2,1)S(1)}, u32[]{:S(2)}, u32[]{:S(2)}) collective-permute-start(bf16[128,256]{1,0:T(8,128)(2,1)S(1)} %get-tuple-element.51.refs_1_), channel_id=1, source_target_pairs={{0,16},{8,24},{16,32},{24,40},{32,48},{40,56},{48,64},{56,72},{64,... | collective-permute-start | bytes 196616 | tf_op jit(solution)/shard_map/ppermute | solution.py:387
  108.5 2.8 %collective-permute-start.15 = (bf16[128,256]{1,0:T(8,128)(2,1)S(1)}, bf16[128,256]{1,0:T(8,128)(2,1)S(1)}, u32[]{:S(2)}, u32[]{:S(2)}) collective-permute-start(bf16[128,256]{1,0:T(8,128)(2,1)S(1)} %get-tuple-element.51.refs_1_), channel_id=1, source_target_pairs={{0,8},{8,16},{16,24},{24,32},{32,40},{40,48},{48,56},{56,64},{64,7... | collective-permute-start | bytes 196616 | tf_op jit(solution)/shard_map/ppermute | solution.py:387
  111.3 2.4 %collective-permute-done.16.refs_5_ = bf16[128,256]{1,0:T(8,128)(2,1)S(1)} collective-permute-done((bf16[128,256]{1,0:T(8,128)(2,1)S(1)}, bf16[128,256]{1,0:T(8,128)(2,1)S(1)}, u32[]{:S(2)}, u32[]{:S(2)}) %collective-permute-start.16) | collective-permute-done | bytes 65568 | tf_op jit(solution)/shard_map/ppermute | solution.py:387
  113.7 3.2 %collective-permute-done.15.refs_3_ = bf16[128,256]{1,0:T(8,128)(2,1)S(1)} collective-permute-done((bf16[128,256]{1,0:T(8,128)(2,1)S(1)}, bf16[128,256]{1,0:T(8,128)(2,1)S(1)}, u32[]{:S(2)}, u32[]{:S(2)}) %collective-permute-start.15) | collective-permute-done | bytes 65568 | tf_op jit(solution)/shard_map/ppermute | solution.py:387
  116.8 5.4 %attend.1 = (bf16[256,256]{1,0:T(8,128)(2,1)S(1)}, bf16[256,256]{1,0:T(8,128)(2,1)S(1)}) custom-call(s32[4,128]{1,0:T(4,128)S(1)} %copy-done.14, bf16[1024,128]{1,0:T(8,128)(2,1)S(1)} %get-tuple-element.49.q2, bf16[384,256]{1,0:T(8,128)(2,1)S(1)} %get-tuple-element.50.refs_0_, bf16[128,256]{1,0:T(8,128)(2,1)S(1)} %get-tuple-element.51.refs_1_, ...), custom_call_target="tpu_custom_call" | custom-call | tf_op jit(solution)/shard_map/attend/pallas_call | solution.py:270
  122.2 0.3 collective-permute-start.18
  122.5 1.3 collective-permute-done.18.theirs
  123.9 3.0 %project_out.2 = (bf16[64,4608]{1,0:T(8,128)(2,1)S(1)}, bf16[64,4608]{1,0:T(8,128)(2,1)S(1)}) custom-call(bf16[256,256]{1,0:T(8,128)(2,1)S(1)} %get-tuple-element.56.ours, bf16[256,256]{1,0:T(8,128)(2,1)S(1)} %collective-permute-done.18.theirs, bf16[256,4608]{1,0:T(8,128)(2,1)} %w0.3, bf16[256,4608]{1,0:T(8,128)(2,1)} %copy-done.19), custom_call_target="tpu_custom_call" | custom-call | tf_op jit(solution)/shard_map/project_out/pallas_call | solution.py:315
  126.9 0.5 collective-permute-start.20
  127.5 3.0 %project_out.3 = (f32[64,4608]{1,0:T(8,128)S(1)}, f32[64,4608]{1,0:T(8,128)S(1)}) custom-call(bf16[256,256]{1,0:T(8,128)(2,1)S(1)} %get-tuple-element.56.ours, bf16[256,256]{1,0:T(8,128)(2,1)S(1)} %collective-permute-done.18.theirs, bf16[256,4608]{1,0:T(8,128)(2,1)} %w0.3, bf16[256,4608]{1,0:T(8,128)(2,1)} %copy-done.19), custom_call_target="tpu_custom_call" | custom-call | tf_op jit(solution)/shard_map/project_out/pallas_call | solution.py:315
  130.5 3.7 %collective-permute-start.19 = (bf16[64,4608]{1,0:T(8,128)(2,1)S(1)}, bf16[64,4608]{1,0:T(8,128)(2,1)S(1)}, u32[]{:S(2)}, u32[]{:S(2)}) collective-permute-start(bf16[64,4608]{1,0:T(8,128)(2,1)S(1)} %get-tuple-element.62), channel_id=1, source_target_pairs={{0,6},{1,3},{2,0},{3,5},{4,2},{5,7},{6,4},{7,1},{8,14},{9,11},{10,... | collective-permute-start | bytes 1769480 | tf_op jit(solution)/shard_map/ppermute | solution.py:129
  134.3 27.0 %collective-permute-done.20 = bf16[64,4608]{1,0:T(8,128)(2,1)S(1)} collective-permute-done((bf16[64,4608]{1,0:T(8,128)(2,1)S(1)}, bf16[64,4608]{1,0:T(8,128)(2,1)S(1)}, u32[]{:S(2)}, u32[]{:S(2)}) %collective-permute-start.20) | collective-permute-done | bytes 589856 | tf_op jit(solution)/shard_map/ppermute | solution.py:129
  161.5 12.0 %collective-permute-done.21 = bf16[64,4608]{1,0:T(8,128)(2,1)S(1)} collective-permute-done((bf16[64,4608]{1,0:T(8,128)(2,1)S(1)}, bf16[64,4608]{1,0:T(8,128)(2,1)S(1)}, u32[]{:S(2)}, u32[]{:S(2)}) %collective-permute-start.21) | collective-permute-done | bytes 589856 | tf_op jit(solution)/shard_map/ppermute | solution.py:129
  173.4 0.3 multiply_reduce_fusion
  173.8 0.9 copy-done.18
  174.7 1.1 add_convert_fusion
  (66 shorter events, 1.2 us)
Async XLA Ops:
  0.0 1.1 copy-start
  0.0 30.9 %collective-permute-start = (bf16[256,4608]{1,0:T(8,128)(2,1)}, bf16[256,4608]{1,0:T(8,128)(2,1)S(1)}, u32[]{:S(2)}, u32[]{:S(2)}) collective-permute-start(bf16[256,4608]{1,0:T(8,128)(2,1)} %w0.3), channel_id=1, source_target_pairs={{0,1},{1,0},{2,3},{3,2},{4,5},{5,4},{6,7},{7,6},{8,9},{9,8},{10,11... | collective-permute-start | bytes 7077896 | tf_op jit(solution)/shard_map/ppermute | solution.py:129
  1.6 0.6 copy-start.20
  3.1 11.3 %copy-start.24 = (pred[8]{0:T(512)(128)(4,1)S(1)}, pred[8]{0:T(512)(128)(4,1)}, u32[]{:S(2)}) copy-start(pred[8]{0:T(512)(128)(4,1)} %constant.45.clone.1) | copy-start | bytes 28
  5.7 19.3 %copy-start.15 = (s32[17]{0:T(128)S(1)}, s32[17]{0:T(128)}, u32[]{:S(2)}) copy-start(s32[17]{0:T(128)} %lengths.2) | copy-start | bytes 208
  5.7 19.3 %copy-start.16 = (f32[1,128]{1,0:T(1,128)S(1)}, f32[1,128]{1,0:T(1,128)}, u32[]{:S(2)}) copy-start(f32[1,128]{1,0:T(1,128)} %constant.47.clone.freq) | copy-start | bytes 1540
  5.7 25.2 %all-to-all-start = ((bf16[32,2,4736]{2,1,0:T(2,128)(2,1)}), bf16[32,2,4736]{2,1,0:T(2,128)(2,1)}, u32[]{:S(2)}, u32[]{:S(2)}) async-start(bf16[32,2,4736]{2,1,0:T(2,128)(2,1)} %reshape.41), calls=%async_computation | async-start | bytes 1212416 | tf_op jit(solution)/shard_map/all_to_all | solution.py:349
  15.7 23.9 %collective-permute-start.5 = (bf16[8,4736]{1,0:T(8,128)(2,1)}, bf16[8,4736]{1,0:T(8,128)(2,1)}, u32[]{:S(2)}, u32[]{:S(2)}) collective-permute-start(bf16[8,4736]{1,0:T(8,128)(2,1)} %fusion.3), channel_id=1, source_target_pairs={{0,4},{1,5},{2,6},{3,7},{4,0},{5,1},{6,2},{7,3},{8,12},{9,13},{10,... | collective-permute-start | bytes 227336 | tf_op jit(solution)/shard_map/ppermute | solution.py:129
  22.0 17.6 %collective-permute-start.4 = (bf16[8,4736]{1,0:T(8,128)(2,1)}, bf16[8,4736]{1,0:T(8,128)(2,1)}, u32[]{:S(2)}, u32[]{:S(2)}) collective-permute-start(bf16[8,4736]{1,0:T(8,128)(2,1)} %fusion.3), channel_id=1, source_target_pairs={{0,6},{1,3},{2,0},{3,5},{4,2},{5,7},{6,4},{7,1},{8,14},{9,11},{10,... | collective-permute-start | bytes 227336 | tf_op jit(solution)/shard_map/ppermute | solution.py:129
  22.6 17.0 %collective-permute-start.3 = (bf16[8,4736]{1,0:T(8,128)(2,1)}, bf16[8,4736]{1,0:T(8,128)(2,1)}, u32[]{:S(2)}, u32[]{:S(2)}) collective-permute-start(bf16[8,4736]{1,0:T(8,128)(2,1)} %fusion.3), channel_id=1, source_target_pairs={{0,2},{1,7},{2,4},{3,1},{4,6},{5,3},{6,0},{7,5},{8,10},{9,15},{10,... | collective-permute-start | bytes 227336 | tf_op jit(solution)/shard_map/ppermute | solution.py:129
  27.0 0.7 copy-start.6
  27.6 0.7 copy-start.8
  28.3 0.6 copy-start.10
  28.9 0.6 copy-start.12
  30.9 3.1 %copy-start.19 = (bf16[256,4608]{1,0:T(8,128)(2,1)}, bf16[256,4608]{1,0:T(8,128)(2,1)S(1)}, u32[]{:S(2)}) copy-start(bf16[256,4608]{1,0:T(8,128)(2,1)S(1)} %collective-permute-done.w1) | copy-start | bytes 7077892
  33.9 2.5 %copy-start.21 = (f32[4608]{0:T(1024)S(1)}, f32[4608]{0:T(1024)}, u32[]{:S(2)}) copy-start(f32[4608]{0:T(1024)} %param.16) | copy-start | bytes 55300
  34.8 9.4 %copy-start.2 = (bf16[4608,128]{1,0:T(8,128)(2,1)S(1)}, bf16[4608,128]{1,0:T(8,128)(2,1)}, u32[]{:S(2)}) copy-start(bf16[4608,128]{1,0:T(8,128)(2,1)} %wv.5) | copy-start | bytes 3538948
  36.3 6.0 %copy-start.17 = (f32[64,4608]{1,0:T(8,128)}, f32[64,4608]{1,0:T(8,128)S(1)}, u32[]{:S(2)}) copy-start(f32[64,4608]{1,0:T(8,128)S(1)} %get-tuple-element.68) | copy-start | bytes 3538948
  36.3 6.0 %copy-start.22 = (bf16[2,4736]{1,0:T(2,128)(2,1)S(1)}, bf16[2,4736]{1,0:T(2,128)(2,1)}, u32[]{:S(2)}) copy-start(bf16[2,4736]{1,0:T(2,128)(2,1)} %fusion.5) | copy-start | bytes 56836
  36.4 7.8 %copy-start.1 = (bf16[4608,128]{1,0:T(8,128)(2,1)S(1)}, bf16[4608,128]{1,0:T(8,128)(2,1)}, u32[]{:S(2)}) copy-start(bf16[4608,128]{1,0:T(8,128)(2,1)} %wk.5) | copy-start | bytes 3538948
  36.6 34.8 %collective-permute-start.2 = (bf16[64,4608]{1,0:T(8,128)(2,1)S(1)}, bf16[64,4608]{1,0:T(8,128)(2,1)}, u32[]{:S(2)}, u32[]{:S(2)}) collective-permute-start(bf16[64,4608]{1,0:T(8,128)(2,1)S(1)} %multiply_convert_fusion.x0), channel_id=1, source_target_pairs={{0,6},{1,3},{2,0},{3,5},{4,2},{5,7},{6,4},{7,1},{8,14},{9,11},{10,... | collective-permute-start | bytes 1769480 | tf_op jit(solution)/shard_map/ppermute | solution.py:129
  38.4 33.0 %collective-permute-start.1 = (bf16[64,4608]{1,0:T(8,128)(2,1)S(1)}, bf16[64,4608]{1,0:T(8,128)(2,1)}, u32[]{:S(2)}, u32[]{:S(2)}) collective-permute-start(bf16[64,4608]{1,0:T(8,128)(2,1)S(1)} %multiply_convert_fusion.x0), channel_id=1, source_target_pairs={{0,2},{1,7},{2,4},{3,1},{4,6},{5,3},{6,0},{7,5},{8,10},{9,15},{10,... | collective-permute-start | bytes 1769480 | tf_op jit(solution)/shard_map/ppermute | solution.py:129
  42.4 1.8 collective-permute-start.6
  45.3 0.7 copy-start.5
  46.0 25.4 %all-to-all-start.1 = ((bf16[32,16,256]{2,1,0:T(8,128)(2,1)}), bf16[32,16,256]{2,1,0:T(8,128)(2,1)}, u32[]{:S(2)}, u32[]{:S(2)}) async-start(bf16[32,16,256]{2,1,0:T(8,128)(2,1)} %copy-done.5), calls=%async_computation.1 | async-start | bytes 524288 | tf_op jit(solution)/shard_map/all_to_all | solution.py:373
  54.4 17.9 %collective-permute-start.8 = (bf16[64,4608]{1,0:T(8,128)(2,1)S(1)}, bf16[64,4608]{1,0:T(8,128)(2,1)}, u32[]{:S(2)}, u32[]{:S(2)}) collective-permute-start(bf16[64,4608]{1,0:T(8,128)(2,1)S(1)} %multiply_convert_fusion.x0), channel_id=1, source_target_pairs={{0,1},{1,0},{2,3},{3,2},{4,5},{5,4},{6,7},{7,6},{8,9},{9,8},{10,11... | collective-permute-start | bytes 1769480 | tf_op jit(solution)/shard_map/ppermute | solution.py:129
  71.4 2.2 %collective-permute-start.9 = (bf16[64,4608]{1,0:T(8,128)(2,1)}, bf16[64,4608]{1,0:T(8,128)(2,1)S(1)}, u32[]{:S(2)}, u32[]{:S(2)}) collective-permute-start(bf16[64,4608]{1,0:T(8,128)(2,1)} %collective-permute-done.2.x4), channel_id=1, source_target_pairs={{0,1},{1,0},{2,3},{3,2},{4,5},{5,4},{6,7},{7,6},{8,9},{9,8},{10,11... | collective-permute-start | bytes 1769480 | tf_op jit(solution)/shard_map/ppermute | solution.py:129
  71.4 3.1 %collective-permute-start.10 = (bf16[64,4608]{1,0:T(8,128)(2,1)}, bf16[64,4608]{1,0:T(8,128)(2,1)S(1)}, u32[]{:S(2)}, u32[]{:S(2)}) collective-permute-start(bf16[64,4608]{1,0:T(8,128)(2,1)} %collective-permute-done.1.x2), channel_id=1, source_target_pairs={{0,1},{1,0},{2,3},{3,2},{4,5},{5,4},{6,7},{7,6},{8,9},{9,8},{10,11... | collective-permute-start | bytes 1769480 | tf_op jit(solution)/shard_map/ppermute | solution.py:129
  71.9 18.5 %collective-permute-start.7 = (bf16[64,4608]{1,0:T(8,128)(2,1)}, bf16[64,4608]{1,0:T(8,128)(2,1)S(1)}, u32[]{:S(2)}, u32[]{:S(2)}) collective-permute-start(bf16[64,4608]{1,0:T(8,128)(2,1)} %collective-permute-done.1.x2), channel_id=1, source_target_pairs={{0,2},{1,7},{2,4},{3,1},{4,6},{5,3},{6,0},{7,5},{8,10},{9,15},{10,... | collective-permute-start | bytes 1769480 | tf_op jit(solution)/shard_map/ppermute | solution.py:129
  74.5 1.7 copy-start.3
  76.2 0.9 copy-start.7
  77.1 0.9 copy-start.9
  78.0 24.3 %copy-start.4 = (bf16[4608,256]{1,0:T(8,128)(2,1)S(1)}, bf16[4608,256]{1,0:T(8,128)(2,1)}, u32[]{:S(2)}) copy-start(bf16[4608,256]{1,0:T(8,128)(2,1)} %wq.3) | copy-start | bytes 7077892
  78.0 24.3 %copy-start.11 = (f32[128,128]{1,0:T(8,128)S(1)}, f32[128,128]{1,0:T(8,128)}, u32[]{:S(2)}) copy-start(f32[128,128]{1,0:T(8,128)} %copy-done.10) | copy-start | bytes 196612
  78.0 24.3 %copy-start.13 = (f32[128,128]{1,0:T(8,128)S(1)}, f32[128,128]{1,0:T(8,128)}, u32[]{:S(2)}) copy-start(f32[128,128]{1,0:T(8,128)} %copy-done.12) | copy-start | bytes 196612
  81.7 10.9 %collective-permute-start.13 = (bf16[384,256]{1,0:T(8,128)(2,1)S(1)}, bf16[384,256]{1,0:T(8,128)(2,1)S(1)}, u32[]{:S(2)}, u32[]{:S(2)}) collective-permute-start(bf16[384,256]{1,0:T(8,128)(2,1)S(1)} %get-tuple-element.50.refs_0_), channel_id=1, source_target_pairs={{0,24},{8,32},{16,40},{24,48},{32,56},{40,64},{48,72},{56,80},{64,... | collective-permute-start | bytes 589832 | tf_op jit(solution)/shard_map/ppermute | solution.py:383
  84.7 11.9 %collective-permute-start.12 = (bf16[384,256]{1,0:T(8,128)(2,1)S(1)}, bf16[384,256]{1,0:T(8,128)(2,1)S(1)}, u32[]{:S(2)}, u32[]{:S(2)}) collective-permute-start(bf16[384,256]{1,0:T(8,128)(2,1)S(1)} %get-tuple-element.50.refs_0_), channel_id=1, source_target_pairs={{0,16},{8,24},{16,32},{24,40},{32,48},{40,56},{48,64},{56,72},{64,... | collective-permute-start | bytes 589832 | tf_op jit(solution)/shard_map/ppermute | solution.py:383
  88.2 12.1 %collective-permute-start.11 = (bf16[384,256]{1,0:T(8,128)(2,1)S(1)}, bf16[384,256]{1,0:T(8,128)(2,1)S(1)}, u32[]{:S(2)}, u32[]{:S(2)}) collective-permute-start(bf16[384,256]{1,0:T(8,128)(2,1)S(1)} %get-tuple-element.50.refs_0_), channel_id=1, source_target_pairs={{0,8},{8,16},{16,24},{24,32},{32,40},{40,48},{48,56},{56,64},{64,7... | collective-permute-start | bytes 589832 | tf_op jit(solution)/shard_map/ppermute | solution.py:383
  100.3 2.0 %collective-permute-start.14 = (bf16[64,4608]{1,0:T(8,128)(2,1)S(1)}, bf16[64,4608]{1,0:T(8,128)(2,1)S(1)}, u32[]{:S(2)}, u32[]{:S(2)}) collective-permute-start(bf16[64,4608]{1,0:T(8,128)(2,1)S(1)} %collective-permute-done.7.x0), channel_id=1, source_target_pairs={{0,1},{1,0},{2,3},{3,2},{4,5},{5,4},{6,7},{7,6},{8,9},{9,8},{10,11... | collective-permute-start | bytes 1769480 | tf_op jit(solution)/shard_map/ppermute | solution.py:129
  102.3 14.6 %copy-start.14 = (s32[4,128]{1,0:T(4,128)S(1)}, s32[4,128]{1,0:T(4,128)}, u32[]{:S(2)}) copy-start(s32[4,128]{1,0:T(4,128)} %pattern.1) | copy-start | bytes 6148
  103.2 8.1 %collective-permute-start.17 = (bf16[128,256]{1,0:T(8,128)(2,1)S(1)}, bf16[128,256]{1,0:T(8,128)(2,1)S(1)}, u32[]{:S(2)}, u32[]{:S(2)}) collective-permute-start(bf16[128,256]{1,0:T(8,128)(2,1)S(1)} %get-tuple-element.51.refs_1_), channel_id=1, source_target_pairs={{0,24},{8,32},{16,40},{24,48},{32,56},{40,64},{48,72},{56,80},{64,... | collective-permute-start | bytes 196616 | tf_op jit(solution)/shard_map/ppermute | solution.py:387
  105.1 8.6 %collective-permute-start.16 = (bf16[128,256]{1,0:T(8,128)(2,1)S(1)}, bf16[128,256]{1,0:T(8,128)(2,1)S(1)}, u32[]{:S(2)}, u32[]{:S(2)}) collective-permute-start(bf16[128,256]{1,0:T(8,128)(2,1)S(1)} %get-tuple-element.51.refs_1_), channel_id=1, source_target_pairs={{0,16},{8,24},{16,32},{24,40},{32,48},{40,56},{48,64},{56,72},{64,... | collective-permute-start | bytes 196616 | tf_op jit(solution)/shard_map/ppermute | solution.py:387
  108.5 8.3 %collective-permute-start.15 = (bf16[128,256]{1,0:T(8,128)(2,1)S(1)}, bf16[128,256]{1,0:T(8,128)(2,1)S(1)}, u32[]{:S(2)}, u32[]{:S(2)}) collective-permute-start(bf16[128,256]{1,0:T(8,128)(2,1)S(1)} %get-tuple-element.51.refs_1_), channel_id=1, source_target_pairs={{0,8},{8,16},{16,24},{24,32},{32,40},{40,48},{48,56},{56,64},{64,7... | collective-permute-start | bytes 196616 | tf_op jit(solution)/shard_map/ppermute | solution.py:387
  122.2 1.7 collective-permute-start.18
  126.9 34.3 %collective-permute-start.20 = (bf16[64,4608]{1,0:T(8,128)(2,1)S(1)}, bf16[64,4608]{1,0:T(8,128)(2,1)S(1)}, u32[]{:S(2)}, u32[]{:S(2)}) collective-permute-start(bf16[64,4608]{1,0:T(8,128)(2,1)S(1)} %get-tuple-element.64), channel_id=1, source_target_pairs={{0,2},{1,7},{2,4},{3,1},{4,6},{5,3},{6,0},{7,5},{8,10},{9,15},{10,... | collective-permute-start | bytes 1769480 | tf_op jit(solution)/shard_map/ppermute | solution.py:129
  130.5 30.9 %collective-permute-start.19 = (bf16[64,4608]{1,0:T(8,128)(2,1)S(1)}, bf16[64,4608]{1,0:T(8,128)(2,1)S(1)}, u32[]{:S(2)}, u32[]{:S(2)}) collective-permute-start(bf16[64,4608]{1,0:T(8,128)(2,1)S(1)} %get-tuple-element.62), channel_id=1, source_target_pairs={{0,6},{1,3},{2,0},{3,5},{4,2},{5,7},{6,4},{7,1},{8,14},{9,11},{10,... | collective-permute-start | bytes 1769480 | tf_op jit(solution)/shard_map/ppermute | solution.py:129
  161.4 12.1 %collective-permute-start.21 = (bf16[64,4608]{1,0:T(8,128)(2,1)S(1)}, bf16[64,4608]{1,0:T(8,128)(2,1)S(1)}, u32[]{:S(2)}, u32[]{:S(2)}) collective-permute-start(bf16[64,4608]{1,0:T(8,128)(2,1)S(1)} %add_convert_fusion.1), channel_id=1, source_target_pairs={{0,2},{1,7},{2,4},{3,1},{4,6},{5,3},{6,0},{7,5},{8,10},{9,15},{10,... | collective-permute-start | bytes 1769480 | tf_op jit(solution)/shard_map/ppermute | solution.py:129
  173.4 1.3 copy-start.18
  173.4 1.3 copy-start.23
where the time goes:
time: 178 us; the launch traced here: 176 us
  waiting for transfers between devices  78 us (44%)
  starting transfers between devices  52.2 us (29%)
  Pallas kernels  19.2 us (11%)
  local copies, waits for them, and re-layouts  17 us (10%)
  other arithmetic  7.23 us (4%)
  matrix products  1.86 us (1%)
    ppermute x16, waiting for transfers between devices, to(): return lax.ppermute(values, 'tensor', pairs)  45.7 us
    ppermute x16, starting transfers between devices, to(): return lax.ppermute(values, 'tensor', pairs)  18.7 us
    all_to_all x1, waiting for transfers between devices, body(): prompt = lax.all_to_all(early_kv, 'dp', 0, 0, tiled=True)  16.9 us
    ppermute x3, waiting for transfers between devices, body(): kvs_a = [kv_a] + [lax.ppermute(kv_a, 'dp', shift) for shift in shifts]  9.83 us
    all_to_all x1, starting transfers between devices, body(): lax.all_to_all(send.reshape(n_dp, per_peer, width), 'dp', 0, 0, tiled=True)  8.62 us
    unnamed x50, local copies, waits for them, and re-layouts  8.57 us
    ppermute x3, starting transfers between devices, body(): kvs_a = [kv_a] + [lax.ppermute(kv_a, 'dp', shift) for shift in shifts]  8.41 us
    all_to_all x1, starting transfers between devices, body(): prompt = lax.all_to_all(early_kv, 'dp', 0, 0, tiled=True)  8.38 us
  transfers between devices with their start and end apart: 24, of which 14 were waited for; matrix products, arithmetic and copies ran while one was open for 9% of the time, Pallas kernels for 6%

commit v1 on v0

--- a/solution.py
+++ b/solution.py
@@ -27,6 +27,7 @@
 SIB = [(t, t ^ 1) for t in range(8)]
 VMEM_BYTES = 16 << 20
 TILES = 6
+CHUNKS = 3
 OTHER = (0, 2, 1, 3)
 
 
@@ -129,30 +130,59 @@
     return lax.ppermute(values, "tensor", pairs)
 
 
-def qkv(pieces, wq, wk, wv, cos, sin):
-    x = jnp.concatenate([r[...] for r in pieces], axis=0)
+def turned(v, c, s):
+    return (v * c + pltpu.roll(v, HD // 2, 1) * s).astype(jnp.bfloat16)
+
+
+def near_kernel(x0, x1, x2, x3, x4, x5, wq, wk, wv, cos, sin, q_out, kv_out, buf, tab, sems):
+    step = D // CHUNKS
+
+    def copies(n):
+        rows = pl.ds(n * step, step)
+        return [
+            pltpu.make_async_copy(w.at[rows], buf.at[rows, pl.ds(start, size)], sems.at[n, i])
+            for i, (w, start, size) in enumerate(
+                ((wq, 0, 2 * HD), (wk, 2 * HD, HD), (wv, 3 * HD, HD))
+            )
+        ]
+
+    tables = [
+        pltpu.make_async_copy(t, tab.at[i], sems.at[CHUNKS, i]) for i, t in enumerate((cos, sin))
+    ]
+    for n in range(CHUNKS):
+        for copy in copies(n):
+            copy.start()
+    for copy in tables:
+        copy.start()
+    total = None
+    for n in range(CHUNKS):
+        for copy in copies(n):
+            copy.wait()
+        cols = slice(n * step, (n + 1) * step)
+        x = jnp.concatenate([r[:, cols] for r in (x0, x1, x2, x3, x4, x5)], axis=0)
+        part = jnp.dot(x, buf[cols], preferred_element_type=jnp.float32)
+        total = part if total is None else total + part
+    for copy in tables:
+        copy.wait()
+    c = tab[0]
+    s = tab[1]
+    q_out[0] = turned(total[:, :HD], c, s)
+    q_out[1] = turned(total[:, HD : 2 * HD], c, s)
+    kv_out[:, :HD] = turned(total[:, 2 * HD : 3 * HD], c, s)
+    kv_out[:, HD:] = total[:, 3 * HD :].astype(jnp.bfloat16)
+
+
+def far_kernel(x0, x1, wq, wk, wv, cos, sin, q_in, q_out, kv_out):
+    x = jnp.concatenate([x0[...], x1[...]], axis=0)
     c = cos[...]
     s = sin[...]
-
-    def turn(v):
-        return (v * c + pltpu.roll(v, HD // 2, 1) * s).astype(jnp.bfloat16)
-
     q = jnp.dot(x, wq[...], preferred_element_type=jnp.float32)
     wkv = jnp.concatenate([wk[...], wv[...]], axis=1)
     kv = jnp.dot(x, wkv, preferred_element_type=jnp.float32)
-    return turn(q[:, :HD]), turn(q[:, HD:]), turn(kv[:, :HD]), kv[:, HD:].astype(jnp.bfloat16)
-
-
-def near_kernel(x0, x1, x2, x3, x4, x5, wq, wk, wv, cos, sin, q_out, kv_out):
-    q0, q1, k, v = qkv((x0, x1, x2, x3, x4, x5), wq, wk, wv, cos, sin)
-    q_out[0] = q0
-    q_out[1] = q1
-    kv_out[:, :HD] = k
-    kv_out[:, HD:] = v
-
-
-def far_kernel(x0, x1, wq, wk, wv, cos, sin, q_in, q_out, kv_out):
-    q0, q1, k, v = qkv((x0, x1), wq, wk, wv, cos, sin)
+    q0 = turned(q[:, :HD], c, s)
+    q1 = turned(q[:, HD:], c, s)
+    k = turned(kv[:, :HD], c, s)
+    v = kv[:, HD:].astype(jnp.bfloat16)
     near = SHARD - BLK
     q_out[:near] = q_in[0]
     q_out[near:SHARD] = q0
@@ -164,17 +194,24 @@
 
 def project_near(*args):
     rows = SHARD - BLK
+    hbm = pl.BlockSpec(memory_space=pltpu.HBM)
+    rest = [pltpu.with_memory_space_constraint(a, pltpu.HBM) for a in args[6:]]
     return pl.pallas_call(
         near_kernel,
-        in_specs=[VMEM] * len(args),
+        in_specs=[VMEM] * 6 + [hbm] * 5,
         out_specs=[VMEM] * 2,
         out_shape=[
             jax.ShapeDtypeStruct((2, rows, HD), jnp.bfloat16),
             jax.ShapeDtypeStruct((rows, 2 * HD), jnp.bfloat16),
         ],
+        scratch_shapes=[
+            pltpu.VMEM((D, 4 * HD), jnp.bfloat16),
+            pltpu.VMEM((2, rows, HD), jnp.float32),
+            pltpu.SemaphoreType.DMA((CHUNKS + 1, 3)),
+        ],
         compiler_params=pltpu.CompilerParams(vmem_limit_bytes=VMEM_BYTES),
         name="project_near",
-    )(*args)
+    )(*args[:6], *rest)
 
 
 def project_far(*args):
@@ -357,7 +394,7 @@
     column = [to(piece, OUT), to(piece, BACK), to(piece, FAR)]
     w_sib = to(w_out, SIB)
 
-    got, w_sib, _ = lax.optimization_barrier((got, w_sib, cos_a))
+    got, _ = lax.optimization_barrier((got, cos_a))
     got = got.reshape(SLOTS, width)
     arrange = order_ids[:, None] == got[:, D].astype(jnp.int32)[None, :]
     packed = jnp.dot(arrange.astype(bf16), got[:, :D], preferred_element_type=jnp.float32).astype(bf16)
@@ -372,7 +409,7 @@
     early_kv = early_keys(lengths, early, to(early, SIB), norm_gain, w_key, w_value, n_dp)
     prompt = lax.all_to_all(early_kv, "dp", 0, 0, tiled=True)
     prompt = prompt.reshape(SHARD, 2 * HD)
-    near_o, near_b, prompt = lax.optimization_barrier((near_o, near_b, prompt))
+    near_o, near_b, prompt, w_sib = lax.optimization_barrier((near_o, near_b, prompt, w_sib))
     far_own = to(near_o, OUT)
     near_os = to(near_b, SIB)
     near_bs = to(near_o, SIB)

time: 178 us -> 165 us (0.927)
  local copies, waits for them, and re-layouts: 17 us -> 4.75 us
  other arithmetic: 7.23 us -> 3.1 us
  starting transfers between devices: 52.2 us -> 55.6 us
  Pallas kernels: 19.2 us -> 21.4 us
    unnamed x50 -> x32, local copies, waits for them, and re-layouts: 8.57 us -> 3.34 us
    ppermute x16, starting transfers between devices: 18.7 us -> 21.8 us  [to(): return lax.ppermute(values, 'tensor', pairs)]
    reshape x1, local copies, waits for them, and re-layouts: 3.05 us -> 0.23 us  [body(): got = got.reshape(SLOTS, width)]
    ppermute x3, waiting for transfers between devices: 9.83 us -> 7.09 us  [body(): kvs_a = [kv_a] + [lax.ppermute(kv_a, 'dp', shift) for shift in shifts]]
    slice x3, local copies, waits for them, and re-layouts: 2.7 us -> 0.04 us  [body(): early = jnp.concatenate([first] + [c[:per_peer] for c in column], axis=0)]
    concatenate x2, other arithmetic: 2.15 us -> 0.06 us  [body(): jnp.concatenate([send_rows, jnp.broadcast_to(send_slots.astype(bf16)[:, N...]
    all_to_all x1, waiting for transfers between devices: 16.9 us -> 18.7 us  [body(): prompt = lax.all_to_all(early_kv, 'dp', 0, 0, tiled=True)]
  transfers between devices with their start and end apart: 24 -> 24, of which waited for: 14 -> 13; matrix products, arithmetic and copies ran while one was open for 9% -> 1% of each run, Pallas kernels for 6% -> 7%
where the time goes in v1:
time: 165 us; the launch traced here: 164 us
  waiting for transfers between devices  78.3 us (47%)
  starting transfers between devices  55.6 us (34%)
  Pallas kernels  21.4 us (13%)
  local copies, waits for them, and re-layouts  4.75 us (3%)
  other arithmetic  3.1 us (2%)
    ppermute x16, waiting for transfers between devices, to(): return lax.ppermute(values, 'tensor', pairs)  47 us
    ppermute x16, starting transfers between devices, to(): return lax.ppermute(values, 'tensor', pairs)  21.8 us
    all_to_all x1, waiting for transfers between devices, body(): prompt = lax.all_to_all(early_kv, 'dp', 0, 0, tiled=True)  18.7 us
    all_to_all x1, starting transfers between devices, body(): lax.all_to_all(send.reshape(n_dp, per_peer, width), 'dp', 0, 0, tiled=True)  8.58 us
    ppermute x3, starting transfers between devices, body(): kvs_a = [kv_a] + [lax.ppermute(kv_a, 'dp', shift) for shift in shifts]  8.42 us
    ppermute x3, starting transfers between devices, body(): kvs_c = [kv_c] + [lax.ppermute(kv_c, 'dp', shift) for shift in shifts]  8.42 us
    all_to_all x1, starting transfers between devices, body(): prompt = lax.all_to_all(early_kv, 'dp', 0, 0, tiled=True)  8.36 us
    ppermute x3, waiting for transfers between devices, body(): kvs_a = [kv_a] + [lax.ppermute(kv_a, 'dp', shift) for shift in shifts]  7.09 us
  transfers between devices with their start and end apart: 24, of which 13 were waited for; matrix products, arithmetic and copies ran while one was open for 1% of the time, Pallas kernels for 7%

profile of v1, /device:TPU:40, one launch (start us, length us, event | category | flops | bytes accessed | tf_op | source)
XLA Modules:
  0.0 164.2 jit_solution(14137810668471657839)
XLA Ops:
  0.0 0.7 and_select_fusion.1
  0.7 0.2 convert_reduce_fusion.1
  0.9 0.1 select_reduce_fusion
  1.0 0.0 copy-done
  1.1 0.3 convolution_convert_fusion.1
  1.4 0.1 broadcast_in_dim.18
  1.5 0.0 copy-start.15
  1.5 1.1 reshape.41
  2.6 8.6 %all-to-all-start = ((bf16[32,2,4736]{2,1,0:T(2,128)(2,1)}), bf16[32,2,4736]{2,1,0:T(2,128)(2,1)S(1)}, u32[]{:S(2)}, u32[]{:S(2)}) async-start(bf16[32,2,4736]{2,1,0:T(2,128)(2,1)} %reshape.41), calls=%async_computation | async-start | bytes 1212416 | tf_op jit(solution)/shard_map/all_to_all | solution.py:386
  11.2 0.1 fusion.3
  11.3 6.4 %collective-permute-start.4 = (bf16[8,4736]{1,0:T(8,128)(2,1)S(1)}, bf16[8,4736]{1,0:T(8,128)(2,1)S(1)}, u32[]{:S(2)}, u32[]{:S(2)}) collective-permute-start(bf16[8,4736]{1,0:T(8,128)(2,1)S(1)} %fusion.3), channel_id=1, source_target_pairs={{0,4},{1,5},{2,6},{3,7},{4,0},{5,1},{6,2},{7,3},{8,12},{9,13},{10,... | collective-permute-start | bytes 227336 | tf_op jit(solution)/shard_map/ppermute | solution.py:130
  17.6 0.6 collective-permute-start.3
  18.2 2.4 %collective-permute-start.2 = (bf16[8,4736]{1,0:T(8,128)(2,1)S(1)}, bf16[8,4736]{1,0:T(8,128)(2,1)S(1)}, u32[]{:S(2)}, u32[]{:S(2)}) collective-permute-start(bf16[8,4736]{1,0:T(8,128)(2,1)S(1)} %fusion.3), channel_id=1, source_target_pairs={{0,2},{1,7},{2,4},{3,1},{4,6},{5,3},{6,0},{7,5},{8,10},{9,15},{10,... | collective-permute-start | bytes 227336 | tf_op jit(solution)/shard_map/ppermute | solution.py:130
  20.6 2.0 %tables.1 = (f32[384,128]{1,0:T(8,128)S(1)}, f32[384,128]{1,0:T(8,128)S(1)}, f32[128,128]{1,0:T(8,128)S(1)}, f32[128,128]{1,0:T(8,128)S(1)}) custom-call(s32[17]{0:T(128)S(1)} %copy-done.9, f32[1,128]{1,0:T(1,128)S(1)} %copy-done.10), custom_call_target="tpu_custom_call" | custom-call | tf_op jit(solution)/shard_map/tables/pallas_call | solution.py:81
  22.6 0.7 copy-done.6
  23.3 0.7 copy-done.7
  24.0 0.2 reshape.42
  24.2 0.1 convert_reduce_fusion
  24.3 0.4 multiply_reduce_fusion.1
  24.8 1.0 copy-done.11
  25.8 0.2 multiply_convert_fusion.x0
  25.9 5.1 %collective-permute-start.1 = (bf16[64,4608]{1,0:T(8,128)(2,1)S(1)}, bf16[64,4608]{1,0:T(8,128)(2,1)S(1)}, u32[]{:S(2)}, u32[]{:S(2)}) collective-permute-start(bf16[64,4608]{1,0:T(8,128)(2,1)S(1)} %multiply_convert_fusion.x0), channel_id=1, source_target_pairs={{0,6},{1,3},{2,0},{3,5},{4,2},{5,7},{6,4},{7,1},{8,14},{9,11},{10,... | collective-permute-start | bytes 1769480 | tf_op jit(solution)/shard_map/ppermute | solution.py:130
  31.1 0.3 collective-permute-start
  31.4 0.1 pad_maximum_fusion.1.own
  31.5 0.1 collective-permute-start.5
  31.6 1.2 collective-permute-done.5.sib
  32.9 1.8 %early.1 = bf16[32,16,256]{2,1,0:T(8,128)(2,1)} custom-call(s32[17]{0:T(128)S(1)} %copy-done.9, f32[1,128]{1,0:T(1,128)S(1)} %copy-done.10, bf16[8,4736]{1,0:T(8,128)(2,1)S(1)} %pad_maximum_fusion.1.own, bf16[8,4736]{1,0:T(8,128)(2,1)S(1)} %collective-permute-done.5.sib, f32[1,4608]{1,0:T(1,128)S(1)} %broadcast_in_dim.19.gain, ...), custom_call_target="tpu_custom_call" | custom-call | tf_op jit(solution)/shard_map/early/pallas_call | solution.py:115
  34.7 8.4 %all-to-all-start.1 = ((bf16[32,16,256]{2,1,0:T(8,128)(2,1)}), bf16[32,16,256]{2,1,0:T(8,128)(2,1)S(1)}, u32[]{:S(2)}, u32[]{:S(2)}) async-start(bf16[32,16,256]{2,1,0:T(8,128)(2,1)} %early.1), calls=%async_computation.1 | async-start | bytes 524288 | tf_op jit(solution)/shard_map/all_to_all | solution.py:410
  43.1 0.1 collective-permute-start.8
  43.2 18.7 %all-to-all-done.1 = bf16[32,16,256]{2,1,0:T(8,128)(2,1)S(1)} async-done(((bf16[32,16,256]{2,1,0:T(8,128)(2,1)}), bf16[32,16,256]{2,1,0:T(8,128)(2,1)S(1)}, u32[]{:S(2)}, u32[]{:S(2)}) %all-to-all-start.1) | async-done | bytes 262176 | tf_op jit(solution)/shard_map/all_to_all | solution.py:410
  61.9 0.1 collective-permute-start.9
  62.0 0.5 collective-permute-start.10
  62.5 1.5 collective-permute-start.7
  64.0 0.0 collective-permute-done.9.x3
  64.0 0.8 collective-permute-done.10.x5
  64.9 4.3 %project_near.1 = (bf16[2,384,128]{2,1,0:T(8,128)(2,1)S(1)}, bf16[384,256]{1,0:T(8,128)(2,1)S(1)}) custom-call(bf16[64,4608]{1,0:T(8,128)(2,1)S(1)} %multiply_convert_fusion.x0, bf16[64,4608]{1,0:T(8,128)(2,1)S(1)} %collective-permute-done.8.x1, bf16[64,4608]{1,0:T(8,128)(2,1)S(1)} %collective-permute-done.x2, ...), custom_call_target="tpu_custom_call" | custom-call | tf_op jit(solution)/shard_map/project_near/pallas_call | solution.py:199
  69.2 3.3 %collective-permute-start.13 = (bf16[384,256]{1,0:T(8,128)(2,1)S(1)}, bf16[384,256]{1,0:T(8,128)(2,1)S(1)}, u32[]{:S(2)}, u32[]{:S(2)}) collective-permute-start(bf16[384,256]{1,0:T(8,128)(2,1)S(1)} %get-tuple-element.50.refs_0_), channel_id=1, source_target_pairs={{0,24},{8,32},{16,40},{24,48},{32,56},{40,64},{48,72},{56,80},{64,... | collective-permute-start | bytes 589832 | tf_op jit(solution)/shard_map/ppermute | solution.py:420
  72.5 3.2 %collective-permute-start.12 = (bf16[384,256]{1,0:T(8,128)(2,1)S(1)}, bf16[384,256]{1,0:T(8,128)(2,1)S(1)}, u32[]{:S(2)}, u32[]{:S(2)}) collective-permute-start(bf16[384,256]{1,0:T(8,128)(2,1)S(1)} %get-tuple-element.50.refs_0_), channel_id=1, source_target_pairs={{0,16},{8,24},{16,32},{24,40},{32,48},{40,56},{48,64},{56,72},{64,... | collective-permute-start | bytes 589832 | tf_op jit(solution)/shard_map/ppermute | solution.py:420
  75.7 2.0 %collective-permute-start.11 = (bf16[384,256]{1,0:T(8,128)(2,1)S(1)}, bf16[384,256]{1,0:T(8,128)(2,1)S(1)}, u32[]{:S(2)}, u32[]{:S(2)}) collective-permute-start(bf16[384,256]{1,0:T(8,128)(2,1)S(1)} %get-tuple-element.50.refs_0_), channel_id=1, source_target_pairs={{0,8},{8,16},{16,24},{24,32},{32,40},{40,48},{48,56},{56,64},{64,7... | collective-permute-start | bytes 589832 | tf_op jit(solution)/shard_map/ppermute | solution.py:420
  77.7 3.2 %collective-permute-done.7.x0 = bf16[64,4608]{1,0:T(8,128)(2,1)S(1)} collective-permute-done((bf16[64,4608]{1,0:T(8,128)(2,1)S(1)}, bf16[64,4608]{1,0:T(8,128)(2,1)S(1)}, u32[]{:S(2)}, u32[]{:S(2)}) %collective-permute-start.7) | collective-permute-done | bytes 589856 | tf_op jit(solution)/shard_map/ppermute | solution.py:130
  80.8 3.5 %collective-permute-done.12.refs_4_ = bf16[384,256]{1,0:T(8,128)(2,1)S(1)} collective-permute-done((bf16[384,256]{1,0:T(8,128)(2,1)S(1)}, bf16[384,256]{1,0:T(8,128)(2,1)S(1)}, u32[]{:S(2)}, u32[]{:S(2)}) %collective-permute-start.12) | collective-permute-done | bytes 196640 | tf_op jit(solution)/shard_map/ppermute | solution.py:420
  84.3 3.6 %collective-permute-done.11.refs_2_ = bf16[384,256]{1,0:T(8,128)(2,1)S(1)} collective-permute-done((bf16[384,256]{1,0:T(8,128)(2,1)S(1)}, bf16[384,256]{1,0:T(8,128)(2,1)S(1)}, u32[]{:S(2)}, u32[]{:S(2)}) %collective-permute-start.11) | collective-permute-done | bytes 196640 | tf_op jit(solution)/shard_map/ppermute | solution.py:420
  87.9 2.0 %collective-permute-done.14.x1 = bf16[64,4608]{1,0:T(8,128)(2,1)S(1)} collective-permute-done((bf16[64,4608]{1,0:T(8,128)(2,1)S(1)}, bf16[64,4608]{1,0:T(8,128)(2,1)S(1)}, u32[]{:S(2)}, u32[]{:S(2)}) %collective-permute-start.14) | collective-permute-done | bytes 589856 | tf_op jit(solution)/shard_map/ppermute | solution.py:130
  90.0 0.9 project_far.1
  90.8 1.9 %collective-permute-start.17 = (bf16[128,256]{1,0:T(8,128)(2,1)S(1)}, bf16[128,256]{1,0:T(8,128)(2,1)S(1)}, u32[]{:S(2)}, u32[]{:S(2)}) collective-permute-start(bf16[128,256]{1,0:T(8,128)(2,1)S(1)} %get-tuple-element.51.refs_1_), channel_id=1, source_target_pairs={{0,24},{8,32},{16,40},{24,48},{32,56},{40,64},{48,72},{56,80},{64,... | collective-permute-start | bytes 196616 | tf_op jit(solution)/shard_map/ppermute | solution.py:424
  92.8 3.7 %collective-permute-start.16 = (bf16[128,256]{1,0:T(8,128)(2,1)S(1)}, bf16[128,256]{1,0:T(8,128)(2,1)S(1)}, u32[]{:S(2)}, u32[]{:S(2)}) collective-permute-start(bf16[128,256]{1,0:T(8,128)(2,1)S(1)} %get-tuple-element.51.refs_1_), channel_id=1, source_target_pairs={{0,16},{8,24},{16,32},{24,40},{32,48},{40,56},{48,64},{56,72},{64,... | collective-permute-start | bytes 196616 | tf_op jit(solution)/shard_map/ppermute | solution.py:424
  96.5 2.8 %collective-permute-start.15 = (bf16[128,256]{1,0:T(8,128)(2,1)S(1)}, bf16[128,256]{1,0:T(8,128)(2,1)S(1)}, u32[]{:S(2)}, u32[]{:S(2)}) collective-permute-start(bf16[128,256]{1,0:T(8,128)(2,1)S(1)} %get-tuple-element.51.refs_1_), channel_id=1, source_target_pairs={{0,8},{8,16},{16,24},{24,32},{32,40},{40,48},{48,56},{56,64},{64,7... | collective-permute-start | bytes 196616 | tf_op jit(solution)/shard_map/ppermute | solution.py:424
  99.3 2.0 %collective-permute-done.16.refs_5_ = bf16[128,256]{1,0:T(8,128)(2,1)S(1)} collective-permute-done((bf16[128,256]{1,0:T(8,128)(2,1)S(1)}, bf16[128,256]{1,0:T(8,128)(2,1)S(1)}, u32[]{:S(2)}, u32[]{:S(2)}) %collective-permute-start.16) | collective-permute-done | bytes 65568 | tf_op jit(solution)/shard_map/ppermute | solution.py:424
  101.3 3.4 %collective-permute-done.15.refs_3_ = bf16[128,256]{1,0:T(8,128)(2,1)S(1)} collective-permute-done((bf16[128,256]{1,0:T(8,128)(2,1)S(1)}, bf16[128,256]{1,0:T(8,128)(2,1)S(1)}, u32[]{:S(2)}, u32[]{:S(2)}) %collective-permute-start.15) | collective-permute-done | bytes 65568 | tf_op jit(solution)/shard_map/ppermute | solution.py:424
  104.8 6.2 %attend.1 = (bf16[256,256]{1,0:T(8,128)(2,1)S(1)}, bf16[256,256]{1,0:T(8,128)(2,1)S(1)}) custom-call(s32[4,128]{1,0:T(4,128)S(1)} %copy-done.8, bf16[1024,128]{1,0:T(8,128)(2,1)S(1)} %get-tuple-element.49.q2, bf16[384,256]{1,0:T(8,128)(2,1)S(1)} %get-tuple-element.50.refs_0_, bf16[128,256]{1,0:T(8,128)(2,1)S(1)} %get-tuple-element.51.refs_1_, ...), custom_call_target="tpu_custom_call" | custom-call | tf_op jit(solution)/shard_map/attend/pallas_call | solution.py:307
  111.0 0.1 collective-permute-start.18
  111.1 1.3 collective-permute-done.18.theirs
  112.5 3.0 %project_out.2 = (bf16[64,4608]{1,0:T(8,128)(2,1)S(1)}, bf16[64,4608]{1,0:T(8,128)(2,1)S(1)}) custom-call(bf16[256,256]{1,0:T(8,128)(2,1)S(1)} %get-tuple-element.56.ours, bf16[256,256]{1,0:T(8,128)(2,1)S(1)} %collective-permute-done.18.theirs, bf16[256,4608]{1,0:T(8,128)(2,1)} %w0.3, bf16[256,4608]{1,0:T(8,128)(2,1)} %collective-permute-done.6.w1), custom_call_target="tpu_custom_call" | custom-call | tf_op jit(solution)/shard_map/project_out/pallas_call | solution.py:352
  115.5 1.8 %collective-permute-start.20 = (bf16[64,4608]{1,0:T(8,128)(2,1)S(1)}, bf16[64,4608]{1,0:T(8,128)(2,1)S(1)}, u32[]{:S(2)}, u32[]{:S(2)}) collective-permute-start(bf16[64,4608]{1,0:T(8,128)(2,1)S(1)} %get-tuple-element.64), channel_id=1, source_target_pairs={{0,2},{1,7},{2,4},{3,1},{4,6},{5,3},{6,0},{7,5},{8,10},{9,15},{10,... | collective-permute-start | bytes 1769480 | tf_op jit(solution)/shard_map/ppermute | solution.py:130
  117.3 3.0 %project_out.3 = (f32[64,4608]{1,0:T(8,128)S(1)}, f32[64,4608]{1,0:T(8,128)S(1)}) custom-call(bf16[256,256]{1,0:T(8,128)(2,1)S(1)} %get-tuple-element.56.ours, bf16[256,256]{1,0:T(8,128)(2,1)S(1)} %collective-permute-done.18.theirs, bf16[256,4608]{1,0:T(8,128)(2,1)} %w0.3, bf16[256,4608]{1,0:T(8,128)(2,1)} %collective-permute-done.6.w1), custom_call_target="tpu_custom_call" | custom-call | tf_op jit(solution)/shard_map/project_out/pallas_call | solution.py:352
  120.3 2.8 %collective-permute-start.19 = (bf16[64,4608]{1,0:T(8,128)(2,1)S(1)}, bf16[64,4608]{1,0:T(8,128)(2,1)S(1)}, u32[]{:S(2)}, u32[]{:S(2)}) collective-permute-start(bf16[64,4608]{1,0:T(8,128)(2,1)S(1)} %get-tuple-element.62), channel_id=1, source_target_pairs={{0,6},{1,3},{2,0},{3,5},{4,2},{5,7},{6,4},{7,1},{8,14},{9,11},{10,... | collective-permute-start | bytes 1769480 | tf_op jit(solution)/shard_map/ppermute | solution.py:130
  123.1 26.6 %collective-permute-done.20 = bf16[64,4608]{1,0:T(8,128)(2,1)S(1)} collective-permute-done((bf16[64,4608]{1,0:T(8,128)(2,1)S(1)}, bf16[64,4608]{1,0:T(8,128)(2,1)S(1)}, u32[]{:S(2)}, u32[]{:S(2)}) %collective-permute-start.20) | collective-permute-done | bytes 589856 | tf_op jit(solution)/shard_map/ppermute | solution.py:130
  149.6 0.1 add_convert_fusion.1
  149.7 0.3 collective-permute-start.21
  150.0 0.8 collective-permute-done.19
  150.8 11.0 %collective-permute-done.21 = bf16[64,4608]{1,0:T(8,128)(2,1)S(1)} collective-permute-done((bf16[64,4608]{1,0:T(8,128)(2,1)S(1)}, bf16[64,4608]{1,0:T(8,128)(2,1)S(1)}, u32[]{:S(2)}, u32[]{:S(2)}) %collective-permute-start.21) | collective-permute-done | bytes 589856 | tf_op jit(solution)/shard_map/ppermute | solution.py:130
  161.8 0.3 multiply_reduce_fusion
  162.1 0.9 copy-done.12
  163.1 1.1 add_convert_fusion
  (48 shorter events, 0.2 us)
Async XLA Ops:
  0.0 1.1 copy-start
  1.5 9.7 %copy-start.15 = (pred[8]{0:T(512)(128)(4,1)S(1)}, pred[8]{0:T(512)(128)(4,1)}, u32[]{:S(2)}) copy-start(pred[8]{0:T(512)(128)(4,1)} %constant.45.clone.1) | copy-start | bytes 28
  2.6 18.0 %copy-start.9 = (s32[17]{0:T(128)S(1)}, s32[17]{0:T(128)}, u32[]{:S(2)}) copy-start(s32[17]{0:T(128)} %lengths.2) | copy-start | bytes 208
  2.6 18.0 %copy-start.10 = (f32[1,128]{1,0:T(1,128)S(1)}, f32[1,128]{1,0:T(1,128)}, u32[]{:S(2)}) copy-start(f32[1,128]{1,0:T(1,128)} %constant.47.clone.freq) | copy-start | bytes 1540
  2.6 21.4 %all-to-all-start = ((bf16[32,2,4736]{2,1,0:T(2,128)(2,1)}), bf16[32,2,4736]{2,1,0:T(2,128)(2,1)S(1)}, u32[]{:S(2)}, u32[]{:S(2)}) async-start(bf16[32,2,4736]{2,1,0:T(2,128)(2,1)} %reshape.41), calls=%async_computation | async-start | bytes 1212416 | tf_op jit(solution)/shard_map/all_to_all | solution.py:386
  11.3 19.8 %collective-permute-start.4 = (bf16[8,4736]{1,0:T(8,128)(2,1)S(1)}, bf16[8,4736]{1,0:T(8,128)(2,1)S(1)}, u32[]{:S(2)}, u32[]{:S(2)}) collective-permute-start(bf16[8,4736]{1,0:T(8,128)(2,1)S(1)} %fusion.3), channel_id=1, source_target_pairs={{0,4},{1,5},{2,6},{3,7},{4,0},{5,1},{6,2},{7,3},{8,12},{9,13},{10,... | collective-permute-start | bytes 227336 | tf_op jit(solution)/shard_map/ppermute | solution.py:130
  17.6 13.7 %collective-permute-start.3 = (bf16[8,4736]{1,0:T(8,128)(2,1)S(1)}, bf16[8,4736]{1,0:T(8,128)(2,1)S(1)}, u32[]{:S(2)}, u32[]{:S(2)}) collective-permute-start(bf16[8,4736]{1,0:T(8,128)(2,1)S(1)} %fusion.3), channel_id=1, source_target_pairs={{0,6},{1,3},{2,0},{3,5},{4,2},{5,7},{6,4},{7,1},{8,14},{9,11},{10,... | collective-permute-start | bytes 227336 | tf_op jit(solution)/shard_map/ppermute | solution.py:130
  18.2 13.1 %collective-permute-start.2 = (bf16[8,4736]{1,0:T(8,128)(2,1)S(1)}, bf16[8,4736]{1,0:T(8,128)(2,1)S(1)}, u32[]{:S(2)}, u32[]{:S(2)}) collective-permute-start(bf16[8,4736]{1,0:T(8,128)(2,1)S(1)} %fusion.3), channel_id=1, source_target_pairs={{0,2},{1,7},{2,4},{3,1},{4,6},{5,3},{6,0},{7,5},{8,10},{9,15},{10,... | collective-permute-start | bytes 227336 | tf_op jit(solution)/shard_map/ppermute | solution.py:130
  20.6 41.4 %collective-permute-start.6 = (bf16[256,4608]{1,0:T(8,128)(2,1)}, bf16[256,4608]{1,0:T(8,128)(2,1)}, u32[]{:S(2)}, u32[]{:S(2)}) collective-permute-start(bf16[256,4608]{1,0:T(8,128)(2,1)} %w0.3), channel_id=1, source_target_pairs={{0,1},{1,0},{2,3},{3,2},{4,5},{5,4},{6,7},{7,6},{8,9},{9,8},{10,11... | collective-permute-start | bytes 7077896 | tf_op jit(solution)/shard_map/ppermute | solution.py:130
  22.6 0.7 copy-start.6
  23.3 0.7 copy-start.7
  24.2 1.5 copy-start.13
  24.3 8.5 %copy-start.3 = (bf16[4608,128]{1,0:T(8,128)(2,1)S(1)}, bf16[4608,128]{1,0:T(8,128)(2,1)}, u32[]{:S(2)}) copy-start(bf16[4608,128]{1,0:T(8,128)(2,1)} %wv.5) | copy-start | bytes 3538948
  24.7 1.0 copy-start.11
  24.7 8.1 %copy-start.1 = (bf16[4608,128]{1,0:T(8,128)(2,1)S(1)}, bf16[4608,128]{1,0:T(8,128)(2,1)}, u32[]{:S(2)}) copy-start(bf16[4608,128]{1,0:T(8,128)(2,1)} %wk.5) | copy-start | bytes 3538948
  25.9 36.0 %collective-permute-start.1 = (bf16[64,4608]{1,0:T(8,128)(2,1)S(1)}, bf16[64,4608]{1,0:T(8,128)(2,1)S(1)}, u32[]{:S(2)}, u32[]{:S(2)}) collective-permute-start(bf16[64,4608]{1,0:T(8,128)(2,1)S(1)} %multiply_convert_fusion.x0), channel_id=1, source_target_pairs={{0,6},{1,3},{2,0},{3,5},{4,2},{5,7},{6,4},{7,1},{8,14},{9,11},{10,... | collective-permute-start | bytes 1769480 | tf_op jit(solution)/shard_map/ppermute | solution.py:130
  31.1 30.8 %collective-permute-start = (bf16[64,4608]{1,0:T(8,128)(2,1)S(1)}, bf16[64,4608]{1,0:T(8,128)(2,1)S(1)}, u32[]{:S(2)}, u32[]{:S(2)}) collective-permute-start(bf16[64,4608]{1,0:T(8,128)(2,1)S(1)} %multiply_convert_fusion.x0), channel_id=1, source_target_pairs={{0,2},{1,7},{2,4},{3,1},{4,6},{5,3},{6,0},{7,5},{8,10},{9,15},{10,... | collective-permute-start | bytes 1769480 | tf_op jit(solution)/shard_map/ppermute | solution.py:130
  31.5 1.4 collective-permute-start.5
  34.7 27.2 %all-to-all-start.1 = ((bf16[32,16,256]{2,1,0:T(8,128)(2,1)}), bf16[32,16,256]{2,1,0:T(8,128)(2,1)S(1)}, u32[]{:S(2)}, u32[]{:S(2)}) async-start(bf16[32,16,256]{2,1,0:T(8,128)(2,1)} %early.1), calls=%async_computation.1 | async-start | bytes 524288 | tf_op jit(solution)/shard_map/all_to_all | solution.py:410
  43.1 20.9 %collective-permute-start.8 = (bf16[64,4608]{1,0:T(8,128)(2,1)S(1)}, bf16[64,4608]{1,0:T(8,128)(2,1)S(1)}, u32[]{:S(2)}, u32[]{:S(2)}) collective-permute-start(bf16[64,4608]{1,0:T(8,128)(2,1)S(1)} %multiply_convert_fusion.x0), channel_id=1, source_target_pairs={{0,1},{1,0},{2,3},{3,2},{4,5},{5,4},{6,7},{7,6},{8,9},{9,8},{10,11... | collective-permute-start | bytes 1769480 | tf_op jit(solution)/shard_map/ppermute | solution.py:130
  61.9 2.1 %collective-permute-start.9 = (bf16[64,4608]{1,0:T(8,128)(2,1)S(1)}, bf16[64,4608]{1,0:T(8,128)(2,1)S(1)}, u32[]{:S(2)}, u32[]{:S(2)}) collective-permute-start(bf16[64,4608]{1,0:T(8,128)(2,1)S(1)} %collective-permute-done.1.x4), channel_id=1, source_target_pairs={{0,1},{1,0},{2,3},{3,2},{4,5},{5,4},{6,7},{7,6},{8,9},{9,8},{10,11... | collective-permute-start | bytes 1769480 | tf_op jit(solution)/shard_map/ppermute | solution.py:130
  62.0 2.8 %collective-permute-start.10 = (bf16[64,4608]{1,0:T(8,128)(2,1)S(1)}, bf16[64,4608]{1,0:T(8,128)(2,1)S(1)}, u32[]{:S(2)}, u32[]{:S(2)}) collective-permute-start(bf16[64,4608]{1,0:T(8,128)(2,1)S(1)} %collective-permute-done.x2), channel_id=1, source_target_pairs={{0,1},{1,0},{2,3},{3,2},{4,5},{5,4},{6,7},{7,6},{8,9},{9,8},{10,11... | collective-permute-start | bytes 1769480 | tf_op jit(solution)/shard_map/ppermute | solution.py:130
  62.5 18.3 %collective-permute-start.7 = (bf16[64,4608]{1,0:T(8,128)(2,1)S(1)}, bf16[64,4608]{1,0:T(8,128)(2,1)S(1)}, u32[]{:S(2)}, u32[]{:S(2)}) collective-permute-start(bf16[64,4608]{1,0:T(8,128)(2,1)S(1)} %collective-permute-done.x2), channel_id=1, source_target_pairs={{0,2},{1,7},{2,4},{3,1},{4,6},{5,3},{6,0},{7,5},{8,10},{9,15},{10,... | collective-permute-start | bytes 1769480 | tf_op jit(solution)/shard_map/ppermute | solution.py:130
  64.9 25.1 %copy-start.2 = (bf16[4608,128]{1,0:T(8,128)(2,1)S(1)}, bf16[4608,128]{1,0:T(8,128)(2,1)}, u32[]{:S(2)}) copy-start(bf16[4608,128]{1,0:T(8,128)(2,1)} %wk.5) | copy-start | bytes 3538948
  64.9 25.1 %copy-start.4 = (bf16[4608,128]{1,0:T(8,128)(2,1)S(1)}, bf16[4608,128]{1,0:T(8,128)(2,1)}, u32[]{:S(2)}) copy-start(bf16[4608,128]{1,0:T(8,128)(2,1)} %wv.5) | copy-start | bytes 3538948
  64.9 25.1 %copy-start.5 = (bf16[4608,256]{1,0:T(8,128)(2,1)S(1)}, bf16[4608,256]{1,0:T(8,128)(2,1)}, u32[]{:S(2)}) copy-start(bf16[4608,256]{1,0:T(8,128)(2,1)} %wq.3) | copy-start | bytes 7077892
  69.2 11.6 %collective-permute-start.13 = (bf16[384,256]{1,0:T(8,128)(2,1)S(1)}, bf16[384,256]{1,0:T(8,128)(2,1)S(1)}, u32[]{:S(2)}, u32[]{:S(2)}) collective-permute-start(bf16[384,256]{1,0:T(8,128)(2,1)S(1)} %get-tuple-element.50.refs_0_), channel_id=1, source_target_pairs={{0,24},{8,32},{16,40},{24,48},{32,56},{40,64},{48,72},{56,80},{64,... | collective-permute-start | bytes 589832 | tf_op jit(solution)/shard_map/ppermute | solution.py:420
  72.5 11.8 %collective-permute-start.12 = (bf16[384,256]{1,0:T(8,128)(2,1)S(1)}, bf16[384,256]{1,0:T(8,128)(2,1)S(1)}, u32[]{:S(2)}, u32[]{:S(2)}) collective-permute-start(bf16[384,256]{1,0:T(8,128)(2,1)S(1)} %get-tuple-element.50.refs_0_), channel_id=1, source_target_pairs={{0,16},{8,24},{16,32},{24,40},{32,48},{40,56},{48,64},{56,72},{64,... | collective-permute-start | bytes 589832 | tf_op jit(solution)/shard_map/ppermute | solution.py:420
  75.7 12.3 %collective-permute-start.11 = (bf16[384,256]{1,0:T(8,128)(2,1)S(1)}, bf16[384,256]{1,0:T(8,128)(2,1)S(1)}, u32[]{:S(2)}, u32[]{:S(2)}) collective-permute-start(bf16[384,256]{1,0:T(8,128)(2,1)S(1)} %get-tuple-element.50.refs_0_), channel_id=1, source_target_pairs={{0,8},{8,16},{16,24},{24,32},{32,40},{40,48},{48,56},{56,64},{64,7... | collective-permute-start | bytes 589832 | tf_op jit(solution)/shard_map/ppermute | solution.py:420
  87.9 2.0 %collective-permute-start.14 = (bf16[64,4608]{1,0:T(8,128)(2,1)S(1)}, bf16[64,4608]{1,0:T(8,128)(2,1)S(1)}, u32[]{:S(2)}, u32[]{:S(2)}) collective-permute-start(bf16[64,4608]{1,0:T(8,128)(2,1)S(1)} %collective-permute-done.7.x0), channel_id=1, source_target_pairs={{0,1},{1,0},{2,3},{3,2},{4,5},{5,4},{6,7},{7,6},{8,9},{9,8},{10,11... | collective-permute-start | bytes 1769480 | tf_op jit(solution)/shard_map/ppermute | solution.py:130
  89.9 14.8 %copy-start.8 = (s32[4,128]{1,0:T(4,128)S(1)}, s32[4,128]{1,0:T(4,128)}, u32[]{:S(2)}) copy-start(s32[4,128]{1,0:T(4,128)} %pattern.1) | copy-start | bytes 6148
  90.8 8.4 %collective-permute-start.17 = (bf16[128,256]{1,0:T(8,128)(2,1)S(1)}, bf16[128,256]{1,0:T(8,128)(2,1)S(1)}, u32[]{:S(2)}, u32[]{:S(2)}) collective-permute-start(bf16[128,256]{1,0:T(8,128)(2,1)S(1)} %get-tuple-element.51.refs_1_), channel_id=1, source_target_pairs={{0,24},{8,32},{16,40},{24,48},{32,56},{40,64},{48,72},{56,80},{64,... | collective-permute-start | bytes 196616 | tf_op jit(solution)/shard_map/ppermute | solution.py:424
  92.8 8.6 %collective-permute-start.16 = (bf16[128,256]{1,0:T(8,128)(2,1)S(1)}, bf16[128,256]{1,0:T(8,128)(2,1)S(1)}, u32[]{:S(2)}, u32[]{:S(2)}) collective-permute-start(bf16[128,256]{1,0:T(8,128)(2,1)S(1)} %get-tuple-element.51.refs_1_), channel_id=1, source_target_pairs={{0,16},{8,24},{16,32},{24,40},{32,48},{40,56},{48,64},{56,72},{64,... | collective-permute-start | bytes 196616 | tf_op jit(solution)/shard_map/ppermute | solution.py:424
  96.5 8.3 %collective-permute-start.15 = (bf16[128,256]{1,0:T(8,128)(2,1)S(1)}, bf16[128,256]{1,0:T(8,128)(2,1)S(1)}, u32[]{:S(2)}, u32[]{:S(2)}) collective-permute-start(bf16[128,256]{1,0:T(8,128)(2,1)S(1)} %get-tuple-element.51.refs_1_), channel_id=1, source_target_pairs={{0,8},{8,16},{16,24},{24,32},{32,40},{40,48},{48,56},{56,64},{64,7... | collective-permute-start | bytes 196616 | tf_op jit(solution)/shard_map/ppermute | solution.py:424
  111.0 1.4 collective-permute-start.18
  115.5 34.1 %collective-permute-start.20 = (bf16[64,4608]{1,0:T(8,128)(2,1)S(1)}, bf16[64,4608]{1,0:T(8,128)(2,1)S(1)}, u32[]{:S(2)}, u32[]{:S(2)}) collective-permute-start(bf16[64,4608]{1,0:T(8,128)(2,1)S(1)} %get-tuple-element.64), channel_id=1, source_target_pairs={{0,2},{1,7},{2,4},{3,1},{4,6},{5,3},{6,0},{7,5},{8,10},{9,15},{10,... | collective-permute-start | bytes 1769480 | tf_op jit(solution)/shard_map/ppermute | solution.py:130
  120.3 30.5 %collective-permute-start.19 = (bf16[64,4608]{1,0:T(8,128)(2,1)S(1)}, bf16[64,4608]{1,0:T(8,128)(2,1)S(1)}, u32[]{:S(2)}, u32[]{:S(2)}) collective-permute-start(bf16[64,4608]{1,0:T(8,128)(2,1)S(1)} %get-tuple-element.62), channel_id=1, source_target_pairs={{0,6},{1,3},{2,0},{3,5},{4,2},{5,7},{6,4},{7,1},{8,14},{9,11},{10,... | collective-permute-start | bytes 1769480 | tf_op jit(solution)/shard_map/ppermute | solution.py:130
  149.7 12.1 %collective-permute-start.21 = (bf16[64,4608]{1,0:T(8,128)(2,1)S(1)}, bf16[64,4608]{1,0:T(8,128)(2,1)S(1)}, u32[]{:S(2)}, u32[]{:S(2)}) collective-permute-start(bf16[64,4608]{1,0:T(8,128)(2,1)S(1)} %add_convert_fusion.1), channel_id=1, source_target_pairs={{0,2},{1,7},{2,4},{3,1},{4,6},{5,3},{6,0},{7,5},{8,10},{9,15},{10,... | collective-permute-start | bytes 1769480 | tf_op jit(solution)/shard_map/ppermute | solution.py:130
  161.8 1.3 copy-start.12
  161.8 1.3 copy-start.14

commit v2 on v1

--- a/solution.py
+++ b/solution.py
@@ -228,70 +228,102 @@
     )(*args)
 
 
-def attend_kernel(pattern, q2, *refs):
-    kvs = refs[:8]
-    prompt = refs[8]
-    ours, theirs, acc, tot = refs[9:]
+def attend_tile(q, blocks, acc, tot):
+    some = blocks[0][2]
+    for block in blocks[1:]:
+        some = some | block[2]
+
+    @pl.when(some)
+    def _():
+        k = jnp.concatenate([ref[row : row + BLK, :HD] for ref, row, _, _ in blocks], axis=0)
+        v = jnp.concatenate([ref[row : row + BLK, HD:] for ref, row, _, _ in blocks], axis=0)
+        scores = lax.dot_general(q[...], k, (((1,), (1,)), ((), ())), preferred_element_type=jnp.float32)
+        weights = jnp.exp2(jnp.tanh(scores * (QUERY_SCALE / SOFT_CAP)) * (SOFT_CAP * math.log2(math.e)))
+        rows = []
+        for i in range(2 * PLANES):
+            part = weights[i * BLK : (i + 1) * BLK]
+            cols = [
+                block[3][i % PLANES](part[:, j * BLK : (j + 1) * BLK]) for j, block in enumerate(blocks)
+            ]
+            rows.append(jnp.concatenate(cols, axis=1))
+        weights = jnp.concatenate(rows, axis=0)
+        sums = weights[:, :BLK]
+        for j in range(1, len(blocks)):
+            sums = sums + weights[:, j * BLK : (j + 1) * BLK]
+        tot[...] += sums
+        acc[...] += jnp.dot(weights.astype(jnp.bfloat16), v, preferred_element_type=jnp.float32)
+
+
+def scaled(flag):
+    return lambda part: part * flag.astype(jnp.float32)
+
+
+def causal(flag, core):
+    def mask(part):
+        flip = core * SLOTS
+        rows_id = lax.broadcasted_iota(jnp.int32, (BLK, BLK), 0) ^ flip
+        cols_id = lax.broadcasted_iota(jnp.int32, (BLK, BLK), 1) ^ flip
+        return jnp.where(cols_id <= rows_id, part, 0.0) * flag.astype(jnp.float32)
+
+    return mask
+
+
+def window_block(pattern, order, core, source, b, ref, row):
+    d = lax.axis_index("dp")
+    shard = jnp.maximum(d - source, 0)
+    flags = [
+        (pattern[order[i], shard * PLANES + order[b]] == 1).astype(jnp.int32) for i in range(PLANES)
+    ]
+    some = flags[0] + flags[1] + flags[2] + flags[3] > 0
+    if source:
+        some = some & (d - source >= 1)
+        flags = [jnp.where(some, f, 0) for f in flags]
+    masks = [causal(f, core) if source == 0 and i == b else scaled(f) for i, f in enumerate(flags)]
+    return ref, row, some, masks
+
+
+def attend_kernel(pattern, q, own_a, own_c, w1, w2, w3, prompt, acc, tot):
     acc[...] = jnp.zeros_like(acc)
     tot[...] = jnp.zeros_like(tot)
     core, order = plane_order()
     d = lax.axis_index("dp")
     lane = lax.broadcasted_iota(jnp.int32, (1, BLK), 1)
 
-    def block(ref, row, some, masks):
-        @pl.when(some)
-        def _():
-            k = ref[row : row + BLK, :HD]
-            v = ref[row : row + BLK, HD:]
-            scores = lax.dot_general(
-                q2[...], k, (((1,), (1,)), ((), ())), preferred_element_type=jnp.float32
-            )
-            weights = jnp.exp2(jnp.tanh(scores * (QUERY_SCALE / SOFT_CAP)) * (SOFT_CAP * math.log2(math.e)))
-            parts = []
-            for i in range(2 * PLANES):
-                parts.append(masks[i % PLANES](weights[i * BLK : (i + 1) * BLK]))
-            weights = jnp.concatenate(parts, axis=0)
-            tot[...] += weights
-            acc[...] += jnp.dot(weights.astype(jnp.bfloat16), v, preferred_element_type=jnp.float32)
-
-    def scaled(flag):
-        return lambda part: part * flag.astype(jnp.float32)
-
-    def causal(flag):
-        def mask(part):
-            flip = core * SLOTS
-            rows_id = lax.broadcasted_iota(jnp.int32, (BLK, BLK), 0) ^ flip
-            cols_id = lax.broadcasted_iota(jnp.int32, (BLK, BLK), 1) ^ flip
-            return jnp.where(cols_id <= rows_id, part, 0.0) * flag.astype(jnp.float32)
-
-        return mask
-
-    def seen(i, shard, plane):
-        return (pattern[order[i], shard * PLANES + plane] == 1).astype(jnp.int32)
-
-    for source in range(4):
-        shard = jnp.maximum(d - source, 0)
-        for b in range(PLANES):
-            flags = [seen(i, shard, order[b]) for i in range(PLANES)]
-            some = flags[0] + flags[1] + flags[2] + flags[3] > 0
-            if source:
-                some = some & (d - source >= 1)
-            masks = [causal(f) if source == 0 and i == b else scaled(f) for i, f in enumerate(flags)]
-            ref, row = (kvs[2 * source], b * BLK) if b < 3 else (kvs[2 * source + 1], 0)
-            block(ref, row, some, masks)
+    def window(source, b, ref, row):
+        return window_block(pattern, order, core, source, b, ref, row)
+
+    attend_tile(q, [window(0, 0, own_a, 0), window(0, 1, own_a, BLK)], acc, tot)
+    attend_tile(q, [window(0, 2, own_a, 2 * BLK), window(0, 3, own_c, 0)], acc, tot)
+    for source, ref in ((1, w1), (2, w2), (3, w3)):
+        attend_tile(q, [window(source, 0, ref, 0), window(source, 1, ref, BLK)], acc, tot)
+    attend_tile(q, [window(1, 2, w1, 2 * BLK), window(2, 2, w2, 2 * BLK)], acc, tot)
+    attend_tile(q, [window(3, 2, w3, 2 * BLK)], acc, tot)
 
     masks = []
     some = 0
     for i in range(PLANES):
-        flags = [seen(i, 0, order[b]) for b in range(PLANES)]
+        flags = [(pattern[order[i], order[b]] == 1).astype(jnp.int32) for b in range(PLANES)]
         some += flags[0] + flags[1] + flags[2] + flags[3]
         row = jnp.zeros((1, BLK), jnp.float32)
         for b in range(2 * PLANES):
             flag = flags[b if b < PLANES else OTHER[b - PLANES]]
             row = jnp.where(lane % 16 // 2 == b, flag.astype(jnp.float32), row)
         masks.append(lambda part, row=row: part * row)
-    for b in range(PLANES):
-        block(prompt, b * BLK, (some > 0) & (d >= 1), masks)
+    seen = (some > 0) & (d >= 1)
+    for b in range(0, PLANES, 2):
+        attend_tile(q, [(prompt, (b + j) * BLK, seen, masks) for j in range(2)], acc, tot)
+
+
+def attend_far_kernel(pattern, q, w1, w2, w3, acc_in, tot_in, ours, theirs, acc, tot):
+    acc[...] = acc_in[...]
+    tot[...] = tot_in[...]
+    core, order = plane_order()
+
+    def window(source, ref):
+        return window_block(pattern, order, core, source, 3, ref, 0)
+
+    attend_tile(q, [window(1, w1), window(2, w2)], acc, tot)
+    attend_tile(q, [window(3, w3)], acc, tot)
     for head in range(2):
         for i in range(PLANES):
             lo = head * SHARD + i * BLK
@@ -303,19 +335,27 @@
             theirs[j * SLOTS : (j + 1) * SLOTS, lanes] = part[SLOTS:]
 
 
-def attend(pattern, q2, kvs, prompt):
+def attend(pattern, *args):
     return pl.pallas_call(
         attend_kernel,
-        in_specs=[SMEM] + [VMEM] * 10,
+        in_specs=[SMEM] + [VMEM] * len(args),
+        out_specs=[VMEM] * 2,
+        out_shape=[jax.ShapeDtypeStruct((2 * SHARD, HD), jnp.float32)] * 2,
+        compiler_params=pltpu.CompilerParams(vmem_limit_bytes=VMEM_BYTES),
+        name="attend",
+    )(pattern, *args)
+
+
+def attend_far(pattern, *args):
+    return pl.pallas_call(
+        attend_far_kernel,
+        in_specs=[SMEM] + [VMEM] * len(args),
         out_specs=[VMEM] * 2,
         out_shape=[jax.ShapeDtypeStruct((PLANES * SLOTS, 2 * HD), jnp.bfloat16)] * 2,
-        scratch_shapes=[
-            pltpu.VMEM((1024, HD), jnp.float32),
-            pltpu.VMEM((1024, HD), jnp.float32),
-        ],
-        compiler_params=pltpu.CompilerParams(vmem_limit_bytes=VMEM_BYTES),
-        name="attend",
-    )(pattern, q2, *kvs, prompt)
+        scratch_shapes=[pltpu.VMEM((2 * SHARD, HD), jnp.float32)] * 2,
+        compiler_params=pltpu.CompilerParams(vmem_limit_bytes=VMEM_BYTES),
+        name="attend_far",
+    )(pattern, *args)
 
 
 def out_kernel(chunks, ours, theirs, w0, w1, first, second, buf, sems):
@@ -418,12 +458,12 @@
     )
     shifts = [[(s, s + k) for s in range(n_dp - k)] for k in (1, 2, 3)]
     kvs_a = [kv_a] + [lax.ppermute(kv_a, "dp", shift) for shift in shifts]
-    far_own, kvs_a = lax.optimization_barrier((far_own, kvs_a))
+    far_own, kv_a = lax.optimization_barrier((far_own, kv_a))
     far_s = to(far_own, SIB)
     q, kv_c = project_far(far_own, far_s, w_query, w_key, w_value, cos_c, sin_c, q_a)
-    kvs_c = [kv_c] + [lax.ppermute(kv_c, "dp", shift) for shift in shifts]
-    kvs = [x for pair in zip(kvs_a, kvs_c) for x in pair]
-    ours, theirs = attend(pattern, q, kvs, prompt)
+    kvs_c = [lax.ppermute(kv_c, "dp", shift) for shift in shifts]
+    acc, tot = attend(pattern, q, kv_a, kv_c, *kvs_a[1:], prompt)
+    ours, theirs = attend_far(pattern, q, *kvs_c, acc, tot)
 
     theirs = to(theirs, SIB)
     sum_far, sum_o = project_out((3, 1), bf16, ours, theirs, w_out, w_sib)

time: 165 us -> 163 us (0.988); the launches traced: 164 us -> 160 us
  waiting for transfers between devices: 78.3 us -> 70.6 us
  starting transfers between devices: 55.6 us -> 59.3 us
    ppermute x3, waiting for transfers between devices: 7.09 us -> 0.01 us  [body(): kvs_a = [kv_a] + [lax.ppermute(kv_a, 'dp', shift) for shift in shifts]]
    ppermute x3, waiting for transfers between devices: 5.49 us -> 1.58 us  [body(): kvs_c = [lax.ppermute(kv_c, 'dp', shift) for shift in shifts]]
    ppermute x16, waiting for transfers between devices: 47 us -> 50.3 us  [to(): return lax.ppermute(values, 'tensor', pairs)]
    ppermute x3, starting transfers between devices: 8.42 us -> 10.9 us  [body(): kvs_c = [lax.ppermute(kv_c, 'dp', shift) for shift in shifts]]
    pallas_call x1 -> x2, Pallas kernels: 6.23 us -> 5.84 us  [the longest x1 4.42 us: attend(): pl.pallas_call(attend_kernel, in_specs=[SMEM] + [VMEM] * len(args), out_s...]
  transfers between devices with their start and end apart: 24 -> 24, of which waited for: 13 -> 8; matrix products, arithmetic and copies ran while one was open for 1% -> 1% of each run, Pallas kernels for 7% -> 10%
where the time goes in v2:
time: 163 us; the launch traced here: 160 us
  waiting for transfers between devices  70.6 us (43%)
  starting transfers between devices  59.3 us (36%)
  Pallas kernels  21 us (13%)
  local copies, waits for them, and re-layouts  4.78 us (3%)
  other arithmetic  3.09 us (2%)
    ppermute x16, waiting for transfers between devices, to(): return lax.ppermute(values, 'tensor', pairs)  50.3 us
    ppermute x16, starting transfers between devices, to(): return lax.ppermute(values, 'tensor', pairs)  23.1 us
    all_to_all x1, waiting for transfers between devices, body(): prompt = lax.all_to_all(early_kv, 'dp', 0, 0, tiled=True)  18.7 us
    ppermute x3, starting transfers between devices, body(): kvs_c = [lax.ppermute(kv_c, 'dp', shift) for shift in shifts]  10.9 us
    all_to_all x1, starting transfers between devices, body(): lax.all_to_all(send.reshape(n_dp, per_peer, width), 'dp', 0, 0, tiled=True)  8.58 us
    ppermute x3, starting transfers between devices, body(): kvs_a = [kv_a] + [lax.ppermute(kv_a, 'dp', shift) for shift in shifts]  8.44 us
    all_to_all x1, starting transfers between devices, body(): prompt = lax.all_to_all(early_kv, 'dp', 0, 0, tiled=True)  8.36 us
    pallas_call x2, Pallas kernels, project_out(): pl.pallas_call(functools.partial(out_kernel, chunks), in_specs=[VMEM] * 2...  6.09 us
  transfers between devices with their start and end apart: 24, of which 8 were waited for; matrix products, arithmetic and copies ran while one was open for 1% of the time, Pallas kernels for 10%

profile of v2, /device:TPU:40, one launch (start us, length us, event | category | flops | bytes accessed | tf_op | source)
XLA Modules:
  0.0 159.9 jit_solution(16474526688489045514)
XLA Ops:
  0.0 0.7 and_select_fusion.1
  0.7 0.2 convert_reduce_fusion.1
  0.9 0.1 select_reduce_fusion
  1.0 0.0 copy-done
  1.1 0.3 convolution_convert_fusion.1
  1.4 0.1 broadcast_in_dim.18
  1.5 0.0 copy-start.15
  1.5 1.1 reshape.41
  2.6 8.6 %all-to-all-start = ((bf16[32,2,4736]{2,1,0:T(2,128)(2,1)}), bf16[32,2,4736]{2,1,0:T(2,128)(2,1)S(1)}, u32[]{:S(2)}, u32[]{:S(2)}) async-start(bf16[32,2,4736]{2,1,0:T(2,128)(2,1)} %reshape.41), calls=%async_computation | async-start | bytes 1212416 | tf_op jit(solution)/shard_map/all_to_all | solution.py:426
  11.2 0.1 fusion.3
  11.3 6.4 %collective-permute-start.4 = (bf16[8,4736]{1,0:T(8,128)(2,1)S(1)}, bf16[8,4736]{1,0:T(8,128)(2,1)S(1)}, u32[]{:S(2)}, u32[]{:S(2)}) collective-permute-start(bf16[8,4736]{1,0:T(8,128)(2,1)S(1)} %fusion.3), channel_id=1, source_target_pairs={{0,4},{1,5},{2,6},{3,7},{4,0},{5,1},{6,2},{7,3},{8,12},{9,13},{10,... | collective-permute-start | bytes 227336 | tf_op jit(solution)/shard_map/ppermute | solution.py:130
  17.6 0.6 collective-permute-start.3
  18.2 2.4 %collective-permute-start.2 = (bf16[8,4736]{1,0:T(8,128)(2,1)S(1)}, bf16[8,4736]{1,0:T(8,128)(2,1)S(1)}, u32[]{:S(2)}, u32[]{:S(2)}) collective-permute-start(bf16[8,4736]{1,0:T(8,128)(2,1)S(1)} %fusion.3), channel_id=1, source_target_pairs={{0,2},{1,7},{2,4},{3,1},{4,6},{5,3},{6,0},{7,5},{8,10},{9,15},{10,... | collective-permute-start | bytes 227336 | tf_op jit(solution)/shard_map/ppermute | solution.py:130
  20.6 2.0 %tables.1 = (f32[384,128]{1,0:T(8,128)S(1)}, f32[384,128]{1,0:T(8,128)S(1)}, f32[128,128]{1,0:T(8,128)S(1)}, f32[128,128]{1,0:T(8,128)S(1)}) custom-call(s32[17]{0:T(128)S(1)} %copy-done.9, f32[1,128]{1,0:T(1,128)S(1)} %copy-done.10), custom_call_target="tpu_custom_call" | custom-call | tf_op jit(solution)/shard_map/tables/pallas_call | solution.py:81
  22.6 0.7 copy-done.6
  23.3 0.7 copy-done.7
  24.0 0.2 reshape.42
  24.2 0.0 copy-start.13
  24.2 0.1 convert_reduce_fusion
  24.4 0.0 copy-start.3
  24.4 0.4 multiply_reduce_fusion.1
  24.8 0.0 copy-start.1
  24.8 1.0 copy-done.11
  25.8 0.2 multiply_convert_fusion.x0
  26.0 5.1 %collective-permute-start.1 = (bf16[64,4608]{1,0:T(8,128)(2,1)S(1)}, bf16[64,4608]{1,0:T(8,128)(2,1)S(1)}, u32[]{:S(2)}, u32[]{:S(2)}) collective-permute-start(bf16[64,4608]{1,0:T(8,128)(2,1)S(1)} %multiply_convert_fusion.x0), channel_id=1, source_target_pairs={{0,6},{1,3},{2,0},{3,5},{4,2},{5,7},{6,4},{7,1},{8,14},{9,11},{10,... | collective-permute-start | bytes 1769480 | tf_op jit(solution)/shard_map/ppermute | solution.py:130
  31.1 0.3 collective-permute-start
  31.4 0.1 pad_maximum_fusion.1.own
  31.5 0.1 collective-permute-start.5
  31.6 1.2 collective-permute-done.5.sib
  32.9 1.8 %early.1 = bf16[32,16,256]{2,1,0:T(8,128)(2,1)} custom-call(s32[17]{0:T(128)S(1)} %copy-done.9, f32[1,128]{1,0:T(1,128)S(1)} %copy-done.10, bf16[8,4736]{1,0:T(8,128)(2,1)S(1)} %pad_maximum_fusion.1.own, bf16[8,4736]{1,0:T(8,128)(2,1)S(1)} %collective-permute-done.5.sib, f32[1,4608]{1,0:T(1,128)S(1)} %broadcast_in_dim.19.gain, ...), custom_call_target="tpu_custom_call" | custom-call | tf_op jit(solution)/shard_map/early/pallas_call | solution.py:115
  34.7 8.4 %all-to-all-start.1 = ((bf16[32,16,256]{2,1,0:T(8,128)(2,1)}), bf16[32,16,256]{2,1,0:T(8,128)(2,1)S(1)}, u32[]{:S(2)}, u32[]{:S(2)}) async-start(bf16[32,16,256]{2,1,0:T(8,128)(2,1)} %early.1), calls=%async_computation.1 | async-start | bytes 524288 | tf_op jit(solution)/shard_map/all_to_all | solution.py:450
  43.1 0.1 collective-permute-start.8
  43.2 18.7 %all-to-all-done.1 = bf16[32,16,256]{2,1,0:T(8,128)(2,1)S(1)} async-done(((bf16[32,16,256]{2,1,0:T(8,128)(2,1)}), bf16[32,16,256]{2,1,0:T(8,128)(2,1)S(1)}, u32[]{:S(2)}, u32[]{:S(2)}) %all-to-all-start.1) | async-done | bytes 262176 | tf_op jit(solution)/shard_map/all_to_all | solution.py:450
  61.9 0.1 collective-permute-start.9
  62.0 0.5 collective-permute-start.10
  62.5 1.5 collective-permute-start.7
  64.0 0.0 collective-permute-done.9.x3
  64.0 0.8 collective-permute-done.10.x5
  64.9 4.3 %project_near.1 = (bf16[2,384,128]{2,1,0:T(8,128)(2,1)S(1)}, bf16[384,256]{1,0:T(8,128)(2,1)S(1)}) custom-call(bf16[64,4608]{1,0:T(8,128)(2,1)S(1)} %multiply_convert_fusion.x0, bf16[64,4608]{1,0:T(8,128)(2,1)S(1)} %collective-permute-done.8.x1, bf16[64,4608]{1,0:T(8,128)(2,1)S(1)} %collective-permute-done.x2, ...), custom_call_target="tpu_custom_call" | custom-call | tf_op jit(solution)/shard_map/project_near/pallas_call | solution.py:199
  69.2 11.6 %collective-permute-done.7.x0 = bf16[64,4608]{1,0:T(8,128)(2,1)S(1)} collective-permute-done((bf16[64,4608]{1,0:T(8,128)(2,1)S(1)}, bf16[64,4608]{1,0:T(8,128)(2,1)S(1)}, u32[]{:S(2)}, u32[]{:S(2)}) %collective-permute-start.7) | collective-permute-done | bytes 589856 | tf_op jit(solution)/shard_map/ppermute | solution.py:130
  80.9 3.3 %collective-permute-start.17 = (bf16[384,256]{1,0:T(8,128)(2,1)S(1)}, bf16[384,256]{1,0:T(8,128)(2,1)S(1)}, u32[]{:S(2)}, u32[]{:S(2)}) collective-permute-start(bf16[384,256]{1,0:T(8,128)(2,1)S(1)} %get-tuple-element.50.own_a), channel_id=1, source_target_pairs={{0,24},{8,32},{16,40},{24,48},{32,56},{40,64},{48,72},{56,80},{64,... | collective-permute-start | bytes 589832 | tf_op jit(solution)/shard_map/ppermute | solution.py:460
  84.1 3.2 %collective-permute-start.16 = (bf16[384,256]{1,0:T(8,128)(2,1)S(1)}, bf16[384,256]{1,0:T(8,128)(2,1)S(1)}, u32[]{:S(2)}, u32[]{:S(2)}) collective-permute-start(bf16[384,256]{1,0:T(8,128)(2,1)S(1)} %get-tuple-element.50.own_a), channel_id=1, source_target_pairs={{0,16},{8,24},{16,32},{24,40},{32,48},{40,56},{48,64},{56,72},{64,... | collective-permute-start | bytes 589832 | tf_op jit(solution)/shard_map/ppermute | solution.py:460
  87.3 2.0 %collective-permute-start.15 = (bf16[384,256]{1,0:T(8,128)(2,1)S(1)}, bf16[384,256]{1,0:T(8,128)(2,1)S(1)}, u32[]{:S(2)}, u32[]{:S(2)}) collective-permute-start(bf16[384,256]{1,0:T(8,128)(2,1)S(1)} %get-tuple-element.50.own_a), channel_id=1, source_target_pairs={{0,8},{8,16},{16,24},{24,32},{32,40},{40,48},{48,56},{56,64},{64,7... | collective-permute-start | bytes 589832 | tf_op jit(solution)/shard_map/ppermute | solution.py:460
  89.4 0.0 copy-start.8
  89.4 0.9 project_far.1
  90.3 6.2 %collective-permute-start.14 = (bf16[128,256]{1,0:T(8,128)(2,1)S(1)}, bf16[128,256]{1,0:T(8,128)(2,1)S(1)}, u32[]{:S(2)}, u32[]{:S(2)}) collective-permute-start(bf16[128,256]{1,0:T(8,128)(2,1)S(1)} %get-tuple-element.49.own_c), channel_id=1, source_target_pairs={{0,24},{8,32},{16,40},{24,48},{32,56},{40,64},{48,72},{56,80},{64,... | collective-permute-start | bytes 196616 | tf_op jit(solution)/shard_map/ppermute | solution.py:464
  96.5 2.5 %collective-permute-start.13 = (bf16[128,256]{1,0:T(8,128)(2,1)S(1)}, bf16[128,256]{1,0:T(8,128)(2,1)S(1)}, u32[]{:S(2)}, u32[]{:S(2)}) collective-permute-start(bf16[128,256]{1,0:T(8,128)(2,1)S(1)} %get-tuple-element.49.own_c), channel_id=1, source_target_pairs={{0,16},{8,24},{16,32},{24,40},{32,48},{40,56},{48,64},{56,72},{64,... | collective-permute-start | bytes 196616 | tf_op jit(solution)/shard_map/ppermute | solution.py:464
  99.0 2.2 %collective-permute-start.12 = (bf16[128,256]{1,0:T(8,128)(2,1)S(1)}, bf16[128,256]{1,0:T(8,128)(2,1)S(1)}, u32[]{:S(2)}, u32[]{:S(2)}) collective-permute-start(bf16[128,256]{1,0:T(8,128)(2,1)S(1)} %get-tuple-element.49.own_c), channel_id=1, source_target_pairs={{0,8},{8,16},{16,24},{24,32},{32,40},{40,48},{48,56},{56,64},{64,7... | collective-permute-start | bytes 196616 | tf_op jit(solution)/shard_map/ppermute | solution.py:464
  101.2 4.4 %attend.1 = (f32[1024,128]{1,0:T(8,128)S(1)}, f32[1024,128]{1,0:T(8,128)S(1)}) custom-call(s32[4,128]{1,0:T(4,128)S(1)} %copy-done.8, bf16[1024,128]{1,0:T(8,128)(2,1)S(1)} %get-tuple-element.48.q, bf16[384,256]{1,0:T(8,128)(2,1)S(1)} %get-tuple-element.50.own_a, bf16[128,256]{1,0:T(8,128)(2,1)S(1)} %get-tuple-element.49.own_c, ...), custom_call_target="tpu_custom_call" | custom-call | tf_op jit(solution)/shard_map/attend/pallas_call | solution.py:339
  105.7 1.6 collective-permute-done.12.w1
  107.2 1.4 attend_far.1
  108.7 0.1 collective-permute-start.18
  108.8 1.3 collective-permute-done.18.theirs
  110.1 3.0 %project_out.2 = (bf16[64,4608]{1,0:T(8,128)(2,1)S(1)}, bf16[64,4608]{1,0:T(8,128)(2,1)S(1)}) custom-call(bf16[256,256]{1,0:T(8,128)(2,1)S(1)} %get-tuple-element.54.ours, bf16[256,256]{1,0:T(8,128)(2,1)S(1)} %collective-permute-done.18.theirs, bf16[256,4608]{1,0:T(8,128)(2,1)} %w0.3, bf16[256,4608]{1,0:T(8,128)(2,1)} %collective-permute-done.6.w1), custom_call_target="tpu_custom_call" | custom-call | tf_op jit(solution)/shard_map/project_out/pallas_call | solution.py:392
  113.2 1.0 collective-permute-start.20
  114.1 3.0 %project_out.3 = (f32[64,4608]{1,0:T(8,128)S(1)}, f32[64,4608]{1,0:T(8,128)S(1)}) custom-call(bf16[256,256]{1,0:T(8,128)(2,1)S(1)} %get-tuple-element.54.ours, bf16[256,256]{1,0:T(8,128)(2,1)S(1)} %collective-permute-done.18.theirs, bf16[256,4608]{1,0:T(8,128)(2,1)} %w0.3, bf16[256,4608]{1,0:T(8,128)(2,1)} %collective-permute-done.6.w1), custom_call_target="tpu_custom_call" | custom-call | tf_op jit(solution)/shard_map/project_out/pallas_call | solution.py:392
  117.2 3.3 %collective-permute-start.19 = (bf16[64,4608]{1,0:T(8,128)(2,1)S(1)}, bf16[64,4608]{1,0:T(8,128)(2,1)S(1)}, u32[]{:S(2)}, u32[]{:S(2)}) collective-permute-start(bf16[64,4608]{1,0:T(8,128)(2,1)S(1)} %get-tuple-element.60), channel_id=1, source_target_pairs={{0,6},{1,3},{2,0},{3,5},{4,2},{5,7},{6,4},{7,1},{8,14},{9,11},{10,... | collective-permute-start | bytes 1769480 | tf_op jit(solution)/shard_map/ppermute | solution.py:130
  120.5 20.8 %collective-permute-done.20 = bf16[64,4608]{1,0:T(8,128)(2,1)S(1)} collective-permute-done((bf16[64,4608]{1,0:T(8,128)(2,1)S(1)}, bf16[64,4608]{1,0:T(8,128)(2,1)S(1)}, u32[]{:S(2)}, u32[]{:S(2)}) %collective-permute-start.20) | collective-permute-done | bytes 589856 | tf_op jit(solution)/shard_map/ppermute | solution.py:130
  141.3 0.1 add_convert_fusion.1
  141.4 1.8 %collective-permute-start.21 = (bf16[64,4608]{1,0:T(8,128)(2,1)S(1)}, bf16[64,4608]{1,0:T(8,128)(2,1)S(1)}, u32[]{:S(2)}, u32[]{:S(2)}) collective-permute-start(bf16[64,4608]{1,0:T(8,128)(2,1)S(1)} %add_convert_fusion.1), channel_id=1, source_target_pairs={{0,2},{1,7},{2,4},{3,1},{4,6},{5,3},{6,0},{7,5},{8,10},{9,15},{10,... | collective-permute-start | bytes 1769480 | tf_op jit(solution)/shard_map/ppermute | solution.py:130
  143.1 14.4 %collective-permute-done.21 = bf16[64,4608]{1,0:T(8,128)(2,1)S(1)} collective-permute-done((bf16[64,4608]{1,0:T(8,128)(2,1)S(1)}, bf16[64,4608]{1,0:T(8,128)(2,1)S(1)}, u32[]{:S(2)}, u32[]{:S(2)}) %collective-permute-start.21) | collective-permute-done | bytes 589856 | tf_op jit(solution)/shard_map/ppermute | solution.py:130
  157.6 0.3 multiply_reduce_fusion
  157.9 0.9 copy-done.12
  158.8 1.1 add_convert_fusion
  (49 shorter events, 0.2 us)
Async XLA Ops:
  0.0 1.1 copy-start
  1.5 9.7 %copy-start.15 = (pred[8]{0:T(512)(128)(4,1)S(1)}, pred[8]{0:T(512)(128)(4,1)}, u32[]{:S(2)}) copy-start(pred[8]{0:T(512)(128)(4,1)} %constant.45.clone.1) | copy-start | bytes 28
  2.6 18.0 %copy-start.9 = (s32[17]{0:T(128)S(1)}, s32[17]{0:T(128)}, u32[]{:S(2)}) copy-start(s32[17]{0:T(128)} %lengths.2) | copy-start | bytes 208
  2.6 18.0 %copy-start.10 = (f32[1,128]{1,0:T(1,128)S(1)}, f32[1,128]{1,0:T(1,128)}, u32[]{:S(2)}) copy-start(f32[1,128]{1,0:T(1,128)} %constant.47.clone.freq) | copy-start | bytes 1540
  2.6 21.4 %all-to-all-start = ((bf16[32,2,4736]{2,1,0:T(2,128)(2,1)}), bf16[32,2,4736]{2,1,0:T(2,128)(2,1)S(1)}, u32[]{:S(2)}, u32[]{:S(2)}) async-start(bf16[32,2,4736]{2,1,0:T(2,128)(2,1)} %reshape.41), calls=%async_computation | async-start | bytes 1212416 | tf_op jit(solution)/shard_map/all_to_all | solution.py:426
  11.3 19.8 %collective-permute-start.4 = (bf16[8,4736]{1,0:T(8,128)(2,1)S(1)}, bf16[8,4736]{1,0:T(8,128)(2,1)S(1)}, u32[]{:S(2)}, u32[]{:S(2)}) collective-permute-start(bf16[8,4736]{1,0:T(8,128)(2,1)S(1)} %fusion.3), channel_id=1, source_target_pairs={{0,4},{1,5},{2,6},{3,7},{4,0},{5,1},{6,2},{7,3},{8,12},{9,13},{10,... | collective-permute-start | bytes 227336 | tf_op jit(solution)/shard_map/ppermute | solution.py:130
  17.6 13.7 %collective-permute-start.3 = (bf16[8,4736]{1,0:T(8,128)(2,1)S(1)}, bf16[8,4736]{1,0:T(8,128)(2,1)S(1)}, u32[]{:S(2)}, u32[]{:S(2)}) collective-permute-start(bf16[8,4736]{1,0:T(8,128)(2,1)S(1)} %fusion.3), channel_id=1, source_target_pairs={{0,6},{1,3},{2,0},{3,5},{4,2},{5,7},{6,4},{7,1},{8,14},{9,11},{10,... | collective-permute-start | bytes 227336 | tf_op jit(solution)/shard_map/ppermute | solution.py:130
  18.2 13.1 %collective-permute-start.2 = (bf16[8,4736]{1,0:T(8,128)(2,1)S(1)}, bf16[8,4736]{1,0:T(8,128)(2,1)S(1)}, u32[]{:S(2)}, u32[]{:S(2)}) collective-permute-start(bf16[8,4736]{1,0:T(8,128)(2,1)S(1)} %fusion.3), channel_id=1, source_target_pairs={{0,2},{1,7},{2,4},{3,1},{4,6},{5,3},{6,0},{7,5},{8,10},{9,15},{10,... | collective-permute-start | bytes 227336 | tf_op jit(solution)/shard_map/ppermute | solution.py:130
  20.6 41.4 %collective-permute-start.6 = (bf16[256,4608]{1,0:T(8,128)(2,1)}, bf16[256,4608]{1,0:T(8,128)(2,1)}, u32[]{:S(2)}, u32[]{:S(2)}) collective-permute-start(bf16[256,4608]{1,0:T(8,128)(2,1)} %w0.3), channel_id=1, source_target_pairs={{0,1},{1,0},{2,3},{3,2},{4,5},{5,4},{6,7},{7,6},{8,9},{9,8},{10,11... | collective-permute-start | bytes 7077896 | tf_op jit(solution)/shard_map/ppermute | solution.py:130
  22.6 0.7 copy-start.6
  23.3 0.7 copy-start.7
  24.2 1.6 copy-start.13
  24.4 8.5 %copy-start.3 = (bf16[4608,128]{1,0:T(8,128)(2,1)S(1)}, bf16[4608,128]{1,0:T(8,128)(2,1)}, u32[]{:S(2)}) copy-start(bf16[4608,128]{1,0:T(8,128)(2,1)} %wv.5) | copy-start | bytes 3538948
  24.8 1.0 copy-start.11
  24.8 8.1 %copy-start.1 = (bf16[4608,128]{1,0:T(8,128)(2,1)S(1)}, bf16[4608,128]{1,0:T(8,128)(2,1)}, u32[]{:S(2)}) copy-start(bf16[4608,128]{1,0:T(8,128)(2,1)} %wk.5) | copy-start | bytes 3538948
  26.0 36.0 %collective-permute-start.1 = (bf16[64,4608]{1,0:T(8,128)(2,1)S(1)}, bf16[64,4608]{1,0:T(8,128)(2,1)S(1)}, u32[]{:S(2)}, u32[]{:S(2)}) collective-permute-start(bf16[64,4608]{1,0:T(8,128)(2,1)S(1)} %multiply_convert_fusion.x0), channel_id=1, source_target_pairs={{0,6},{1,3},{2,0},{3,5},{4,2},{5,7},{6,4},{7,1},{8,14},{9,11},{10,... | collective-permute-start | bytes 1769480 | tf_op jit(solution)/shard_map/ppermute | solution.py:130
  31.1 30.8 %collective-permute-start = (bf16[64,4608]{1,0:T(8,128)(2,1)S(1)}, bf16[64,4608]{1,0:T(8,128)(2,1)S(1)}, u32[]{:S(2)}, u32[]{:S(2)}) collective-permute-start(bf16[64,4608]{1,0:T(8,128)(2,1)S(1)} %multiply_convert_fusion.x0), channel_id=1, source_target_pairs={{0,2},{1,7},{2,4},{3,1},{4,6},{5,3},{6,0},{7,5},{8,10},{9,15},{10,... | collective-permute-start | bytes 1769480 | tf_op jit(solution)/shard_map/ppermute | solution.py:130
  31.5 1.4 collective-permute-start.5
  34.7 27.2 %all-to-all-start.1 = ((bf16[32,16,256]{2,1,0:T(8,128)(2,1)}), bf16[32,16,256]{2,1,0:T(8,128)(2,1)S(1)}, u32[]{:S(2)}, u32[]{:S(2)}) async-start(bf16[32,16,256]{2,1,0:T(8,128)(2,1)} %early.1), calls=%async_computation.1 | async-start | bytes 524288 | tf_op jit(solution)/shard_map/all_to_all | solution.py:450
  43.1 20.9 %collective-permute-start.8 = (bf16[64,4608]{1,0:T(8,128)(2,1)S(1)}, bf16[64,4608]{1,0:T(8,128)(2,1)S(1)}, u32[]{:S(2)}, u32[]{:S(2)}) collective-permute-start(bf16[64,4608]{1,0:T(8,128)(2,1)S(1)} %multiply_convert_fusion.x0), channel_id=1, source_target_pairs={{0,1},{1,0},{2,3},{3,2},{4,5},{5,4},{6,7},{7,6},{8,9},{9,8},{10,11... | collective-permute-start | bytes 1769480 | tf_op jit(solution)/shard_map/ppermute | solution.py:130
  61.9 2.1 %collective-permute-start.9 = (bf16[64,4608]{1,0:T(8,128)(2,1)S(1)}, bf16[64,4608]{1,0:T(8,128)(2,1)S(1)}, u32[]{:S(2)}, u32[]{:S(2)}) collective-permute-start(bf16[64,4608]{1,0:T(8,128)(2,1)S(1)} %collective-permute-done.1.x4), channel_id=1, source_target_pairs={{0,1},{1,0},{2,3},{3,2},{4,5},{5,4},{6,7},{7,6},{8,9},{9,8},{10,11... | collective-permute-start | bytes 1769480 | tf_op jit(solution)/shard_map/ppermute | solution.py:130
  62.0 2.8 %collective-permute-start.10 = (bf16[64,4608]{1,0:T(8,128)(2,1)S(1)}, bf16[64,4608]{1,0:T(8,128)(2,1)S(1)}, u32[]{:S(2)}, u32[]{:S(2)}) collective-permute-start(bf16[64,4608]{1,0:T(8,128)(2,1)S(1)} %collective-permute-done.x2), channel_id=1, source_target_pairs={{0,1},{1,0},{2,3},{3,2},{4,5},{5,4},{6,7},{7,6},{8,9},{9,8},{10,11... | collective-permute-start | bytes 1769480 | tf_op jit(solution)/shard_map/ppermute | solution.py:130
  62.5 18.3 %collective-permute-start.7 = (bf16[64,4608]{1,0:T(8,128)(2,1)S(1)}, bf16[64,4608]{1,0:T(8,128)(2,1)S(1)}, u32[]{:S(2)}, u32[]{:S(2)}) collective-permute-start(bf16[64,4608]{1,0:T(8,128)(2,1)S(1)} %collective-permute-done.x2), channel_id=1, source_target_pairs={{0,2},{1,7},{2,4},{3,1},{4,6},{5,3},{6,0},{7,5},{8,10},{9,15},{10,... | collective-permute-start | bytes 1769480 | tf_op jit(solution)/shard_map/ppermute | solution.py:130
  64.9 24.5 %copy-start.2 = (bf16[4608,128]{1,0:T(8,128)(2,1)S(1)}, bf16[4608,128]{1,0:T(8,128)(2,1)}, u32[]{:S(2)}) copy-start(bf16[4608,128]{1,0:T(8,128)(2,1)} %wk.5) | copy-start | bytes 3538948
  64.9 24.5 %copy-start.4 = (bf16[4608,128]{1,0:T(8,128)(2,1)S(1)}, bf16[4608,128]{1,0:T(8,128)(2,1)}, u32[]{:S(2)}) copy-start(bf16[4608,128]{1,0:T(8,128)(2,1)} %wv.5) | copy-start | bytes 3538948
  64.9 24.5 %copy-start.5 = (bf16[4608,256]{1,0:T(8,128)(2,1)S(1)}, bf16[4608,256]{1,0:T(8,128)(2,1)}, u32[]{:S(2)}) copy-start(bf16[4608,256]{1,0:T(8,128)(2,1)} %wq.3) | copy-start | bytes 7077892
  80.8 8.5 %collective-permute-start.11 = (bf16[64,4608]{1,0:T(8,128)(2,1)S(1)}, bf16[64,4608]{1,0:T(8,128)(2,1)S(1)}, u32[]{:S(2)}, u32[]{:S(2)}) collective-permute-start(bf16[64,4608]{1,0:T(8,128)(2,1)S(1)} %collective-permute-done.7.x0), channel_id=1, source_target_pairs={{0,1},{1,0},{2,3},{3,2},{4,5},{5,4},{6,7},{7,6},{8,9},{9,8},{10,11... | collective-permute-start | bytes 1769480 | tf_op jit(solution)/shard_map/ppermute | solution.py:130
  80.9 18.1 %collective-permute-start.17 = (bf16[384,256]{1,0:T(8,128)(2,1)S(1)}, bf16[384,256]{1,0:T(8,128)(2,1)S(1)}, u32[]{:S(2)}, u32[]{:S(2)}) collective-permute-start(bf16[384,256]{1,0:T(8,128)(2,1)S(1)} %get-tuple-element.50.own_a), channel_id=1, source_target_pairs={{0,24},{8,32},{16,40},{24,48},{32,56},{40,64},{48,72},{56,80},{64,... | collective-permute-start | bytes 589832 | tf_op jit(solution)/shard_map/ppermute | solution.py:460
  84.1 17.0 %collective-permute-start.16 = (bf16[384,256]{1,0:T(8,128)(2,1)S(1)}, bf16[384,256]{1,0:T(8,128)(2,1)S(1)}, u32[]{:S(2)}, u32[]{:S(2)}) collective-permute-start(bf16[384,256]{1,0:T(8,128)(2,1)S(1)} %get-tuple-element.50.own_a), channel_id=1, source_target_pairs={{0,16},{8,24},{16,32},{24,40},{32,48},{40,56},{48,64},{56,72},{64,... | collective-permute-start | bytes 589832 | tf_op jit(solution)/shard_map/ppermute | solution.py:460
  87.3 13.9 %collective-permute-start.15 = (bf16[384,256]{1,0:T(8,128)(2,1)S(1)}, bf16[384,256]{1,0:T(8,128)(2,1)S(1)}, u32[]{:S(2)}, u32[]{:S(2)}) collective-permute-start(bf16[384,256]{1,0:T(8,128)(2,1)S(1)} %get-tuple-element.50.own_a), channel_id=1, source_target_pairs={{0,8},{8,16},{16,24},{24,32},{32,40},{40,48},{48,56},{56,64},{64,7... | collective-permute-start | bytes 589832 | tf_op jit(solution)/shard_map/ppermute | solution.py:460
  89.4 11.9 %copy-start.8 = (s32[4,128]{1,0:T(4,128)S(1)}, s32[4,128]{1,0:T(4,128)}, u32[]{:S(2)}) copy-start(s32[4,128]{1,0:T(4,128)} %pattern.3) | copy-start | bytes 6148
  90.3 15.4 %collective-permute-start.14 = (bf16[128,256]{1,0:T(8,128)(2,1)S(1)}, bf16[128,256]{1,0:T(8,128)(2,1)S(1)}, u32[]{:S(2)}, u32[]{:S(2)}) collective-permute-start(bf16[128,256]{1,0:T(8,128)(2,1)S(1)} %get-tuple-element.49.own_c), channel_id=1, source_target_pairs={{0,24},{8,32},{16,40},{24,48},{32,56},{40,64},{48,72},{56,80},{64,... | collective-permute-start | bytes 196616 | tf_op jit(solution)/shard_map/ppermute | solution.py:464
  96.5 9.2 %collective-permute-start.13 = (bf16[128,256]{1,0:T(8,128)(2,1)S(1)}, bf16[128,256]{1,0:T(8,128)(2,1)S(1)}, u32[]{:S(2)}, u32[]{:S(2)}) collective-permute-start(bf16[128,256]{1,0:T(8,128)(2,1)S(1)} %get-tuple-element.49.own_c), channel_id=1, source_target_pairs={{0,16},{8,24},{16,32},{24,40},{32,48},{40,56},{48,64},{56,72},{64,... | collective-permute-start | bytes 196616 | tf_op jit(solution)/shard_map/ppermute | solution.py:464
  99.0 8.3 %collective-permute-start.12 = (bf16[128,256]{1,0:T(8,128)(2,1)S(1)}, bf16[128,256]{1,0:T(8,128)(2,1)S(1)}, u32[]{:S(2)}, u32[]{:S(2)}) collective-permute-start(bf16[128,256]{1,0:T(8,128)(2,1)S(1)} %get-tuple-element.49.own_c), channel_id=1, source_target_pairs={{0,8},{8,16},{16,24},{24,32},{32,40},{40,48},{48,56},{56,64},{64,7... | collective-permute-start | bytes 196616 | tf_op jit(solution)/shard_map/ppermute | solution.py:464
  108.7 1.4 collective-permute-start.18
  113.2 28.1 %collective-permute-start.20 = (bf16[64,4608]{1,0:T(8,128)(2,1)S(1)}, bf16[64,4608]{1,0:T(8,128)(2,1)S(1)}, u32[]{:S(2)}, u32[]{:S(2)}) collective-permute-start(bf16[64,4608]{1,0:T(8,128)(2,1)S(1)} %get-tuple-element.62), channel_id=1, source_target_pairs={{0,2},{1,7},{2,4},{3,1},{4,6},{5,3},{6,0},{7,5},{8,10},{9,15},{10,... | collective-permute-start | bytes 1769480 | tf_op jit(solution)/shard_map/ppermute | solution.py:130
  117.2 26.0 %collective-permute-start.19 = (bf16[64,4608]{1,0:T(8,128)(2,1)S(1)}, bf16[64,4608]{1,0:T(8,128)(2,1)S(1)}, u32[]{:S(2)}, u32[]{:S(2)}) collective-permute-start(bf16[64,4608]{1,0:T(8,128)(2,1)S(1)} %get-tuple-element.60), channel_id=1, source_target_pairs={{0,6},{1,3},{2,0},{3,5},{4,2},{5,7},{6,4},{7,1},{8,14},{9,11},{10,... | collective-permute-start | bytes 1769480 | tf_op jit(solution)/shard_map/ppermute | solution.py:130
  141.4 16.2 %collective-permute-start.21 = (bf16[64,4608]{1,0:T(8,128)(2,1)S(1)}, bf16[64,4608]{1,0:T(8,128)(2,1)S(1)}, u32[]{:S(2)}, u32[]{:S(2)}) collective-permute-start(bf16[64,4608]{1,0:T(8,128)(2,1)S(1)} %add_convert_fusion.1), channel_id=1, source_target_pairs={{0,2},{1,7},{2,4},{3,1},{4,6},{5,3},{6,0},{7,5},{8,10},{9,15},{10,... | collective-permute-start | bytes 1769480 | tf_op jit(solution)/shard_map/ppermute | solution.py:130
  157.5 1.3 copy-start.12
  157.5 1.3 copy-start.14

commit v3 on v2

--- a/solution.py
+++ b/solution.py
@@ -426,30 +426,30 @@
     got = lax.all_to_all(send.reshape(n_dp, per_peer, width), "dp", 0, 0, tiled=True)
 
     core, order = plane_order()
-    later, _ = lax.optimization_barrier((lengths, send))
-    cos_a, sin_a, cos_c, sin_c = tables(later)
-
     first = send[:per_peer]
     piece = jnp.pad(first, ((0, 8 - per_peer), (0, 0)))
     column = [to(piece, OUT), to(piece, BACK), to(piece, FAR)]
-    w_sib = to(w_out, SIB)
-
-    got, _ = lax.optimization_barrier((got, cos_a))
+
     got = got.reshape(SLOTS, width)
     arrange = order_ids[:, None] == got[:, D].astype(jnp.int32)[None, :]
     packed = jnp.dot(arrange.astype(bf16), got[:, :D], preferred_element_type=jnp.float32).astype(bf16)
+    packed = lax.optimization_barrier(packed)
     normed = rms_scale(packed.astype(jnp.float32), norm_gain).astype(bf16)
 
     near_o = to(normed, OUT)
     near_b = to(normed, BACK)
     own_s = to(normed, SIB)
 
-    column, _ = lax.optimization_barrier((column, normed))
+    column, later, _ = lax.optimization_barrier((column, lengths, normed))
+    cos_a, sin_a, cos_c, sin_c = tables(later)
+    w_sib = to(w_out, SIB)
     early = jnp.concatenate([first] + [c[:per_peer] for c in column], axis=0)
     early_kv = early_keys(lengths, early, to(early, SIB), norm_gain, w_key, w_value, n_dp)
     prompt = lax.all_to_all(early_kv, "dp", 0, 0, tiled=True)
     prompt = prompt.reshape(SHARD, 2 * HD)
-    near_o, near_b, prompt, w_sib = lax.optimization_barrier((near_o, near_b, prompt, w_sib))
+    near_o, near_b, prompt, w_sib, cos_a = lax.optimization_barrier(
+        (near_o, near_b, prompt, w_sib, cos_a)
+    )
     far_own = to(near_o, OUT)
     near_os = to(near_b, SIB)
     near_bs = to(near_o, SIB)

time: 163 us -> 158 us (0.969)
  the two profiles are of different devices: /device:TPU:40 before, /device:TPU:8 now
where the time goes in v3:
time: 158 us; the launch traced here: 157 us
  waiting for transfers between devices  67.4 us (43%)
  starting transfers between devices  61.4 us (39%)
  Pallas kernels  19.9 us (13%)
  local copies, waits for them, and re-layouts  4.13 us (3%)
  other arithmetic  3.43 us (2%)
    ppermute x16, waiting for transfers between devices, to(): return lax.ppermute(values, 'tensor', pairs)  49.6 us
    ppermute x16, starting transfers between devices, to(): return lax.ppermute(values, 'tensor', pairs)  25.8 us
    all_to_all x1, waiting for transfers between devices, body(): prompt = lax.all_to_all(early_kv, 'dp', 0, 0, tiled=True)  13 us
    ppermute x3, starting transfers between devices, body(): kvs_c = [lax.ppermute(kv_c, 'dp', shift) for shift in shifts]  10.9 us
    all_to_all x1, starting transfers between devices, body(): lax.all_to_all(send.reshape(n_dp, per_peer, width), 'dp', 0, 0, tiled=True)  8.88 us
    ppermute x3, starting transfers between devices, body(): kvs_a = [kv_a] + [lax.ppermute(kv_a, 'dp', shift) for shift in shifts]  8.49 us
    all_to_all x1, starting transfers between devices, body(): prompt = lax.all_to_all(early_kv, 'dp', 0, 0, tiled=True)  7.36 us
    pallas_call x2, Pallas kernels, project_out(): pl.pallas_call(functools.partial(out_kernel, chunks), in_specs=[VMEM] * 2...  6.09 us
  transfers between devices with their start and end apart: 24, of which 11 were waited for; matrix products, arithmetic and copies ran while one was open for 1% of the time, Pallas kernels for 10%

profile of v3, /device:TPU:8, one launch (start us, length us, event | category | flops | bytes accessed | tf_op | source)
XLA Modules:
  0.0 157.4 jit_solution(7349478216610850252)
XLA Ops:
  0.0 0.7 and_select_fusion.1
  0.7 0.2 convert_reduce_fusion.1
  0.9 0.1 select_reduce_fusion
  1.0 0.0 copy-done
  1.1 0.3 convolution_convert_fusion.1
  1.4 0.1 broadcast_in_dim.18
  1.5 0.0 copy-start.15
  1.5 1.1 reshape.41
  2.6 8.9 %all-to-all-start = ((bf16[32,2,4736]{2,1,0:T(2,128)(2,1)}), bf16[32,2,4736]{2,1,0:T(2,128)(2,1)S(1)}, u32[]{:S(2)}, u32[]{:S(2)}) async-start(bf16[32,2,4736]{2,1,0:T(2,128)(2,1)} %reshape.41), calls=%async_computation | async-start | bytes 1212416 | tf_op jit(solution)/shard_map/all_to_all | solution.py:426
  11.5 0.1 fusion.6
  11.6 6.4 %collective-permute-start.4 = (bf16[8,4736]{1,0:T(8,128)(2,1)S(1)}, bf16[8,4736]{1,0:T(8,128)(2,1)S(1)}, u32[]{:S(2)}, u32[]{:S(2)}) collective-permute-start(bf16[8,4736]{1,0:T(8,128)(2,1)S(1)} %fusion.6), channel_id=1, source_target_pairs={{0,4},{1,5},{2,6},{3,7},{4,0},{5,1},{6,2},{7,3},{8,12},{9,13},{10,... | collective-permute-start | bytes 227336 | tf_op jit(solution)/shard_map/ppermute | solution.py:130
  17.9 0.6 collective-permute-start.3
  18.5 2.4 %collective-permute-start.2 = (bf16[8,4736]{1,0:T(8,128)(2,1)S(1)}, bf16[8,4736]{1,0:T(8,128)(2,1)S(1)}, u32[]{:S(2)}, u32[]{:S(2)}) collective-permute-start(bf16[8,4736]{1,0:T(8,128)(2,1)S(1)} %fusion.6), channel_id=1, source_target_pairs={{0,2},{1,7},{2,4},{3,1},{4,6},{5,3},{6,0},{7,5},{8,10},{9,15},{10,... | collective-permute-start | bytes 227336 | tf_op jit(solution)/shard_map/ppermute | solution.py:130
  20.9 1.8 %all-to-all-done = bf16[32,2,4736]{2,1,0:T(2,128)(2,1)S(1)} async-done(((bf16[32,2,4736]{2,1,0:T(2,128)(2,1)}), bf16[32,2,4736]{2,1,0:T(2,128)(2,1)S(1)}, u32[]{:S(2)}, u32[]{:S(2)}) %all-to-all-start) | async-done | bytes 606240 | tf_op jit(solution)/shard_map/all_to_all | solution.py:426
  22.6 0.2 reshape.42
  22.9 0.0 copy-start.13
  22.9 0.1 convert_reduce_fusion
  23.0 0.3 convolution_convert_fusion
  23.4 0.0 copy-start.10
  23.4 0.2 fusion
  23.6 0.5 copy-done.11
  24.1 0.2 fusion.2.x0
  24.3 9.3 %collective-permute-start.1 = (bf16[64,4608]{1,0:T(8,128)(2,1)S(1)}, bf16[64,4608]{1,0:T(8,128)(2,1)S(1)}, u32[]{:S(2)}, u32[]{:S(2)}) collective-permute-start(bf16[64,4608]{1,0:T(8,128)(2,1)S(1)} %fusion.2.x0), channel_id=1, source_target_pairs={{0,6},{1,3},{2,0},{3,5},{4,2},{5,7},{6,4},{7,1},{8,14},{9,11},{10,... | collective-permute-start | bytes 1769480 | tf_op jit(solution)/shard_map/ppermute | solution.py:130
  33.7 0.1 pad_maximum_fusion.1.own
  33.8 0.1 collective-permute-start.5
  33.9 1.2 collective-permute-done.5.sib
  35.2 1.9 %early.1 = bf16[32,16,256]{2,1,0:T(8,128)(2,1)} custom-call(s32[17]{0:T(128)S(1)} %copy-done.9, f32[1,128]{1,0:T(1,128)S(1)} %copy-done.10, bf16[8,4736]{1,0:T(8,128)(2,1)S(1)} %pad_maximum_fusion.1.own, bf16[8,4736]{1,0:T(8,128)(2,1)S(1)} %collective-permute-done.5.sib, f32[1,4608]{1,0:T(1,128)S(1)} %broadcast_in_dim.19.gain, ...), custom_call_target="tpu_custom_call" | custom-call | tf_op jit(solution)/shard_map/early/pallas_call | solution.py:115
  37.0 7.4 %all-to-all-start.1 = ((bf16[32,16,256]{2,1,0:T(8,128)(2,1)}), bf16[32,16,256]{2,1,0:T(8,128)(2,1)S(1)}, u32[]{:S(2)}, u32[]{:S(2)}) async-start(bf16[32,16,256]{2,1,0:T(8,128)(2,1)} %early.1), calls=%async_computation.1 | async-start | bytes 524288 | tf_op jit(solution)/shard_map/all_to_all | solution.py:448
  44.4 0.1 collective-permute-start.8
  44.5 2.0 %tables.1 = (f32[384,128]{1,0:T(8,128)S(1)}, f32[384,128]{1,0:T(8,128)S(1)}, f32[128,128]{1,0:T(8,128)S(1)}, f32[128,128]{1,0:T(8,128)S(1)}) custom-call(s32[17]{0:T(128)S(1)} %copy-done.9, f32[1,128]{1,0:T(1,128)S(1)} %copy-done.10), custom_call_target="tpu_custom_call" | custom-call | tf_op jit(solution)/shard_map/tables/pallas_call | solution.py:81
  46.6 0.7 copy-done.6
  47.2 0.7 copy-done.7
  47.9 13.0 %all-to-all-done.1 = bf16[32,16,256]{2,1,0:T(8,128)(2,1)S(1)} async-done(((bf16[32,16,256]{2,1,0:T(8,128)(2,1)}), bf16[32,16,256]{2,1,0:T(8,128)(2,1)S(1)}, u32[]{:S(2)}, u32[]{:S(2)}) %all-to-all-start.1) | async-done | bytes 262176 | tf_op jit(solution)/shard_map/all_to_all | solution.py:448
  61.0 0.1 collective-permute-start.9
  61.1 0.5 collective-permute-start.10
  61.6 2.0 %collective-permute-start.7 = (bf16[64,4608]{1,0:T(8,128)(2,1)S(1)}, bf16[64,4608]{1,0:T(8,128)(2,1)S(1)}, u32[]{:S(2)}, u32[]{:S(2)}) collective-permute-start(bf16[64,4608]{1,0:T(8,128)(2,1)S(1)} %collective-permute-done.x2), channel_id=1, source_target_pairs={{0,2},{1,7},{2,4},{3,1},{4,6},{5,3},{6,0},{7,5},{8,10},{9,15},{10,... | collective-permute-start | bytes 1769480 | tf_op jit(solution)/shard_map/ppermute | solution.py:130
  63.6 0.3 collective-permute-done.10.x5
  63.9 4.3 %project_near.1 = (bf16[2,384,128]{2,1,0:T(8,128)(2,1)S(1)}, bf16[384,256]{1,0:T(8,128)(2,1)S(1)}) custom-call(bf16[64,4608]{1,0:T(8,128)(2,1)S(1)} %fusion.2.x0, bf16[64,4608]{1,0:T(8,128)(2,1)S(1)} %collective-permute-done.8.x1, bf16[64,4608]{1,0:T(8,128)(2,1)S(1)} %collective-permute-done.x2, bf16[64,4608]{1,0:T(8,128)(2,1)S(1)} %collective-permute-done.9.x3, ...), custom_call_target="tpu_custom_call" | custom-call | tf_op jit(solution)/shard_map/project_near/pallas_call | solution.py:199
  68.3 11.1 %collective-permute-done.7.x0 = bf16[64,4608]{1,0:T(8,128)(2,1)S(1)} collective-permute-done((bf16[64,4608]{1,0:T(8,128)(2,1)S(1)}, bf16[64,4608]{1,0:T(8,128)(2,1)S(1)}, u32[]{:S(2)}, u32[]{:S(2)}) %collective-permute-start.7) | collective-permute-done | bytes 589856 | tf_op jit(solution)/shard_map/ppermute | solution.py:130
  79.4 3.2 %collective-permute-start.17 = (bf16[384,256]{1,0:T(8,128)(2,1)S(1)}, bf16[384,256]{1,0:T(8,128)(2,1)S(1)}, u32[]{:S(2)}, u32[]{:S(2)}) collective-permute-start(bf16[384,256]{1,0:T(8,128)(2,1)S(1)} %get-tuple-element.50.own_a), channel_id=1, source_target_pairs={{0,24},{8,32},{16,40},{24,48},{32,56},{40,64},{48,72},{56,80},{64,... | collective-permute-start | bytes 589832 | tf_op jit(solution)/shard_map/ppermute | solution.py:460
  82.6 3.4 %collective-permute-start.16 = (bf16[384,256]{1,0:T(8,128)(2,1)S(1)}, bf16[384,256]{1,0:T(8,128)(2,1)S(1)}, u32[]{:S(2)}, u32[]{:S(2)}) collective-permute-start(bf16[384,256]{1,0:T(8,128)(2,1)S(1)} %get-tuple-element.50.own_a), channel_id=1, source_target_pairs={{0,16},{8,24},{16,32},{24,40},{32,48},{40,56},{48,64},{56,72},{64,... | collective-permute-start | bytes 589832 | tf_op jit(solution)/shard_map/ppermute | solution.py:460
  86.0 1.9 %collective-permute-start.15 = (bf16[384,256]{1,0:T(8,128)(2,1)S(1)}, bf16[384,256]{1,0:T(8,128)(2,1)S(1)}, u32[]{:S(2)}, u32[]{:S(2)}) collective-permute-start(bf16[384,256]{1,0:T(8,128)(2,1)S(1)} %get-tuple-element.50.own_a), channel_id=1, source_target_pairs={{0,8},{8,16},{16,24},{24,32},{32,40},{40,48},{48,56},{56,64},{64,7... | collective-permute-start | bytes 589832 | tf_op jit(solution)/shard_map/ppermute | solution.py:460
  88.0 0.9 project_far.1
  88.8 5.5 %collective-permute-start.14 = (bf16[128,256]{1,0:T(8,128)(2,1)S(1)}, bf16[128,256]{1,0:T(8,128)(2,1)S(1)}, u32[]{:S(2)}, u32[]{:S(2)}) collective-permute-start(bf16[128,256]{1,0:T(8,128)(2,1)S(1)} %get-tuple-element.49.own_c), channel_id=1, source_target_pairs={{0,24},{8,32},{16,40},{24,48},{32,56},{40,64},{48,72},{56,80},{64,... | collective-permute-start | bytes 196616 | tf_op jit(solution)/shard_map/ppermute | solution.py:464
  94.4 3.4 %collective-permute-start.13 = (bf16[128,256]{1,0:T(8,128)(2,1)S(1)}, bf16[128,256]{1,0:T(8,128)(2,1)S(1)}, u32[]{:S(2)}, u32[]{:S(2)}) collective-permute-start(bf16[128,256]{1,0:T(8,128)(2,1)S(1)} %get-tuple-element.49.own_c), channel_id=1, source_target_pairs={{0,16},{8,24},{16,32},{24,40},{32,48},{40,56},{48,64},{56,72},{64,... | collective-permute-start | bytes 196616 | tf_op jit(solution)/shard_map/ppermute | solution.py:464
  97.8 1.9 %collective-permute-start.12 = (bf16[128,256]{1,0:T(8,128)(2,1)S(1)}, bf16[128,256]{1,0:T(8,128)(2,1)S(1)}, u32[]{:S(2)}, u32[]{:S(2)}) collective-permute-start(bf16[128,256]{1,0:T(8,128)(2,1)S(1)} %get-tuple-element.49.own_c), channel_id=1, source_target_pairs={{0,8},{8,16},{16,24},{24,32},{32,40},{40,48},{48,56},{56,64},{64,7... | collective-permute-start | bytes 196616 | tf_op jit(solution)/shard_map/ppermute | solution.py:464
  99.8 3.3 %attend.1 = (f32[1024,128]{1,0:T(8,128)S(1)}, f32[1024,128]{1,0:T(8,128)S(1)}) custom-call(s32[4,128]{1,0:T(4,128)S(1)} %copy-done.8, bf16[1024,128]{1,0:T(8,128)(2,1)S(1)} %get-tuple-element.48.q, bf16[384,256]{1,0:T(8,128)(2,1)S(1)} %get-tuple-element.50.own_a, bf16[128,256]{1,0:T(8,128)(2,1)S(1)} %get-tuple-element.49.own_c, ...), custom_call_target="tpu_custom_call" | custom-call | tf_op jit(solution)/shard_map/attend/pallas_call | solution.py:339
  103.1 0.2 collective-permute-done.13.w2
  103.4 2.7 %collective-permute-done.12.w1 = bf16[128,256]{1,0:T(8,128)(2,1)S(1)} collective-permute-done((bf16[128,256]{1,0:T(8,128)(2,1)S(1)}, bf16[128,256]{1,0:T(8,128)(2,1)S(1)}, u32[]{:S(2)}, u32[]{:S(2)}) %collective-permute-start.12) | collective-permute-done | bytes 65568 | tf_op jit(solution)/shard_map/ppermute | solution.py:464
  106.1 1.4 attend_far.1
  107.5 0.1 collective-permute-start.18
  107.6 1.3 collective-permute-done.18.theirs
  109.0 3.0 %project_out.2 = (bf16[64,4608]{1,0:T(8,128)(2,1)S(1)}, bf16[64,4608]{1,0:T(8,128)(2,1)S(1)}) custom-call(bf16[256,256]{1,0:T(8,128)(2,1)S(1)} %get-tuple-element.54.ours, bf16[256,256]{1,0:T(8,128)(2,1)S(1)} %collective-permute-done.18.theirs, bf16[256,4608]{1,0:T(8,128)(2,1)} %w0.3, bf16[256,4608]{1,0:T(8,128)(2,1)} %collective-permute-done.6.w1), custom_call_target="tpu_custom_call" | custom-call | tf_op jit(solution)/shard_map/project_out/pallas_call | solution.py:392
  112.0 1.2 collective-permute-start.20
  113.2 3.0 %project_out.3 = (f32[64,4608]{1,0:T(8,128)S(1)}, f32[64,4608]{1,0:T(8,128)S(1)}) custom-call(bf16[256,256]{1,0:T(8,128)(2,1)S(1)} %get-tuple-element.54.ours, bf16[256,256]{1,0:T(8,128)(2,1)S(1)} %collective-permute-done.18.theirs, bf16[256,4608]{1,0:T(8,128)(2,1)} %w0.3, bf16[256,4608]{1,0:T(8,128)(2,1)} %collective-permute-done.6.w1), custom_call_target="tpu_custom_call" | custom-call | tf_op jit(solution)/shard_map/project_out/pallas_call | solution.py:392
  116.3 3.1 %collective-permute-start.19 = (bf16[64,4608]{1,0:T(8,128)(2,1)S(1)}, bf16[64,4608]{1,0:T(8,128)(2,1)S(1)}, u32[]{:S(2)}, u32[]{:S(2)}) collective-permute-start(bf16[64,4608]{1,0:T(8,128)(2,1)S(1)} %get-tuple-element.60), channel_id=1, source_target_pairs={{0,6},{1,3},{2,0},{3,5},{4,2},{5,7},{6,4},{7,1},{8,14},{9,11},{10,... | collective-permute-start | bytes 1769480 | tf_op jit(solution)/shard_map/ppermute | solution.py:130
  119.4 23.0 %collective-permute-done.20 = bf16[64,4608]{1,0:T(8,128)(2,1)S(1)} collective-permute-done((bf16[64,4608]{1,0:T(8,128)(2,1)S(1)}, bf16[64,4608]{1,0:T(8,128)(2,1)S(1)}, u32[]{:S(2)}, u32[]{:S(2)}) %collective-permute-start.20) | collective-permute-done | bytes 589856 | tf_op jit(solution)/shard_map/ppermute | solution.py:130
  142.4 0.1 add_convert_fusion
  142.5 0.1 collective-permute-start.21
  142.6 3.3 %collective-permute-done.19 = bf16[64,4608]{1,0:T(8,128)(2,1)S(1)} collective-permute-done((bf16[64,4608]{1,0:T(8,128)(2,1)S(1)}, bf16[64,4608]{1,0:T(8,128)(2,1)S(1)}, u32[]{:S(2)}, u32[]{:S(2)}) %collective-permute-start.19) | collective-permute-done | bytes 589856 | tf_op jit(solution)/shard_map/ppermute | solution.py:130
  145.9 9.2 %collective-permute-done.21 = bf16[64,4608]{1,0:T(8,128)(2,1)S(1)} collective-permute-done((bf16[64,4608]{1,0:T(8,128)(2,1)S(1)}, bf16[64,4608]{1,0:T(8,128)(2,1)S(1)}, u32[]{:S(2)}, u32[]{:S(2)}) %collective-permute-start.21) | collective-permute-done | bytes 589856 | tf_op jit(solution)/shard_map/ppermute | solution.py:130
  155.2 0.3 multiply_reduce_fusion
  155.5 0.7 copy-done.12
  156.2 1.2 fusion.3
  (50 shorter events, 0.2 us)
Async XLA Ops:
  0.0 1.1 copy-start
  1.5 10.0 %copy-start.15 = (pred[8]{0:T(512)(128)(4,1)S(1)}, pred[8]{0:T(512)(128)(4,1)}, u32[]{:S(2)}) copy-start(pred[8]{0:T(512)(128)(4,1)} %constant.45.clone.1) | copy-start | bytes 28
  2.6 20.1 %all-to-all-start = ((bf16[32,2,4736]{2,1,0:T(2,128)(2,1)}), bf16[32,2,4736]{2,1,0:T(2,128)(2,1)S(1)}, u32[]{:S(2)}, u32[]{:S(2)}) async-start(bf16[32,2,4736]{2,1,0:T(2,128)(2,1)} %reshape.41), calls=%async_computation | async-start | bytes 1212416 | tf_op jit(solution)/shard_map/all_to_all | solution.py:426
  11.6 22.1 %collective-permute-start.4 = (bf16[8,4736]{1,0:T(8,128)(2,1)S(1)}, bf16[8,4736]{1,0:T(8,128)(2,1)S(1)}, u32[]{:S(2)}, u32[]{:S(2)}) collective-permute-start(bf16[8,4736]{1,0:T(8,128)(2,1)S(1)} %fusion.6), channel_id=1, source_target_pairs={{0,4},{1,5},{2,6},{3,7},{4,0},{5,1},{6,2},{7,3},{8,12},{9,13},{10,... | collective-permute-start | bytes 227336 | tf_op jit(solution)/shard_map/ppermute | solution.py:130
  17.9 15.7 %collective-permute-start.3 = (bf16[8,4736]{1,0:T(8,128)(2,1)S(1)}, bf16[8,4736]{1,0:T(8,128)(2,1)S(1)}, u32[]{:S(2)}, u32[]{:S(2)}) collective-permute-start(bf16[8,4736]{1,0:T(8,128)(2,1)S(1)} %fusion.6), channel_id=1, source_target_pairs={{0,6},{1,3},{2,0},{3,5},{4,2},{5,7},{6,4},{7,1},{8,14},{9,11},{10,... | collective-permute-start | bytes 227336 | tf_op jit(solution)/shard_map/ppermute | solution.py:130
  18.5 15.1 %collective-permute-start.2 = (bf16[8,4736]{1,0:T(8,128)(2,1)S(1)}, bf16[8,4736]{1,0:T(8,128)(2,1)S(1)}, u32[]{:S(2)}, u32[]{:S(2)}) collective-permute-start(bf16[8,4736]{1,0:T(8,128)(2,1)S(1)} %fusion.6), channel_id=1, source_target_pairs={{0,2},{1,7},{2,4},{3,1},{4,6},{5,3},{6,0},{7,5},{8,10},{9,15},{10,... | collective-permute-start | bytes 227336 | tf_op jit(solution)/shard_map/ppermute | solution.py:130
  20.9 40.1 %collective-permute-start.6 = (bf16[256,4608]{1,0:T(8,128)(2,1)}, bf16[256,4608]{1,0:T(8,128)(2,1)}, u32[]{:S(2)}, u32[]{:S(2)}) collective-permute-start(bf16[256,4608]{1,0:T(8,128)(2,1)} %w0.3), channel_id=1, source_target_pairs={{0,1},{1,0},{2,3},{3,2},{4,5},{5,4},{6,7},{7,6},{8,9},{9,8},{10,11... | collective-permute-start | bytes 7077896 | tf_op jit(solution)/shard_map/ppermute | solution.py:130
  22.9 1.3 copy-start.13
  23.0 12.2 %copy-start.3 = (bf16[4608,128]{1,0:T(8,128)(2,1)S(1)}, bf16[4608,128]{1,0:T(8,128)(2,1)}, u32[]{:S(2)}) copy-start(bf16[4608,128]{1,0:T(8,128)(2,1)} %wv.5) | copy-start | bytes 3538948
  23.3 0.8 copy-start.11
  23.3 11.8 %copy-start.1 = (bf16[4608,128]{1,0:T(8,128)(2,1)S(1)}, bf16[4608,128]{1,0:T(8,128)(2,1)}, u32[]{:S(2)}) copy-start(bf16[4608,128]{1,0:T(8,128)(2,1)} %wk.5) | copy-start | bytes 3538948
  23.3 11.8 %copy-start.9 = (s32[17]{0:T(128)S(1)}, s32[17]{0:T(128)}, u32[]{:S(2)}) copy-start(s32[17]{0:T(128)} %lengths.2) | copy-start | bytes 208
  23.4 11.8 %copy-start.10 = (f32[1,128]{1,0:T(1,128)S(1)}, f32[1,128]{1,0:T(1,128)}, u32[]{:S(2)}) copy-start(f32[1,128]{1,0:T(1,128)} %constant.47.clone.freq) | copy-start | bytes 1540
  24.3 36.6 %collective-permute-start.1 = (bf16[64,4608]{1,0:T(8,128)(2,1)S(1)}, bf16[64,4608]{1,0:T(8,128)(2,1)S(1)}, u32[]{:S(2)}, u32[]{:S(2)}) collective-permute-start(bf16[64,4608]{1,0:T(8,128)(2,1)S(1)} %fusion.2.x0), channel_id=1, source_target_pairs={{0,6},{1,3},{2,0},{3,5},{4,2},{5,7},{6,4},{7,1},{8,14},{9,11},{10,... | collective-permute-start | bytes 1769480 | tf_op jit(solution)/shard_map/ppermute | solution.py:130
  33.6 27.4 %collective-permute-start = (bf16[64,4608]{1,0:T(8,128)(2,1)S(1)}, bf16[64,4608]{1,0:T(8,128)(2,1)S(1)}, u32[]{:S(2)}, u32[]{:S(2)}) collective-permute-start(bf16[64,4608]{1,0:T(8,128)(2,1)S(1)} %fusion.2.x0), channel_id=1, source_target_pairs={{0,2},{1,7},{2,4},{3,1},{4,6},{5,3},{6,0},{7,5},{8,10},{9,15},{10,... | collective-permute-start | bytes 1769480 | tf_op jit(solution)/shard_map/ppermute | solution.py:130
  33.8 1.4 collective-permute-start.5
  37.0 23.9 %all-to-all-start.1 = ((bf16[32,16,256]{2,1,0:T(8,128)(2,1)}), bf16[32,16,256]{2,1,0:T(8,128)(2,1)S(1)}, u32[]{:S(2)}, u32[]{:S(2)}) async-start(bf16[32,16,256]{2,1,0:T(8,128)(2,1)} %early.1), calls=%async_computation.1 | async-start | bytes 524288 | tf_op jit(solution)/shard_map/all_to_all | solution.py:448
  44.4 19.2 %collective-permute-start.8 = (bf16[64,4608]{1,0:T(8,128)(2,1)S(1)}, bf16[64,4608]{1,0:T(8,128)(2,1)S(1)}, u32[]{:S(2)}, u32[]{:S(2)}) collective-permute-start(bf16[64,4608]{1,0:T(8,128)(2,1)S(1)} %fusion.2.x0), channel_id=1, source_target_pairs={{0,1},{1,0},{2,3},{3,2},{4,5},{5,4},{6,7},{7,6},{8,9},{9,8},{10,11... | collective-permute-start | bytes 1769480 | tf_op jit(solution)/shard_map/ppermute | solution.py:130
  46.5 0.7 copy-start.6
  47.2 0.7 copy-start.7
  61.0 2.6 %collective-permute-start.9 = (bf16[64,4608]{1,0:T(8,128)(2,1)S(1)}, bf16[64,4608]{1,0:T(8,128)(2,1)S(1)}, u32[]{:S(2)}, u32[]{:S(2)}) collective-permute-start(bf16[64,4608]{1,0:T(8,128)(2,1)S(1)} %collective-permute-done.1.x4), channel_id=1, source_target_pairs={{0,1},{1,0},{2,3},{3,2},{4,5},{5,4},{6,7},{7,6},{8,9},{9,8},{10,11... | collective-permute-start | bytes 1769480 | tf_op jit(solution)/shard_map/ppermute | solution.py:130
  61.1 2.8 %collective-permute-start.10 = (bf16[64,4608]{1,0:T(8,128)(2,1)S(1)}, bf16[64,4608]{1,0:T(8,128)(2,1)S(1)}, u32[]{:S(2)}, u32[]{:S(2)}) collective-permute-start(bf16[64,4608]{1,0:T(8,128)(2,1)S(1)} %collective-permute-done.x2), channel_id=1, source_target_pairs={{0,1},{1,0},{2,3},{3,2},{4,5},{5,4},{6,7},{7,6},{8,9},{9,8},{10,11... | collective-permute-start | bytes 1769480 | tf_op jit(solution)/shard_map/ppermute | solution.py:130
  61.6 17.8 %collective-permute-start.7 = (bf16[64,4608]{1,0:T(8,128)(2,1)S(1)}, bf16[64,4608]{1,0:T(8,128)(2,1)S(1)}, u32[]{:S(2)}, u32[]{:S(2)}) collective-permute-start(bf16[64,4608]{1,0:T(8,128)(2,1)S(1)} %collective-permute-done.x2), channel_id=1, source_target_pairs={{0,2},{1,7},{2,4},{3,1},{4,6},{5,3},{6,0},{7,5},{8,10},{9,15},{10,... | collective-permute-start | bytes 1769480 | tf_op jit(solution)/shard_map/ppermute | solution.py:130
  63.9 24.0 %copy-start.2 = (bf16[4608,128]{1,0:T(8,128)(2,1)S(1)}, bf16[4608,128]{1,0:T(8,128)(2,1)}, u32[]{:S(2)}) copy-start(bf16[4608,128]{1,0:T(8,128)(2,1)} %wk.5) | copy-start | bytes 3538948
  63.9 24.0 %copy-start.4 = (bf16[4608,128]{1,0:T(8,128)(2,1)S(1)}, bf16[4608,128]{1,0:T(8,128)(2,1)}, u32[]{:S(2)}) copy-start(bf16[4608,128]{1,0:T(8,128)(2,1)} %wv.5) | copy-start | bytes 3538948
  63.9 24.0 %copy-start.5 = (bf16[4608,256]{1,0:T(8,128)(2,1)S(1)}, bf16[4608,256]{1,0:T(8,128)(2,1)}, u32[]{:S(2)}) copy-start(bf16[4608,256]{1,0:T(8,128)(2,1)} %wq.3) | copy-start | bytes 7077892
  79.4 8.5 %collective-permute-start.11 = (bf16[64,4608]{1,0:T(8,128)(2,1)S(1)}, bf16[64,4608]{1,0:T(8,128)(2,1)S(1)}, u32[]{:S(2)}, u32[]{:S(2)}) collective-permute-start(bf16[64,4608]{1,0:T(8,128)(2,1)S(1)} %collective-permute-done.7.x0), channel_id=1, source_target_pairs={{0,1},{1,0},{2,3},{3,2},{4,5},{5,4},{6,7},{7,6},{8,9},{9,8},{10,11... | collective-permute-start | bytes 1769480 | tf_op jit(solution)/shard_map/ppermute | solution.py:130
  79.4 18.4 %collective-permute-start.17 = (bf16[384,256]{1,0:T(8,128)(2,1)S(1)}, bf16[384,256]{1,0:T(8,128)(2,1)S(1)}, u32[]{:S(2)}, u32[]{:S(2)}) collective-permute-start(bf16[384,256]{1,0:T(8,128)(2,1)S(1)} %get-tuple-element.50.own_a), channel_id=1, source_target_pairs={{0,24},{8,32},{16,40},{24,48},{32,56},{40,64},{48,72},{56,80},{64,... | collective-permute-start | bytes 589832 | tf_op jit(solution)/shard_map/ppermute | solution.py:460
  82.6 17.2 %collective-permute-start.16 = (bf16[384,256]{1,0:T(8,128)(2,1)S(1)}, bf16[384,256]{1,0:T(8,128)(2,1)S(1)}, u32[]{:S(2)}, u32[]{:S(2)}) collective-permute-start(bf16[384,256]{1,0:T(8,128)(2,1)S(1)} %get-tuple-element.50.own_a), channel_id=1, source_target_pairs={{0,16},{8,24},{16,32},{24,40},{32,48},{40,56},{48,64},{56,72},{64,... | collective-permute-start | bytes 589832 | tf_op jit(solution)/shard_map/ppermute | solution.py:460
  86.0 13.8 %collective-permute-start.15 = (bf16[384,256]{1,0:T(8,128)(2,1)S(1)}, bf16[384,256]{1,0:T(8,128)(2,1)S(1)}, u32[]{:S(2)}, u32[]{:S(2)}) collective-permute-start(bf16[384,256]{1,0:T(8,128)(2,1)S(1)} %get-tuple-element.50.own_a), channel_id=1, source_target_pairs={{0,8},{8,16},{16,24},{24,32},{32,40},{40,48},{48,56},{56,64},{64,7... | collective-permute-start | bytes 589832 | tf_op jit(solution)/shard_map/ppermute | solution.py:460
  88.0 11.8 %copy-start.8 = (s32[4,128]{1,0:T(4,128)S(1)}, s32[4,128]{1,0:T(4,128)}, u32[]{:S(2)}) copy-start(s32[4,128]{1,0:T(4,128)} %pattern.3) | copy-start | bytes 6148
  88.8 14.3 %collective-permute-start.14 = (bf16[128,256]{1,0:T(8,128)(2,1)S(1)}, bf16[128,256]{1,0:T(8,128)(2,1)S(1)}, u32[]{:S(2)}, u32[]{:S(2)}) collective-permute-start(bf16[128,256]{1,0:T(8,128)(2,1)S(1)} %get-tuple-element.49.own_c), channel_id=1, source_target_pairs={{0,24},{8,32},{16,40},{24,48},{32,56},{40,64},{48,72},{56,80},{64,... | collective-permute-start | bytes 196616 | tf_op jit(solution)/shard_map/ppermute | solution.py:464
  94.4 9.0 %collective-permute-start.13 = (bf16[128,256]{1,0:T(8,128)(2,1)S(1)}, bf16[128,256]{1,0:T(8,128)(2,1)S(1)}, u32[]{:S(2)}, u32[]{:S(2)}) collective-permute-start(bf16[128,256]{1,0:T(8,128)(2,1)S(1)} %get-tuple-element.49.own_c), channel_id=1, source_target_pairs={{0,16},{8,24},{16,32},{24,40},{32,48},{40,56},{48,64},{56,72},{64,... | collective-permute-start | bytes 196616 | tf_op jit(solution)/shard_map/ppermute | solution.py:464
  97.8 8.3 %collective-permute-start.12 = (bf16[128,256]{1,0:T(8,128)(2,1)S(1)}, bf16[128,256]{1,0:T(8,128)(2,1)S(1)}, u32[]{:S(2)}, u32[]{:S(2)}) collective-permute-start(bf16[128,256]{1,0:T(8,128)(2,1)S(1)} %get-tuple-element.49.own_c), channel_id=1, source_target_pairs={{0,8},{8,16},{16,24},{24,32},{32,40},{40,48},{48,56},{56,64},{64,7... | collective-permute-start | bytes 196616 | tf_op jit(solution)/shard_map/ppermute | solution.py:464
  107.5 1.4 collective-permute-start.18
  112.0 30.3 %collective-permute-start.20 = (bf16[64,4608]{1,0:T(8,128)(2,1)S(1)}, bf16[64,4608]{1,0:T(8,128)(2,1)S(1)}, u32[]{:S(2)}, u32[]{:S(2)}) collective-permute-start(bf16[64,4608]{1,0:T(8,128)(2,1)S(1)} %get-tuple-element.62), channel_id=1, source_target_pairs={{0,2},{1,7},{2,4},{3,1},{4,6},{5,3},{6,0},{7,5},{8,10},{9,15},{10,... | collective-permute-start | bytes 1769480 | tf_op jit(solution)/shard_map/ppermute | solution.py:130
  116.3 29.7 %collective-permute-start.19 = (bf16[64,4608]{1,0:T(8,128)(2,1)S(1)}, bf16[64,4608]{1,0:T(8,128)(2,1)S(1)}, u32[]{:S(2)}, u32[]{:S(2)}) collective-permute-start(bf16[64,4608]{1,0:T(8,128)(2,1)S(1)} %get-tuple-element.60), channel_id=1, source_target_pairs={{0,6},{1,3},{2,0},{3,5},{4,2},{5,7},{6,4},{7,1},{8,14},{9,11},{10,... | collective-permute-start | bytes 1769480 | tf_op jit(solution)/shard_map/ppermute | solution.py:130
  142.5 12.7 %collective-permute-start.21 = (bf16[64,4608]{1,0:T(8,128)(2,1)S(1)}, bf16[64,4608]{1,0:T(8,128)(2,1)S(1)}, u32[]{:S(2)}, u32[]{:S(2)}) collective-permute-start(bf16[64,4608]{1,0:T(8,128)(2,1)S(1)} %add_convert_fusion), channel_id=1, source_target_pairs={{0,2},{1,7},{2,4},{3,1},{4,6},{5,3},{6,0},{7,5},{8,10},{9,15},{10,... | collective-permute-start | bytes 1769480 | tf_op jit(solution)/shard_map/ppermute | solution.py:130
  155.2 1.1 copy-start.12
  155.2 1.1 copy-start.14

commit v4 on v3

--- a/solution.py
+++ b/solution.py
@@ -445,10 +445,8 @@
     w_sib = to(w_out, SIB)
     early = jnp.concatenate([first] + [c[:per_peer] for c in column], axis=0)
     early_kv = early_keys(lengths, early, to(early, SIB), norm_gain, w_key, w_value, n_dp)
-    prompt = lax.all_to_all(early_kv, "dp", 0, 0, tiled=True)
-    prompt = prompt.reshape(SHARD, 2 * HD)
-    near_o, near_b, prompt, w_sib, cos_a = lax.optimization_barrier(
-        (near_o, near_b, prompt, w_sib, cos_a)
+    near_o, near_b, early_kv, w_sib, cos_a = lax.optimization_barrier(
+        (near_o, near_b, early_kv, w_sib, cos_a)
     )
     far_own = to(near_o, OUT)
     near_os = to(near_b, SIB)
@@ -458,7 +456,10 @@
     )
     shifts = [[(s, s + k) for s in range(n_dp - k)] for k in (1, 2, 3)]
     kvs_a = [kv_a] + [lax.ppermute(kv_a, "dp", shift) for shift in shifts]
-    far_own, kv_a = lax.optimization_barrier((far_own, kv_a))
+    early_kv, kv_a = lax.optimization_barrier((early_kv, kv_a))
+    prompt = lax.all_to_all(early_kv, "dp", 0, 0, tiled=True)
+    prompt = prompt.reshape(SHARD, 2 * HD)
+    far_own, prompt = lax.optimization_barrier((far_own, prompt))
     far_s = to(far_own, SIB)
     q, kv_c = project_far(far_own, far_s, w_query, w_key, w_value, cos_c, sin_c, q_a)
     kvs_c = [lax.ppermute(kv_c, "dp", shift) for shift in shifts]

time: 158 us -> 170 us (1.076)
  the two profiles are of different devices: /device:TPU:8 before, /device:TPU:73 now
where the time goes in v4:
time: 170 us; the launch traced here: 169 us
  waiting for transfers between devices  65.7 us (39%)
  starting transfers between devices  61.4 us (36%)
  Pallas kernels  22.1 us (13%)
  local copies, waits for them, and re-layouts  12.6 us (7%)
  other arithmetic  6.15 us (4%)
    ppermute x16, waiting for transfers between devices, to(): return lax.ppermute(values, 'tensor', pairs)  61.7 us
    ppermute x16, starting transfers between devices, to(): return lax.ppermute(values, 'tensor', pairs)  27.7 us
    ppermute x3, starting transfers between devices, body(): kvs_c = [lax.ppermute(kv_c, 'dp', shift) for shift in shifts]  11.9 us
    all_to_all x1, starting transfers between devices, body(): lax.all_to_all(send.reshape(n_dp, per_peer, width), 'dp', 0, 0, tiled=True)  8.39 us
    ppermute x3, starting transfers between devices, body(): kvs_a = [kv_a] + [lax.ppermute(kv_a, 'dp', shift) for shift in shifts]  7.94 us
    pallas_call x2, Pallas kernels, project_out(): pl.pallas_call(functools.partial(out_kernel, chunks), in_specs=[VMEM] * 2...  6.09 us
    all_to_all x1, starting transfers between devices, body(): prompt = lax.all_to_all(early_kv, 'dp', 0, 0, tiled=True)  5.5 us
    pallas_call x1, Pallas kernels, project_near(): pl.pallas_call(near_kernel, in_specs=[VMEM] * 6 + [hbm] * 5, out_specs=[V...  5.41 us
  transfers between devices with their start and end apart: 24, of which 9 were waited for; matrix products, arithmetic and copies ran while one was open for 5% of the time, Pallas kernels for 10%

profile of v4, /device:TPU:73, one launch (start us, length us, event | category | flops | bytes accessed | tf_op | source)
XLA Modules:
  0.0 168.9 jit_solution(11837588973821004201)
XLA Ops:
  0.0 0.7 and_select_fusion.1
  0.7 0.2 convert_reduce_fusion.1
  0.9 0.1 select_reduce_fusion
  1.1 0.3 convolution_convert_fusion.1
  1.4 0.9 pad_maximum_fusion
  2.3 2.7 %reshape.41 = bf16[32,2,4736]{2,1,0:T(2,128)(2,1)} reshape(bf16[64,4736]{1,0:T(8,128)(2,1)} %pad_maximum_fusion) | data formatting | bytes 1212416 | tf_op jit(solution)/shard_map/reshape | solution.py:426
  5.1 8.4 %all-to-all-start = ((bf16[32,2,4736]{2,1,0:T(2,128)(2,1)}), bf16[32,2,4736]{2,1,0:T(2,128)(2,1)}, u32[]{:S(2)}, u32[]{:S(2)}) async-start(bf16[32,2,4736]{2,1,0:T(2,128)(2,1)} %reshape.41), calls=%async_computation | async-start | bytes 1212416 | tf_op jit(solution)/shard_map/all_to_all | solution.py:426
  13.5 1.4 fusion.6
  14.8 4.2 %collective-permute-start.4 = (bf16[8,4736]{1,0:T(8,128)(2,1)}, bf16[8,4736]{1,0:T(8,128)(2,1)}, u32[]{:S(2)}, u32[]{:S(2)}) collective-permute-start(bf16[8,4736]{1,0:T(8,128)(2,1)} %fusion.6), channel_id=1, source_target_pairs={{0,4},{1,5},{2,6},{3,7},{4,0},{5,1},{6,2},{7,3},{8,12},{9,13},{10,... | collective-permute-start | bytes 227336 | tf_op jit(solution)/shard_map/ppermute | solution.py:130
  19.0 2.4 %collective-permute-start.2 = (bf16[8,4736]{1,0:T(8,128)(2,1)}, bf16[8,4736]{1,0:T(8,128)(2,1)}, u32[]{:S(2)}, u32[]{:S(2)}) collective-permute-start(bf16[8,4736]{1,0:T(8,128)(2,1)} %fusion.6), channel_id=1, source_target_pairs={{0,2},{1,7},{2,4},{3,1},{4,6},{5,3},{6,0},{7,5},{8,10},{9,15},{10,... | collective-permute-start | bytes 227336 | tf_op jit(solution)/shard_map/ppermute | solution.py:130
  21.4 3.3 %collective-permute-start.6 = (bf16[256,4608]{1,0:T(8,128)(2,1)S(1)}, bf16[256,4608]{1,0:T(8,128)(2,1)}, u32[]{:S(2)}, u32[]{:S(2)}) collective-permute-start(bf16[256,4608]{1,0:T(8,128)(2,1)S(1)} %copy-done.13), channel_id=1, source_target_pairs={{0,1},{1,0},{2,3},{3,2},{4,5},{5,4},{6,7},{7,6},{8,9},{9,8},{10,11... | collective-permute-start | bytes 7077896 | tf_op jit(solution)/shard_map/ppermute | solution.py:130
  24.7 0.6 fusion.8
  25.3 2.0 %reshape.42 = bf16[64,4736]{1,0:T(8,128)(2,1)S(1)} reshape(bf16[32,2,4736]{2,1,0:T(2,128)(2,1)} %all-to-all-done) | data formatting | bytes 1212416 | tf_op jit(solution)/shard_map/reshape | solution.py:433
  27.3 0.1 convert_reduce_fusion
  27.4 0.3 convolution_convert_fusion
  27.8 0.2 fusion
  28.0 0.5 copy-done.14
  28.6 0.2 fusion.2.x0
  28.8 1.5 collective-permute-start.1
  30.3 1.0 collective-permute-start
  31.2 0.9 slice.25
  32.1 0.9 slice.26
  33.0 0.9 slice.27
  33.9 0.1 pad_maximum_fusion.1.own
  34.0 4.9 %collective-permute-start.5 = (bf16[8,4736]{1,0:T(8,128)(2,1)S(1)}, bf16[8,4736]{1,0:T(8,128)(2,1)S(1)}, u32[]{:S(2)}, u32[]{:S(2)}) collective-permute-start(bf16[8,4736]{1,0:T(8,128)(2,1)S(1)} %pad_maximum_fusion.1.own), channel_id=1, source_target_pairs={{0,1},{1,0},{2,3},{3,2},{4,5},{5,4},{6,7},{7,6},{8,9},{9,8},{10,11... | collective-permute-start | bytes 227336 | tf_op jit(solution)/shard_map/ppermute | solution.py:130
  39.0 0.1 collective-permute-start.8
  39.1 2.0 %tables.1 = (f32[384,128]{1,0:T(8,128)S(1)}, f32[384,128]{1,0:T(8,128)S(1)}, f32[128,128]{1,0:T(8,128)S(1)}, f32[128,128]{1,0:T(8,128)S(1)}) custom-call(s32[17]{0:T(128)S(1)} %copy-done.11, f32[1,128]{1,0:T(1,128)S(1)} %copy-done.12), custom_call_target="tpu_custom_call" | custom-call | tf_op jit(solution)/shard_map/tables/pallas_call | solution.py:81
  41.2 0.7 copy-done.8
  41.8 0.7 copy-done.9
  42.5 1.8 %early.1 = bf16[32,16,256]{2,1,0:T(8,128)(2,1)} custom-call(s32[17]{0:T(128)S(1)} %copy-done.11, f32[1,128]{1,0:T(1,128)S(1)} %copy-done.12, bf16[8,4736]{1,0:T(8,128)(2,1)S(1)} %pad_maximum_fusion.1.own, bf16[8,4736]{1,0:T(8,128)(2,1)S(1)} %collective-permute-done.5.sib, f32[1,4608]{1,0:T(1,128)S(1)} %broadcast_in_dim.19.gain, ...), custom_call_target="tpu_custom_call" | custom-call | tf_op jit(solution)/shard_map/early/pallas_call | solution.py:115
  44.4 14.9 %collective-permute-done.x2 = bf16[64,4608]{1,0:T(8,128)(2,1)} collective-permute-done((bf16[64,4608]{1,0:T(8,128)(2,1)S(1)}, bf16[64,4608]{1,0:T(8,128)(2,1)}, u32[]{:S(2)}, u32[]{:S(2)}) %collective-permute-start) | collective-permute-done | bytes 589856 | tf_op jit(solution)/shard_map/ppermute | solution.py:130
  59.3 1.5 collective-permute-start.9
  60.8 0.3 collective-permute-start.10
  61.0 1.3 collective-permute-done.9.x3
  62.4 1.1 collective-permute-done.10.x5
  63.4 5.4 %project_near.1 = (bf16[2,384,128]{2,1,0:T(8,128)(2,1)S(1)}, bf16[384,256]{1,0:T(8,128)(2,1)S(1)}) custom-call(bf16[64,4608]{1,0:T(8,128)(2,1)S(1)} %fusion.2.x0, bf16[64,4608]{1,0:T(8,128)(2,1)S(1)} %collective-permute-done.8.x1, bf16[64,4608]{1,0:T(8,128)(2,1)} %collective-permute-done.x2, bf16[64,4608]{1,0:T(8,128)(2,1)S(1)} %collective-permute-done.9.x3, ...), custom_call_target="tpu_custom_call" | custom-call | tf_op jit(solution)/shard_map/project_near/pallas_call | solution.py:199
  68.9 0.7 copy-done.6
  69.5 5.5 %all-to-all-start.1 = ((bf16[32,16,256]{2,1,0:T(8,128)(2,1)}), bf16[32,16,256]{2,1,0:T(8,128)(2,1)S(1)}, u32[]{:S(2)}, u32[]{:S(2)}) async-start(bf16[32,16,256]{2,1,0:T(8,128)(2,1)} %early.1), calls=%async_computation.1 | async-start | bytes 524288 | tf_op jit(solution)/shard_map/all_to_all | solution.py:460
  75.0 3.3 %collective-permute-done.7.x0 = bf16[64,4608]{1,0:T(8,128)(2,1)} collective-permute-done((bf16[64,4608]{1,0:T(8,128)(2,1)}, bf16[64,4608]{1,0:T(8,128)(2,1)}, u32[]{:S(2)}, u32[]{:S(2)}) %collective-permute-start.7) | collective-permute-done | bytes 589856 | tf_op jit(solution)/shard_map/ppermute | solution.py:130
  78.4 3.9 %all-to-all-done.1 = bf16[32,16,256]{2,1,0:T(8,128)(2,1)S(1)} async-done(((bf16[32,16,256]{2,1,0:T(8,128)(2,1)}), bf16[32,16,256]{2,1,0:T(8,128)(2,1)S(1)}, u32[]{:S(2)}, u32[]{:S(2)}) %all-to-all-start.1) | async-done | bytes 262176 | tf_op jit(solution)/shard_map/all_to_all | solution.py:460
  82.3 1.9 %collective-permute-start.11 = (bf16[64,4608]{1,0:T(8,128)(2,1)}, bf16[64,4608]{1,0:T(8,128)(2,1)S(1)}, u32[]{:S(2)}, u32[]{:S(2)}) collective-permute-start(bf16[64,4608]{1,0:T(8,128)(2,1)} %collective-permute-done.7.x0), channel_id=1, source_target_pairs={{0,1},{1,0},{2,3},{3,2},{4,5},{5,4},{6,7},{7,6},{8,9},{9,8},{10,11... | collective-permute-start | bytes 1769480 | tf_op jit(solution)/shard_map/ppermute | solution.py:130
  84.2 2.8 %collective-permute-start.17 = (bf16[384,256]{1,0:T(8,128)(2,1)}, bf16[384,256]{1,0:T(8,128)(2,1)S(1)}, u32[]{:S(2)}, u32[]{:S(2)}) collective-permute-start(bf16[384,256]{1,0:T(8,128)(2,1)} %copy-done.6), channel_id=1, source_target_pairs={{0,24},{8,32},{16,40},{24,48},{32,56},{40,64},{48,72},{56,80},{64,... | collective-permute-start | bytes 589832 | tf_op jit(solution)/shard_map/ppermute | solution.py:458
  87.0 3.2 %collective-permute-start.16 = (bf16[384,256]{1,0:T(8,128)(2,1)}, bf16[384,256]{1,0:T(8,128)(2,1)S(1)}, u32[]{:S(2)}, u32[]{:S(2)}) collective-permute-start(bf16[384,256]{1,0:T(8,128)(2,1)} %copy-done.6), channel_id=1, source_target_pairs={{0,16},{8,24},{16,32},{24,40},{32,48},{40,56},{48,64},{56,72},{64,... | collective-permute-start | bytes 589832 | tf_op jit(solution)/shard_map/ppermute | solution.py:458
  90.2 1.9 %collective-permute-start.15 = (bf16[384,256]{1,0:T(8,128)(2,1)}, bf16[384,256]{1,0:T(8,128)(2,1)S(1)}, u32[]{:S(2)}, u32[]{:S(2)}) collective-permute-start(bf16[384,256]{1,0:T(8,128)(2,1)} %copy-done.6), channel_id=1, source_target_pairs={{0,8},{8,16},{16,24},{24,32},{32,40},{40,48},{48,56},{56,64},{64,7... | collective-permute-start | bytes 589832 | tf_op jit(solution)/shard_map/ppermute | solution.py:458
  92.2 1.7 copy-done.5
  93.9 2.0 %project_far.1 = (bf16[1024,128]{1,0:T(8,128)(2,1)S(1)}, bf16[128,256]{1,0:T(8,128)(2,1)S(1)}) custom-call(bf16[64,4608]{1,0:T(8,128)(2,1)} %collective-permute-done.7.x0, bf16[64,4608]{1,0:T(8,128)(2,1)S(1)} %collective-permute-done.11.x1, bf16[4608,256]{1,0:T(8,128)(2,1)S(1)} %copy-done.5, bf16[4608,128]{1,0:T(8,128)(2,1)S(1)} %copy-done.2, ...), custom_call_target="tpu_custom_call" | custom-call | tf_op jit(solution)/shard_map/project_far/pallas_call | solution.py:218
  95.8 5.4 %collective-permute-start.14 = (bf16[128,256]{1,0:T(8,128)(2,1)S(1)}, bf16[128,256]{1,0:T(8,128)(2,1)S(1)}, u32[]{:S(2)}, u32[]{:S(2)}) collective-permute-start(bf16[128,256]{1,0:T(8,128)(2,1)S(1)} %get-tuple-element.53.own_c), channel_id=1, source_target_pairs={{0,24},{8,32},{16,40},{24,48},{32,56},{40,64},{48,72},{56,80},{64,... | collective-permute-start | bytes 196616 | tf_op jit(solution)/shard_map/ppermute | solution.py:465
  101.2 2.8 %collective-permute-start.13 = (bf16[128,256]{1,0:T(8,128)(2,1)S(1)}, bf16[128,256]{1,0:T(8,128)(2,1)S(1)}, u32[]{:S(2)}, u32[]{:S(2)}) collective-permute-start(bf16[128,256]{1,0:T(8,128)(2,1)S(1)} %get-tuple-element.53.own_c), channel_id=1, source_target_pairs={{0,16},{8,24},{16,32},{24,40},{32,48},{40,56},{48,64},{56,72},{64,... | collective-permute-start | bytes 196616 | tf_op jit(solution)/shard_map/ppermute | solution.py:465
  104.0 3.8 %collective-permute-start.12 = (bf16[128,256]{1,0:T(8,128)(2,1)S(1)}, bf16[128,256]{1,0:T(8,128)(2,1)S(1)}, u32[]{:S(2)}, u32[]{:S(2)}) collective-permute-start(bf16[128,256]{1,0:T(8,128)(2,1)S(1)} %get-tuple-element.53.own_c), channel_id=1, source_target_pairs={{0,8},{8,16},{16,24},{24,32},{32,40},{40,48},{48,56},{56,64},{64,7... | collective-permute-start | bytes 196616 | tf_op jit(solution)/shard_map/ppermute | solution.py:465
  107.8 3.3 %attend.1 = (f32[1024,128]{1,0:T(8,128)S(1)}, f32[1024,128]{1,0:T(8,128)S(1)}) custom-call(s32[4,128]{1,0:T(4,128)S(1)} %copy-done.10, bf16[1024,128]{1,0:T(8,128)(2,1)S(1)} %get-tuple-element.52.q, bf16[384,256]{1,0:T(8,128)(2,1)S(1)} %copy-done.7, bf16[128,256]{1,0:T(8,128)(2,1)S(1)} %get-tuple-element.53.own_c, ...), custom_call_target="tpu_custom_call" | custom-call | tf_op jit(solution)/shard_map/attend/pallas_call | solution.py:339
  111.3 1.4 attend_far.1
  112.7 2.5 %collective-permute-start.18 = (bf16[256,256]{1,0:T(8,128)(2,1)S(1)}, bf16[256,256]{1,0:T(8,128)(2,1)S(1)}, u32[]{:S(2)}, u32[]{:S(2)}) collective-permute-start(bf16[256,256]{1,0:T(8,128)(2,1)S(1)} %get-tuple-element.59), channel_id=1, source_target_pairs={{0,1},{1,0},{2,3},{3,2},{4,5},{5,4},{6,7},{7,6},{8,9},{9,8},{10,11... | collective-permute-start | bytes 393224 | tf_op jit(solution)/shard_map/ppermute | solution.py:130
  115.2 1.0 collective-permute-done.18.theirs
  116.2 3.0 %project_out.2 = (bf16[64,4608]{1,0:T(8,128)(2,1)S(1)}, bf16[64,4608]{1,0:T(8,128)(2,1)S(1)}) custom-call(bf16[256,256]{1,0:T(8,128)(2,1)S(1)} %get-tuple-element.58.ours, bf16[256,256]{1,0:T(8,128)(2,1)S(1)} %collective-permute-done.18.theirs, bf16[256,4608]{1,0:T(8,128)(2,1)} %w0.3, bf16[256,4608]{1,0:T(8,128)(2,1)} %collective-permute-done.6.w1), custom_call_target="tpu_custom_call" | custom-call | tf_op jit(solution)/shard_map/project_out/pallas_call | solution.py:392
  119.3 1.4 collective-permute-start.20
  120.7 3.0 %project_out.3 = (f32[64,4608]{1,0:T(8,128)S(1)}, f32[64,4608]{1,0:T(8,128)S(1)}) custom-call(bf16[256,256]{1,0:T(8,128)(2,1)S(1)} %get-tuple-element.58.ours, bf16[256,256]{1,0:T(8,128)(2,1)S(1)} %collective-permute-done.18.theirs, bf16[256,4608]{1,0:T(8,128)(2,1)} %w0.3, bf16[256,4608]{1,0:T(8,128)(2,1)} %collective-permute-done.6.w1), custom_call_target="tpu_custom_call" | custom-call | tf_op jit(solution)/shard_map/project_out/pallas_call | solution.py:392
  123.7 2.5 %collective-permute-start.19 = (bf16[64,4608]{1,0:T(8,128)(2,1)S(1)}, bf16[64,4608]{1,0:T(8,128)(2,1)S(1)}, u32[]{:S(2)}, u32[]{:S(2)}) collective-permute-start(bf16[64,4608]{1,0:T(8,128)(2,1)S(1)} %get-tuple-element.64), channel_id=1, source_target_pairs={{0,6},{1,3},{2,0},{3,5},{4,2},{5,7},{6,4},{7,1},{8,14},{9,11},{10,... | collective-permute-start | bytes 1769480 | tf_op jit(solution)/shard_map/ppermute | solution.py:130
  126.3 29.4 %collective-permute-done.20 = bf16[64,4608]{1,0:T(8,128)(2,1)S(1)} collective-permute-done((bf16[64,4608]{1,0:T(8,128)(2,1)S(1)}, bf16[64,4608]{1,0:T(8,128)(2,1)S(1)}, u32[]{:S(2)}, u32[]{:S(2)}) %collective-permute-start.20) | collective-permute-done | bytes 589856 | tf_op jit(solution)/shard_map/ppermute | solution.py:130
  155.6 0.1 add_convert_fusion
  155.8 0.2 collective-permute-start.21
  156.0 10.7 %collective-permute-done.21 = bf16[64,4608]{1,0:T(8,128)(2,1)S(1)} collective-permute-done((bf16[64,4608]{1,0:T(8,128)(2,1)S(1)}, bf16[64,4608]{1,0:T(8,128)(2,1)S(1)}, u32[]{:S(2)}, u32[]{:S(2)}) %collective-permute-start.21) | collective-permute-done | bytes 589856 | tf_op jit(solution)/shard_map/ppermute | solution.py:130
  166.7 0.3 multiply_reduce_fusion
  167.0 0.7 copy-done.15
  167.7 1.2 fusion.3
  (56 shorter events, 0.4 us)
Async XLA Ops:
  0.0 1.1 copy-start
  2.3 19.1 %copy-start.13 = (bf16[256,4608]{1,0:T(8,128)(2,1)S(1)}, bf16[256,4608]{1,0:T(8,128)(2,1)}, u32[]{:S(2)}) copy-start(bf16[256,4608]{1,0:T(8,128)(2,1)} %w0.3) | copy-start | bytes 7077892
  5.1 20.2 %all-to-all-start = ((bf16[32,2,4736]{2,1,0:T(2,128)(2,1)}), bf16[32,2,4736]{2,1,0:T(2,128)(2,1)}, u32[]{:S(2)}, u32[]{:S(2)}) async-start(bf16[32,2,4736]{2,1,0:T(2,128)(2,1)} %reshape.41), calls=%async_computation | async-start | bytes 1212416 | tf_op jit(solution)/shard_map/all_to_all | solution.py:426
  14.8 15.4 %collective-permute-start.4 = (bf16[8,4736]{1,0:T(8,128)(2,1)}, bf16[8,4736]{1,0:T(8,128)(2,1)}, u32[]{:S(2)}, u32[]{:S(2)}) collective-permute-start(bf16[8,4736]{1,0:T(8,128)(2,1)} %fusion.6), channel_id=1, source_target_pairs={{0,4},{1,5},{2,6},{3,7},{4,0},{5,1},{6,2},{7,3},{8,12},{9,13},{10,... | collective-permute-start | bytes 227336 | tf_op jit(solution)/shard_map/ppermute | solution.py:130
  19.0 12.2 %collective-permute-start.3 = (bf16[8,4736]{1,0:T(8,128)(2,1)}, bf16[8,4736]{1,0:T(8,128)(2,1)}, u32[]{:S(2)}, u32[]{:S(2)}) collective-permute-start(bf16[8,4736]{1,0:T(8,128)(2,1)} %fusion.6), channel_id=1, source_target_pairs={{0,6},{1,3},{2,0},{3,5},{4,2},{5,7},{6,4},{7,1},{8,14},{9,11},{10,... | collective-permute-start | bytes 227336 | tf_op jit(solution)/shard_map/ppermute | solution.py:130
  19.0 12.2 %collective-permute-start.2 = (bf16[8,4736]{1,0:T(8,128)(2,1)}, bf16[8,4736]{1,0:T(8,128)(2,1)}, u32[]{:S(2)}, u32[]{:S(2)}) collective-permute-start(bf16[8,4736]{1,0:T(8,128)(2,1)} %fusion.6), channel_id=1, source_target_pairs={{0,2},{1,7},{2,4},{3,1},{4,6},{5,3},{6,0},{7,5},{8,10},{9,15},{10,... | collective-permute-start | bytes 227336 | tf_op jit(solution)/shard_map/ppermute | solution.py:130
  21.4 37.9 %collective-permute-start.6 = (bf16[256,4608]{1,0:T(8,128)(2,1)S(1)}, bf16[256,4608]{1,0:T(8,128)(2,1)}, u32[]{:S(2)}, u32[]{:S(2)}) collective-permute-start(bf16[256,4608]{1,0:T(8,128)(2,1)S(1)} %copy-done.13), channel_id=1, source_target_pairs={{0,1},{1,0},{2,3},{3,2},{4,5},{5,4},{6,7},{7,6},{8,9},{9,8},{10,11... | collective-permute-start | bytes 7077896 | tf_op jit(solution)/shard_map/ppermute | solution.py:130
  27.3 1.3 copy-start.16
  27.4 15.1 %copy-start.3 = (bf16[4608,128]{1,0:T(8,128)(2,1)S(1)}, bf16[4608,128]{1,0:T(8,128)(2,1)}, u32[]{:S(2)}) copy-start(bf16[4608,128]{1,0:T(8,128)(2,1)} %wv.5) | copy-start | bytes 3538948
  27.7 0.8 copy-start.14
  27.8 6.2 %copy-start.17 = (bf16[2,4736]{1,0:T(2,128)(2,1)S(1)}, bf16[2,4736]{1,0:T(2,128)(2,1)}, u32[]{:S(2)}) copy-start(bf16[2,4736]{1,0:T(2,128)(2,1)} %fusion.8) | copy-start | bytes 56836
  27.8 11.3 %copy-start.11 = (s32[17]{0:T(128)S(1)}, s32[17]{0:T(128)}, u32[]{:S(2)}) copy-start(s32[17]{0:T(128)} %lengths.2) | copy-start | bytes 208
  27.8 11.3 %copy-start.12 = (f32[1,128]{1,0:T(1,128)S(1)}, f32[1,128]{1,0:T(1,128)}, u32[]{:S(2)}) copy-start(f32[1,128]{1,0:T(1,128)} %constant.47.clone.freq) | copy-start | bytes 1540
  27.8 14.7 %copy-start.1 = (bf16[4608,128]{1,0:T(8,128)(2,1)S(1)}, bf16[4608,128]{1,0:T(8,128)(2,1)}, u32[]{:S(2)}) copy-start(bf16[4608,128]{1,0:T(8,128)(2,1)} %wk.5) | copy-start | bytes 3538948
  28.8 15.6 %collective-permute-start.1 = (bf16[64,4608]{1,0:T(8,128)(2,1)S(1)}, bf16[64,4608]{1,0:T(8,128)(2,1)S(1)}, u32[]{:S(2)}, u32[]{:S(2)}) collective-permute-start(bf16[64,4608]{1,0:T(8,128)(2,1)S(1)} %fusion.2.x0), channel_id=1, source_target_pairs={{0,6},{1,3},{2,0},{3,5},{4,2},{5,7},{6,4},{7,1},{8,14},{9,11},{10,... | collective-permute-start | bytes 1769480 | tf_op jit(solution)/shard_map/ppermute | solution.py:130
  30.3 29.0 %collective-permute-start = (bf16[64,4608]{1,0:T(8,128)(2,1)S(1)}, bf16[64,4608]{1,0:T(8,128)(2,1)}, u32[]{:S(2)}, u32[]{:S(2)}) collective-permute-start(bf16[64,4608]{1,0:T(8,128)(2,1)S(1)} %fusion.2.x0), channel_id=1, source_target_pairs={{0,2},{1,7},{2,4},{3,1},{4,6},{5,3},{6,0},{7,5},{8,10},{9,15},{10,... | collective-permute-start | bytes 1769480 | tf_op jit(solution)/shard_map/ppermute | solution.py:130
  34.0 8.5 %collective-permute-start.5 = (bf16[8,4736]{1,0:T(8,128)(2,1)S(1)}, bf16[8,4736]{1,0:T(8,128)(2,1)S(1)}, u32[]{:S(2)}, u32[]{:S(2)}) collective-permute-start(bf16[8,4736]{1,0:T(8,128)(2,1)S(1)} %pad_maximum_fusion.1.own), channel_id=1, source_target_pairs={{0,1},{1,0},{2,3},{3,2},{4,5},{5,4},{6,7},{7,6},{8,9},{9,8},{10,11... | collective-permute-start | bytes 227336 | tf_op jit(solution)/shard_map/ppermute | solution.py:130
  39.0 22.0 %collective-permute-start.8 = (bf16[64,4608]{1,0:T(8,128)(2,1)S(1)}, bf16[64,4608]{1,0:T(8,128)(2,1)S(1)}, u32[]{:S(2)}, u32[]{:S(2)}) collective-permute-start(bf16[64,4608]{1,0:T(8,128)(2,1)S(1)} %fusion.2.x0), channel_id=1, source_target_pairs={{0,1},{1,0},{2,3},{3,2},{4,5},{5,4},{6,7},{7,6},{8,9},{9,8},{10,11... | collective-permute-start | bytes 1769480 | tf_op jit(solution)/shard_map/ppermute | solution.py:130
  41.1 0.7 copy-start.8
  41.8 0.7 copy-start.9
  59.3 3.1 %collective-permute-start.9 = (bf16[64,4608]{1,0:T(8,128)(2,1)S(1)}, bf16[64,4608]{1,0:T(8,128)(2,1)S(1)}, u32[]{:S(2)}, u32[]{:S(2)}) collective-permute-start(bf16[64,4608]{1,0:T(8,128)(2,1)S(1)} %collective-permute-done.1.x4), channel_id=1, source_target_pairs={{0,1},{1,0},{2,3},{3,2},{4,5},{5,4},{6,7},{7,6},{8,9},{9,8},{10,11... | collective-permute-start | bytes 1769480 | tf_op jit(solution)/shard_map/ppermute | solution.py:130
  60.8 2.7 %collective-permute-start.10 = (bf16[64,4608]{1,0:T(8,128)(2,1)}, bf16[64,4608]{1,0:T(8,128)(2,1)S(1)}, u32[]{:S(2)}, u32[]{:S(2)}) collective-permute-start(bf16[64,4608]{1,0:T(8,128)(2,1)} %collective-permute-done.x2), channel_id=1, source_target_pairs={{0,1},{1,0},{2,3},{3,2},{4,5},{5,4},{6,7},{7,6},{8,9},{9,8},{10,11... | collective-permute-start | bytes 1769480 | tf_op jit(solution)/shard_map/ppermute | solution.py:130
  61.0 17.4 %collective-permute-start.7 = (bf16[64,4608]{1,0:T(8,128)(2,1)}, bf16[64,4608]{1,0:T(8,128)(2,1)}, u32[]{:S(2)}, u32[]{:S(2)}) collective-permute-start(bf16[64,4608]{1,0:T(8,128)(2,1)} %collective-permute-done.x2), channel_id=1, source_target_pairs={{0,2},{1,7},{2,4},{3,1},{4,6},{5,3},{6,0},{7,5},{8,10},{9,15},{10,... | collective-permute-start | bytes 1769480 | tf_op jit(solution)/shard_map/ppermute | solution.py:130
  63.4 28.7 %copy-start.2 = (bf16[4608,128]{1,0:T(8,128)(2,1)S(1)}, bf16[4608,128]{1,0:T(8,128)(2,1)}, u32[]{:S(2)}) copy-start(bf16[4608,128]{1,0:T(8,128)(2,1)} %wk.5) | copy-start | bytes 3538948
  63.4 28.7 %copy-start.4 = (bf16[4608,128]{1,0:T(8,128)(2,1)S(1)}, bf16[4608,128]{1,0:T(8,128)(2,1)}, u32[]{:S(2)}) copy-start(bf16[4608,128]{1,0:T(8,128)(2,1)} %wv.5) | copy-start | bytes 3538948
  68.9 0.7 copy-start.6
  69.5 12.7 %all-to-all-start.1 = ((bf16[32,16,256]{2,1,0:T(8,128)(2,1)}), bf16[32,16,256]{2,1,0:T(8,128)(2,1)S(1)}, u32[]{:S(2)}, u32[]{:S(2)}) async-start(bf16[32,16,256]{2,1,0:T(8,128)(2,1)} %early.1), calls=%async_computation.1 | async-start | bytes 524288 | tf_op jit(solution)/shard_map/all_to_all | solution.py:460
  82.3 9.9 %collective-permute-start.11 = (bf16[64,4608]{1,0:T(8,128)(2,1)}, bf16[64,4608]{1,0:T(8,128)(2,1)S(1)}, u32[]{:S(2)}, u32[]{:S(2)}) collective-permute-start(bf16[64,4608]{1,0:T(8,128)(2,1)} %collective-permute-done.7.x0), channel_id=1, source_target_pairs={{0,1},{1,0},{2,3},{3,2},{4,5},{5,4},{6,7},{7,6},{8,9},{9,8},{10,11... | collective-permute-start | bytes 1769480 | tf_op jit(solution)/shard_map/ppermute | solution.py:130
  84.2 19.8 %collective-permute-start.17 = (bf16[384,256]{1,0:T(8,128)(2,1)}, bf16[384,256]{1,0:T(8,128)(2,1)S(1)}, u32[]{:S(2)}, u32[]{:S(2)}) collective-permute-start(bf16[384,256]{1,0:T(8,128)(2,1)} %copy-done.6), channel_id=1, source_target_pairs={{0,24},{8,32},{16,40},{24,48},{32,56},{40,64},{48,72},{56,80},{64,... | collective-permute-start | bytes 589832 | tf_op jit(solution)/shard_map/ppermute | solution.py:458
  87.0 20.8 %collective-permute-start.16 = (bf16[384,256]{1,0:T(8,128)(2,1)}, bf16[384,256]{1,0:T(8,128)(2,1)S(1)}, u32[]{:S(2)}, u32[]{:S(2)}) collective-permute-start(bf16[384,256]{1,0:T(8,128)(2,1)} %copy-done.6), channel_id=1, source_target_pairs={{0,16},{8,24},{16,32},{24,40},{32,48},{40,56},{48,64},{56,72},{64,... | collective-permute-start | bytes 589832 | tf_op jit(solution)/shard_map/ppermute | solution.py:458
  90.2 17.6 %collective-permute-start.15 = (bf16[384,256]{1,0:T(8,128)(2,1)}, bf16[384,256]{1,0:T(8,128)(2,1)S(1)}, u32[]{:S(2)}, u32[]{:S(2)}) collective-permute-start(bf16[384,256]{1,0:T(8,128)(2,1)} %copy-done.6), channel_id=1, source_target_pairs={{0,8},{8,16},{16,24},{24,32},{32,40},{40,48},{48,56},{56,64},{64,7... | collective-permute-start | bytes 589832 | tf_op jit(solution)/shard_map/ppermute | solution.py:458
  92.2 1.7 copy-start.5
  93.8 14.0 %copy-start.7 = (bf16[384,256]{1,0:T(8,128)(2,1)S(1)}, bf16[384,256]{1,0:T(8,128)(2,1)}, u32[]{:S(2)}) copy-start(bf16[384,256]{1,0:T(8,128)(2,1)} %copy-done.6) | copy-start | bytes 589828
  93.9 14.0 %copy-start.10 = (s32[4,128]{1,0:T(4,128)S(1)}, s32[4,128]{1,0:T(4,128)}, u32[]{:S(2)}) copy-start(s32[4,128]{1,0:T(4,128)} %pattern.3) | copy-start | bytes 6148
  95.8 15.3 %collective-permute-start.14 = (bf16[128,256]{1,0:T(8,128)(2,1)S(1)}, bf16[128,256]{1,0:T(8,128)(2,1)S(1)}, u32[]{:S(2)}, u32[]{:S(2)}) collective-permute-start(bf16[128,256]{1,0:T(8,128)(2,1)S(1)} %get-tuple-element.53.own_c), channel_id=1, source_target_pairs={{0,24},{8,32},{16,40},{24,48},{32,56},{40,64},{48,72},{56,80},{64,... | collective-permute-start | bytes 196616 | tf_op jit(solution)/shard_map/ppermute | solution.py:465
  101.2 9.9 %collective-permute-start.13 = (bf16[128,256]{1,0:T(8,128)(2,1)S(1)}, bf16[128,256]{1,0:T(8,128)(2,1)S(1)}, u32[]{:S(2)}, u32[]{:S(2)}) collective-permute-start(bf16[128,256]{1,0:T(8,128)(2,1)S(1)} %get-tuple-element.53.own_c), channel_id=1, source_target_pairs={{0,16},{8,24},{16,32},{24,40},{32,48},{40,56},{48,64},{56,72},{64,... | collective-permute-start | bytes 196616 | tf_op jit(solution)/shard_map/ppermute | solution.py:465
  104.0 7.2 %collective-permute-start.12 = (bf16[128,256]{1,0:T(8,128)(2,1)S(1)}, bf16[128,256]{1,0:T(8,128)(2,1)S(1)}, u32[]{:S(2)}, u32[]{:S(2)}) collective-permute-start(bf16[128,256]{1,0:T(8,128)(2,1)S(1)} %get-tuple-element.53.own_c), channel_id=1, source_target_pairs={{0,8},{8,16},{16,24},{24,32},{32,40},{40,48},{48,56},{56,64},{64,7... | collective-permute-start | bytes 196616 | tf_op jit(solution)/shard_map/ppermute | solution.py:465
  112.7 3.5 %collective-permute-start.18 = (bf16[256,256]{1,0:T(8,128)(2,1)S(1)}, bf16[256,256]{1,0:T(8,128)(2,1)S(1)}, u32[]{:S(2)}, u32[]{:S(2)}) collective-permute-start(bf16[256,256]{1,0:T(8,128)(2,1)S(1)} %get-tuple-element.59), channel_id=1, source_target_pairs={{0,1},{1,0},{2,3},{3,2},{4,5},{5,4},{6,7},{7,6},{8,9},{9,8},{10,11... | collective-permute-start | bytes 393224 | tf_op jit(solution)/shard_map/ppermute | solution.py:130
  119.3 36.4 %collective-permute-start.20 = (bf16[64,4608]{1,0:T(8,128)(2,1)S(1)}, bf16[64,4608]{1,0:T(8,128)(2,1)S(1)}, u32[]{:S(2)}, u32[]{:S(2)}) collective-permute-start(bf16[64,4608]{1,0:T(8,128)(2,1)S(1)} %get-tuple-element.66), channel_id=1, source_target_pairs={{0,2},{1,7},{2,4},{3,1},{4,6},{5,3},{6,0},{7,5},{8,10},{9,15},{10,... | collective-permute-start | bytes 1769480 | tf_op jit(solution)/shard_map/ppermute | solution.py:130
  123.7 32.3 %collective-permute-start.19 = (bf16[64,4608]{1,0:T(8,128)(2,1)S(1)}, bf16[64,4608]{1,0:T(8,128)(2,1)S(1)}, u32[]{:S(2)}, u32[]{:S(2)}) collective-permute-start(bf16[64,4608]{1,0:T(8,128)(2,1)S(1)} %get-tuple-element.64), channel_id=1, source_target_pairs={{0,6},{1,3},{2,0},{3,5},{4,2},{5,7},{6,4},{7,1},{8,14},{9,11},{10,... | collective-permute-start | bytes 1769480 | tf_op jit(solution)/shard_map/ppermute | solution.py:130
  155.8 10.9 %collective-permute-start.21 = (bf16[64,4608]{1,0:T(8,128)(2,1)S(1)}, bf16[64,4608]{1,0:T(8,128)(2,1)S(1)}, u32[]{:S(2)}, u32[]{:S(2)}) collective-permute-start(bf16[64,4608]{1,0:T(8,128)(2,1)S(1)} %add_convert_fusion), channel_id=1, source_target_pairs={{0,2},{1,7},{2,4},{3,1},{4,6},{5,3},{6,0},{7,5},{8,10},{9,15},{10,... | collective-permute-start | bytes 1769480 | tf_op jit(solution)/shard_map/ppermute | solution.py:130
  166.7 1.1 copy-start.15
  166.7 1.1 copy-start.18
